TPU v7x, 32 devices: a whole 2x2x4 slice. The times are simulated.
32 devices in a mesh: fsdp: 4 (over y, core), expert: 8 (over z, x).
Axes of the slice: x: 2, y: 2, z: 4, core: 2. Of those that a mesh axis runs over, the one named last changes fastest.
Arguments:
- momentum: bfloat16 [16, 2, 2048, 768], P('expert', None, 'fsdp'), may hold values from -6 to 6
- gradient: bfloat16 [16, 2, 2048, 768], P('expert', None, 'fsdp'), may hold values from -70 to 70
- weights: bfloat16 [16, 2, 2048, 768], P('expert', None, 'fsdp'), may hold values from -0.03125 to 0.03125
- tokens: bfloat16 [2, 512, 2048], P(None, ('fsdp', 'expert')), may hold values from -24 to 24
- routes: int32 [2, 512, 8], P(None, ('fsdp', 'expert')), may hold values from 0 to 15, all different within a row; in each aligned block of 16 rows (0 to 15, 16 to 31, ..., all dimensions but the last counted through in order) at most 16 rows name the same one
- owners: int32 [4, 8], replicated, may hold values from 0 to 7, each once within a row
Outputs:
- hidden: bfloat16 [2, 4, 8, 32, 16, 384], P(None, 'fsdp', 'expert')
Inputs may be any that keep to these rules, and one draw needn't show every extreme that they name: `routes`: in each batch, the 16 rows of one device name each expert at most 16 times, a bound that some block reaches; a row names 8 different experts. `owners`: each row is a permutation.
All inputs are finite; a program needn't handle non-finite values.
Results may differ from a plain program's by a relative error of at most 0.0095.
Values may be sent and summed in bfloat16 or wider, within the bound.
No kernel may reach another device: no remote copies, remote signals or barrier semaphores. Data moves between devices by JAX's collectives and lax.ppermute only.
A program may use at most 128 MiB of HBM per device.

v0:
```python
import math

import jax
import jax.numpy as jnp
from jax import lax
from jax.sharding import PartitionSpec as P

momentum_decay = 0.95
coef_first = 3.4445
coef_second = -4.775
coef_third = 2.0315
step_size = 0.02
eps = 1e-07


def swapped(shard, axis, apart):
    return lax.ppermute(shard, axis, [(i, i ^ 1 << apart) for i in range(lax.axis_size(axis))])


def orthogonalize(update):
    values = update.astype(jnp.float32)
    squares_total = jnp.sum(values * values)
    current = (values / (jnp.sqrt(squares_total) + eps)).astype(jnp.bfloat16)
    for iteration in range(2):
        gram_matrix = lax.dot_general(
            current, current, (((0,), (0,)), ((), ())), preferred_element_type=jnp.float32
        ).astype(jnp.bfloat16)
        square = jnp.dot(gram_matrix, gram_matrix, preferred_element_type=jnp.float32)
        polynomial = (coef_second * gram_matrix.astype(jnp.float32) + coef_third * square).astype(
            jnp.bfloat16
        )
        current = (
            coef_first * current.astype(jnp.float32)
            + jnp.dot(current, polynomial, preferred_element_type=jnp.float32)
        ).astype(jnp.bfloat16)
    return current


def listed_rows(block_rows, block_routes, experts, capacity):
    labels = lax.broadcasted_iota(jnp.int32, (1, 1, experts), 2)
    routed = jnp.any(block_routes[:, :, None] == labels, axis=1).astype(jnp.int32)
    before = jnp.cumsum(routed, axis=0) - routed
    slot_ids = lax.broadcasted_iota(jnp.int32, (capacity, 1, 1), 0)
    select = ((routed[None, :, :] == 1) & (before[None, :, :] == slot_ids)).astype(jnp.bfloat16)
    listed = jnp.einsum("qtx,td->xqd", select, block_rows, preferred_element_type=jnp.float32)
    return listed.astype(jnp.bfloat16)


def dispatch(block_rows, block_routes, dest_expert, experts, capacity):
    listed = listed_rows(block_rows, block_routes, experts, capacity)
    outgoing = jnp.take(listed, dest_expert, axis=0)
    return lax.all_to_all(
        lax.all_to_all(outgoing, "fsdp", split_axis=0, concat_axis=0, tiled=True),
        "expert",
        split_axis=1,
        concat_axis=1,
        tiled=True,
    )


def swiglu(received, pair_weights, half_width):
    model_width = received.shape[-1]
    product = jnp.dot(
        received.reshape(-1, model_width), pair_weights, preferred_element_type=jnp.float32
    )
    result = jax.nn.silu(product[:, :half_width]) * product[:, half_width:]
    return result.astype(jnp.bfloat16).reshape(-1, received.shape[2], half_width)


def on_device(momentum, gradient, weights, tokens, routes, owners):
    fsdp_size = lax.axis_size("fsdp")
    group_size = lax.axis_size("expert")
    per_group = fsdp_size // 2
    experts = per_group * group_size
    local_rows = momentum.shape[2]
    hidden_width = momentum.shape[3]
    half_width = hidden_width // 2
    tok_dev = tokens.shape[1]
    top_count = routes.shape[2]
    capacity = max(2, 2 * tok_dev * top_count // experts)
    fsdp_index = lax.axis_index("fsdp")
    accumulated = momentum_decay * momentum.astype(jnp.float32) + gradient.astype(jnp.float32)
    update = (gradient.astype(jnp.float32) + momentum_decay * accumulated).astype(jnp.bfloat16)
    stacked = update.reshape(fsdp_size, local_rows, hidden_width)
    current_weights = weights.reshape(fsdp_size, local_rows, hidden_width)
    whole_update, whole_weight = (
        lax.all_to_all(stacked, "fsdp", split_axis=0, concat_axis=1, tiled=True),
        lax.all_to_all(current_weights, "fsdp", split_axis=0, concat_axis=1, tiled=True),
    )
    whole_update = whole_update[0]
    whole_weight = whole_weight[0]
    full_rows = whole_update.shape[0]
    update_scale = step_size * 0.2 * math.sqrt(max(full_rows, hidden_width))
    orthogonal = orthogonalize(whole_update)
    renewed = (
        whole_weight.astype(jnp.float32) - update_scale * orthogonal.astype(jnp.float32)
    ).astype(jnp.bfloat16)
    kind_index = fsdp_index % 2
    own_half = lax.dynamic_slice_in_dim(renewed, kind_index * half_width, half_width, 1)
    other_half = lax.dynamic_slice_in_dim(renewed, (1 - kind_index) * half_width, half_width, 1)
    partner = swapped(other_half, "fsdp", 0)
    gate_half = jnp.where(kind_index == 0, own_half, partner)
    up_half = jnp.where(kind_index == 0, partner, own_half)
    pair_weights = jnp.concatenate([gate_half, up_half], axis=1)
    owner_row = lax.dynamic_index_in_dim(owners, fsdp_index, 0, keepdims=False)
    fsdp_iota = lax.broadcasted_iota(jnp.int32, (fsdp_size, group_size), 0)
    group_iota = lax.broadcasted_iota(jnp.int32, (fsdp_size, group_size), 1)
    dest_expert = group_iota * per_group + fsdp_iota // 2
    received = []
    for batch_index in range(2):
        received.append(
            dispatch(tokens[batch_index], routes[batch_index], dest_expert, experts, capacity)
        )
    outputs = [swiglu(rows_in, pair_weights, half_width) for rows_in in received]
    results = jnp.stack(outputs)
    sources = results.shape[1]
    pieces = results.reshape(2, group_size, sources // group_size, capacity, half_width)
    spread = lax.all_to_all(pieces, "expert", split_axis=1, concat_axis=1, tiled=True)
    chosen = jnp.take(spread, owner_row, axis=1)
    collected = lax.all_to_all(chosen, "expert", split_axis=1, concat_axis=1, tiled=True)
    hidden = collected.reshape(2, 1, 1, sources, capacity, half_width)
    return hidden


def solution(mesh):
    in_specs = (
        P("expert", None, "fsdp", None),
        P("expert", None, "fsdp", None),
        P("expert", None, "fsdp", None),
        P(None, ("fsdp", "expert"), None),
        P(None, ("fsdp", "expert"), None),
        P(),
    )
    out_specs = P(None, "fsdp", "expert", None, None, None)
    return jax.shard_map(
        on_device, mesh=mesh, in_specs=in_specs, out_specs=out_specs, check_vma=False
    )
```

profile of v0, /device:TPU:0, one launch (start us, length us, event | category | flops | bytes accessed | tf_op | source)
XLA Modules:
  0.0 316.3 jit_solution(9345454300659282277)
XLA Ops:
  8.7 4.0 %broadcast_select_fusion.1 = (bf16[4,8,16,2048]{3,2,1,0:T(8,128)(2,1)S(1)}, bf16[4,8,16,2048]{3,2,1,0:T(8,128)(2,1)}) fusion(bf16[4,8,16,2048]{3,2,1,0:T(8,128)(2,1)} %bitcast.62, pred[4,8]{1,0:T(4,128)(4,1)S(1)} %compare_and_fusion, bf16[4,8,16,2048]{3,2,1,0:T(8,128)(2,1)} %bitcast.61), kind=kLoop, calls=%fused_computation.24 | loop fusion | flops 2097152 | bytes 8388640 | tf_op jit(solution)/shard_map/jit(_take)/select_n | solution.py:51
  12.7 29.8 %all_to_all.48 = bf16[4,8,16,2048]{3,2,1,0:T(8,128)(2,1)} all-to-all(bf16[4,8,16,2048]{3,2,1,0:T(8,128)(2,1)S(1)} %get-tuple-element.14), channel_id=1, replica_groups=mesh['fsdp'=4,'expert'=8] {'fsdp'}, dimensions={0} | all-to-all | bytes 4194304 | tf_op jit(solution)/shard_map/all_to_all | solution.py:53
  42.5 3.6 %all-to-all-start.4 = ((bf16[4,8,16,2048]{3,2,1,0:T(8,128)(2,1)}), bf16[4,8,16,2048]{3,2,1,0:T(8,128)(2,1)S(1)}, u32[]{:S(2)}, u32[]{:S(2)}) async-start(bf16[4,8,16,2048]{3,2,1,0:T(8,128)(2,1)} %get-tuple-element.15), calls=%async_computation.4 | async-start | bytes 4194304 | tf_op jit(solution)/shard_map/all_to_all | solution.py:53
  46.1 5.9 %fusion.1 = bf16[2,2,512,768]{3,2,1,0:T(8,128)(2,1)} fusion(bf16[2,2,512,768]{3,2,1,0:T(8,128)(2,1)} %param.9, bf16[2,2,512,768]{3,2,1,0:T(8,128)(2,1)} %param.8), kind=kLoop, calls=%fused_computation.8 | loop fusion | flops 11010048 | bytes 9437184 | tf_op jit(solution)/shard_map/convert_element_type | solution.py:83
  52.0 19.8 %all-to-all-done.4 = bf16[4,8,16,2048]{3,2,1,0:T(8,128)(2,1)S(1)} async-done(((bf16[4,8,16,2048]{3,2,1,0:T(8,128)(2,1)}), bf16[4,8,16,2048]{3,2,1,0:T(8,128)(2,1)S(1)}, u32[]{:S(2)}, u32[]{:S(2)}) %all-to-all-start.4) | async-done | bytes 2097184 | tf_op jit(solution)/shard_map/all_to_all | solution.py:53
  73.1 3.7 %all-to-all-start.3 = ((bf16[4,512,768]{2,1,0:T(8,128)(2,1)}), bf16[4,512,768]{2,1,0:T(8,128)(2,1)S(1)}, u32[]{:S(2)}, u32[]{:S(2)}) async-start(bf16[4,512,768]{2,1,0:T(8,128)(2,1)} %bitcast.60), calls=%async_computation.3 | async-start | bytes 6291456 | tf_op jit(solution)/shard_map/all_to_all | solution.py:87
  76.8 4.7 %copy.120 = bf16[2,2,512,768]{2,3,1,0:T(8,128)(2,1)} copy(bf16[2,2,512,768]{3,2,1,0:T(8,128)(2,1)} %param.10) | data formatting | bytes 6291456 | tf_op args[2]
  81.5 32.2 %all-to-all-done.3 = bf16[4,512,768]{2,1,0:T(8,128)(2,1)S(1)} async-done(((bf16[4,512,768]{2,1,0:T(8,128)(2,1)}), bf16[4,512,768]{2,1,0:T(8,128)(2,1)S(1)}, u32[]{:S(2)}, u32[]{:S(2)}) %all-to-all-start.3) | async-done | bytes 3145760 | tf_op jit(solution)/shard_map/all_to_all | solution.py:87
  113.7 4.7 %all-to-all-start.2 = ((bf16[4,512,768]{1,2,0:T(8,128)(2,1)}), bf16[4,512,768]{1,2,0:T(8,128)(2,1)}, u32[]{:S(2)}, u32[]{:S(2)}) async-start(bf16[4,512,768]{1,2,0:T(8,128)(2,1)} %bitcast.57), calls=%async_computation.2 | async-start | bytes 6291456 | tf_op jit(solution)/shard_map/all_to_all | solution.py:88
  123.2 32.2 %all-to-all-done.2 = bf16[4,512,768]{1,2,0:T(8,128)(2,1)} async-done(((bf16[4,512,768]{1,2,0:T(8,128)(2,1)}), bf16[4,512,768]{1,2,0:T(8,128)(2,1)}, u32[]{:S(2)}, u32[]{:S(2)}) %all-to-all-start.2) | async-done | bytes 3145760 | tf_op jit(solution)/shard_map/all_to_all | solution.py:88
  155.3 6.4 %all-to-all-start.1 = ((bf16[4,8,16,2048]{3,2,0,1:T(8,128)(2,1)}), bf16[4,8,16,2048]{3,2,0,1:T(8,128)(2,1)}, u32[]{:S(2)}, u32[]{:S(2)}) async-start(bf16[4,8,16,2048]{3,2,0,1:T(8,128)(2,1)} %copy.118), calls=%async_computation.1 | async-start | bytes 4194304 | tf_op jit(solution)/shard_map/all_to_all | solution.py:52
  166.9 4.7 %copy.122 = bf16[2048,768]{0,1:T(8,128)(2,1)} copy(bf16[2048,768]{1,0:T(8,128)(2,1)} %bitcast.58) | data formatting | bytes 6291456 | tf_op jit(solution)/shard_map/convert_element_type | solution.py:23
  174.3 3.4 %copy.136 = f32[4,96,8,512]{3,2,0,1:T(8,128)} copy(f32[4,96,8,512]{3,2,1,0:T(8,128)S(1)} %convert_bitcast_fusion) | data formatting | bytes 12582912 | tf_op jit(solution)/shard_map/convert_element_type | solution.py:96
  177.7 3.7 %bitcast_convert_fusion = bf16[768,768]{1,0:T(8,128)(2,1)} fusion(bf16[4,512,768]{2,1,0:T(8,128)(2,1)S(1)} %copy-done), kind=kOutput, calls=%fused_computation.20 | convolution fusion | flops 2416508928 | bytes 4325376 | tf_op jit(solution)/shard_map/dot_general | solution.py:25
  181.4 9.6 %add_convert_fusion.1 = bf16[2048,768]{0,1:T(8,128)(2,1)} fusion(bf16[2048,768]{0,1:T(8,128)(2,1)} %copy.122, bf16[2048,768]{1,0:T(8,128)(2,1)S(1)} %bitcast.59, bf16[768,768]{1,0:T(8,128)(2,1)} %bitcast_convert_fusion), kind=kOutput, calls=%fused_computation.14 | convolution fusion | flops 3331129344 | bytes 10616832 | tf_op jit(solution)/shard_map/dot_general | solution.py:34
  191.0 5.5 %convolution_convert_fusion.2 = bf16[768,768]{1,0:T(8,128)(2,1)S(1)} fusion(bf16[2048,768]{0,1:T(8,128)(2,1)} %add_convert_fusion.1), kind=kOutput, calls=%fused_computation.29 | convolution fusion | flops 2416508928 | bytes 4325376 | tf_op jit(solution)/shard_map/dot_general | solution.py:25
  196.5 13.2 %all-to-all-done.1 = bf16[4,8,16,2048]{3,2,0,1:T(8,128)(2,1)} async-done(((bf16[4,8,16,2048]{3,2,0,1:T(8,128)(2,1)}), bf16[4,8,16,2048]{3,2,0,1:T(8,128)(2,1)}, u32[]{:S(2)}, u32[]{:S(2)}) %all-to-all-start.1) | async-done | bytes 2097184 | tf_op jit(solution)/shard_map/all_to_all | solution.py:52
  209.7 3.8 %all-to-all-start.5 = ((bf16[4,8,16,2048]{3,2,0,1:T(8,128)(2,1)}), bf16[4,8,16,2048]{3,2,0,1:T(8,128)(2,1)S(1)}, u32[]{:S(2)}, u32[]{:S(2)}) async-start(bf16[4,8,16,2048]{3,2,0,1:T(8,128)(2,1)} %copy.128), calls=%async_computation.5 | async-start | bytes 4194304 | tf_op jit(solution)/shard_map/all_to_all | solution.py:52
  213.5 10.7 %subtract_convert_fusion = bf16[2048,768]{0,1:T(8,128)(2,1)} fusion(f32[2048,768]{0,1:T(8,128)} %bitcast.63, bf16[2048,768]{0,1:T(8,128)(2,1)} %add_convert_fusion.1, bf16[768,768]{1,0:T(8,128)(2,1)S(1)} %convolution_convert_fusion.2), kind=kOutput, calls=%fused_computation.12 | convolution fusion | flops 3337420800 | bytes 13762560 | tf_op jit(solution)/shard_map/dot_general | solution.py:34
  227.0 3.7 %collective-permute-done = bf16[2048,384]{0,1:T(8,128)(2,1)} collective-permute-done((bf16[2048,384]{0,1:T(8,128)(2,1)}, bf16[2048,384]{0,1:T(8,128)(2,1)}, u32[]{:S(2)}, u32[]{:S(2)}) %collective-permute-start) | collective-permute-done | bytes 1572896 | tf_op jit(solution)/shard_map/ppermute | solution.py:17
  238.7 23.1 %all-to-all-done.5 = bf16[4,8,16,2048]{3,2,0,1:T(8,128)(2,1)S(1)} async-done(((bf16[4,8,16,2048]{3,2,0,1:T(8,128)(2,1)}), bf16[4,8,16,2048]{3,2,0,1:T(8,128)(2,1)S(1)}, u32[]{:S(2)}, u32[]{:S(2)}) %all-to-all-start.5) | async-done | bytes 2097184 | tf_op jit(solution)/shard_map/all_to_all | solution.py:52
  266.8 3.6 %all-to-all-start.6 = ((bf16[2,8,4,16,384]{4,3,2,0,1:T(8,128)(2,1)}), bf16[2,8,4,16,384]{4,3,2,0,1:T(8,128)(2,1)S(1)}, u32[]{:S(2)}, u32[]{:S(2)}) async-start(bf16[2,8,4,16,384]{4,3,2,0,1:T(8,128)(2,1)} %pad_maximum_fusion.3), calls=%async_computation.6 | async-start | bytes 1572864 | tf_op jit(solution)/shard_map/all_to_all | solution.py:118
  270.4 20.3 %all-to-all-done.6 = bf16[2,8,4,16,384]{4,3,2,0,1:T(8,128)(2,1)S(1)} async-done(((bf16[2,8,4,16,384]{4,3,2,0,1:T(8,128)(2,1)}), bf16[2,8,4,16,384]{4,3,2,0,1:T(8,128)(2,1)S(1)}, u32[]{:S(2)}, u32[]{:S(2)}) %all-to-all-start.6) | async-done | bytes 786464 | tf_op jit(solution)/shard_map/all_to_all | solution.py:118
  291.7 23.6 %all_to_all.49 = bf16[2,8,4,16,384]{4,3,2,0,1:T(8,128)(2,1)S(1)} all-to-all(bf16[2,8,4,16,384]{4,3,2,0,1:T(8,128)(2,1)S(1)} %select_bitcast_fusion), channel_id=1, replica_groups=mesh['fsdp'=4,'expert'=8] {'expert'}, dimensions={1} | all-to-all | bytes 1572864 | tf_op jit(solution)/shard_map/all_to_all | solution.py:120
  (68 shorter events, 39.6 us)
Async XLA Ops:
  0.0 3.6 %copy-start.7 = (bf16[2,16,2048]{2,1,0:T(8,128)(2,1)S(1)}, bf16[2,16,2048]{2,1,0:T(8,128)(2,1)}, u32[]{:S(2)}) copy-start(bf16[2,16,2048]{2,1,0:T(8,128)(2,1)} %param.11) | copy-start | bytes 393220
  42.5 29.2 %all-to-all-start.4 = ((bf16[4,8,16,2048]{3,2,1,0:T(8,128)(2,1)}), bf16[4,8,16,2048]{3,2,1,0:T(8,128)(2,1)S(1)}, u32[]{:S(2)}, u32[]{:S(2)}) async-start(bf16[4,8,16,2048]{3,2,1,0:T(8,128)(2,1)} %get-tuple-element.15), calls=%async_computation.4 | async-start | bytes 4194304 | tf_op jit(solution)/shard_map/all_to_all | solution.py:53
  71.7 1.4 copy-start.1
  73.1 40.6 %all-to-all-start.3 = ((bf16[4,512,768]{2,1,0:T(8,128)(2,1)}), bf16[4,512,768]{2,1,0:T(8,128)(2,1)S(1)}, u32[]{:S(2)}, u32[]{:S(2)}) async-start(bf16[4,512,768]{2,1,0:T(8,128)(2,1)} %bitcast.60), calls=%async_computation.3 | async-start | bytes 6291456 | tf_op jit(solution)/shard_map/all_to_all | solution.py:87
  113.7 41.6 %all-to-all-start.2 = ((bf16[4,512,768]{1,2,0:T(8,128)(2,1)}), bf16[4,512,768]{1,2,0:T(8,128)(2,1)}, u32[]{:S(2)}, u32[]{:S(2)}) async-start(bf16[4,512,768]{1,2,0:T(8,128)(2,1)} %bitcast.57), calls=%async_computation.2 | async-start | bytes 6291456 | tf_op jit(solution)/shard_map/all_to_all | solution.py:88
  118.4 3.3 %copy-start.2 = (bf16[4,8,16,2048]{3,2,1,0:T(8,128)(2,1)S(1)}, bf16[4,8,16,2048]{3,2,1,0:T(8,128)(2,1)}, u32[]{:S(2)}) copy-start(bf16[4,8,16,2048]{3,2,1,0:T(8,128)(2,1)} %copy-done.1) | copy-start | bytes 6291460
  155.3 54.4 %all-to-all-start.1 = ((bf16[4,8,16,2048]{3,2,0,1:T(8,128)(2,1)}), bf16[4,8,16,2048]{3,2,0,1:T(8,128)(2,1)}, u32[]{:S(2)}, u32[]{:S(2)}) async-start(bf16[4,8,16,2048]{3,2,0,1:T(8,128)(2,1)} %copy.118), calls=%async_computation.1 | async-start | bytes 4194304 | tf_op jit(solution)/shard_map/all_to_all | solution.py:52
  174.3 3.4 %copy-start = (bf16[4,512,768]{2,1,0:T(8,128)(2,1)S(1)}, bf16[4,512,768]{2,1,0:T(8,128)(2,1)}, u32[]{:S(2)}) copy-start(bf16[4,512,768]{2,1,0:T(8,128)(2,1)} %fusion.3) | copy-start | bytes 9437188
  209.7 52.1 %all-to-all-start.5 = ((bf16[4,8,16,2048]{3,2,0,1:T(8,128)(2,1)}), bf16[4,8,16,2048]{3,2,0,1:T(8,128)(2,1)S(1)}, u32[]{:S(2)}, u32[]{:S(2)}) async-start(bf16[4,8,16,2048]{3,2,0,1:T(8,128)(2,1)} %copy.128), calls=%async_computation.5 | async-start | bytes 4194304 | tf_op jit(solution)/shard_map/all_to_all | solution.py:52
  227.0 3.8 %collective-permute-start = (bf16[2048,384]{0,1:T(8,128)(2,1)}, bf16[2048,384]{0,1:T(8,128)(2,1)}, u32[]{:S(2)}, u32[]{:S(2)}) collective-permute-start(bf16[2048,384]{0,1:T(8,128)(2,1)} %constant_dynamic-slice_fusion), channel_id=1, source_target_pairs={{0,8},{8,0},{16,24},{24,16},{1,9},{9,1},{17,25},{25,17},{2,10},{10... | collective-permute-start | bytes 4718600 | tf_op jit(solution)/shard_map/ppermute | solution.py:17
  233.6 4.8 %copy-start.3 = (bf16[2048,384]{0,1:T(8,128)(2,1)}, bf16[2048,384]{0,1:T(8,128)(2,1)S(1)}, u32[]{:S(2)}) copy-start(bf16[2048,384]{0,1:T(8,128)(2,1)S(1)} %get-tuple-element.6) | copy-start | bytes 4718596
  233.6 4.8 %copy-start.5 = (bf16[2048,384]{0,1:T(8,128)(2,1)}, bf16[2048,384]{0,1:T(8,128)(2,1)S(1)}, u32[]{:S(2)}) copy-start(bf16[2048,384]{0,1:T(8,128)(2,1)S(1)} %get-tuple-element.7) | copy-start | bytes 4718596
  261.8 1.4 copy-start.4
  261.8 1.9 copy-start.6
  265.6 4.8 %copy-start.8 = (s32[4,8]{1,0:T(4,128)S(1)}, s32[4,8]{1,0:T(4,128)}, u32[]{:S(2)}) copy-start(s32[4,8]{1,0:T(4,128)} %param.13) | copy-start | bytes 388
  266.8 24.0 %all-to-all-start.6 = ((bf16[2,8,4,16,384]{4,3,2,0,1:T(8,128)(2,1)}), bf16[2,8,4,16,384]{4,3,2,0,1:T(8,128)(2,1)S(1)}, u32[]{:S(2)}, u32[]{:S(2)}) async-start(bf16[2,8,4,16,384]{4,3,2,0,1:T(8,128)(2,1)} %pad_maximum_fusion.3), calls=%async_computation.6 | async-start | bytes 1572864 | tf_op jit(solution)/shard_map/all_to_all | solution.py:118
where the time goes:
time: 317 us; the launch traced here: 316 us
  waiting for transfers between devices  145 us (46%)
  blocking collectives  53.4 us (17%)
  matrix products  34.8 us (11%)
  local copies, waits for them, and re-layouts  34.7 us (11%)
  starting transfers between devices  25.7 us (8%)
  other arithmetic  22.1 us (7%)
    all_to_all x2, waiting for transfers between devices, dispatch(): lax.all_to_all(lax.all_to_all(outgoing, 'fsdp', split_axis=0, concat_axis...  36.4 us
    all_to_all x1, waiting for transfers between devices, on_device(): lax.all_to_all(stacked, 'fsdp', split_axis=0, concat_axis=1, tiled=True)  32.2 us
    all_to_all x1, waiting for transfers between devices, on_device(): lax.all_to_all(current_weights, 'fsdp', split_axis=0, concat_axis=1, tile...  32.2 us
    all_to_all x1, blocking collectives, dispatch(): lax.all_to_all(outgoing, 'fsdp', split_axis=0, concat_axis=0, tiled=True)  29.8 us
    all_to_all x1, blocking collectives, on_device(): lax.all_to_all(chosen, 'expert', split_axis=1, concat_axis=1, tiled=True)  23.6 us
    all_to_all x1, waiting for transfers between devices, on_device(): lax.all_to_all(pieces, 'expert', split_axis=1, concat_axis=1, tiled=True)  20.3 us
    dot_general x2, matrix products, orthogonalize(): jnp.dot(current, polynomial, preferred_element_type=jnp.float32)  20.3 us
    all_to_all x1, waiting for transfers between devices, dispatch(): lax.all_to_all(outgoing, 'fsdp', split_axis=0, concat_axis=0, tiled=True)  19.8 us
  transfers between devices with their start and end apart: 7, of which 7 were waited for; matrix products, arithmetic and copies ran while one was open for 22% of the time, Pallas kernels for 0%

commit v1 on v0

v1 whole, which is shorter than its diff:
```python
import functools
import math

import jax
import jax.numpy as jnp
import numpy as np
from jax import lax
from jax.experimental import pallas as pl
from jax.experimental.pallas import tpu as pltpu
from jax.sharding import PartitionSpec as P


momentum_decay = 0.95
coef_first = 3.4445
coef_second = -4.775
coef_third = 2.0315
step_size = 0.02
eps = 1e-07


VMEM = pl.BlockSpec(memory_space=pltpu.VMEM)
SMEM = pl.BlockSpec(memory_space=pltpu.SMEM)


def dot(a, b):
    return jnp.dot(a, b, preferred_element_type=jnp.float32)


def swapped(shard, axis, mask):
    return lax.ppermute(shard, axis, [(i, i ^ mask) for i in range(lax.axis_size(axis))])


def moved_along(shard, shift):
    size = lax.axis_size("expert")
    pairs = [(i, i + 2 * shift) for i in range(size) if 0 <= i + 2 * shift < size]
    return lax.ppermute(shard, "expert", pairs)


def slots_of(routes, experts):
    labels = lax.broadcasted_iota(jnp.int32, (1, 1, 1, experts), 3)
    routed = jnp.any(routes[:, :, :, None] == labels, axis=2).astype(jnp.int32)
    count = routes.shape[1]
    later = lax.broadcasted_iota(jnp.int32, (count, count), 0)
    earlier = lax.broadcasted_iota(jnp.int32, (count, count), 1)
    upto = (earlier <= later).astype(jnp.int32)
    place = jnp.sum(upto[None, :, :, None] * routed[:, None, :, :], axis=2)
    return jnp.where(routed == 1, place, 0)


def gathered(block):
    fsdp_size, group_size = lax.axis_size("fsdp"), lax.axis_size("expert")
    f, r = lax.axis_index("fsdp"), lax.axis_index("expert")
    held, masks = block[None], [0]
    if group_size == 8:
        mask = 2
        while mask < fsdp_size:
            held = jnp.concatenate([held, swapped(held, "fsdp", mask)])
            masks += [m ^ mask for m in masks]
            mask *= 2
        up, down = moved_along(held, 1), moved_along(held, -1)
        up2, down2 = moved_along(up, 1), moved_along(down, -1)
        up3, down3 = moved_along(up2, 1), moved_along(down2, -1)
        first = swapped(held, "expert", 1)
        near = jnp.concatenate([up, down])
        near_x = swapped(near, "expert", 1)
        far = up2 + down2
        far_x = swapped(far, "expert", 1)
        ends = up3 + down3
        ends_x = swapped(ends, "expert", 1)
        rows = jnp.concatenate([held, near, far, ends, first, near_x, far_x, ends_x])
        z, x = r // 2, r % 2
        layers = jnp.stack([z, z - 1, z + 1, z ^ 2, z ^ 3])
        layers = jnp.clip(layers, 0, group_size // 2 - 1)
        across = jnp.concatenate([layers * 2 + x, layers * 2 + (x ^ 1)])
        source_r = jnp.repeat(across, len(masks))
        source_f = jnp.tile(f ^ np.array(masks, np.int32), 10)
        return rows, source_f // 2, source_r
    held = lax.all_gather(block, "expert")
    mask = 2
    while mask < fsdp_size:
        held = jnp.concatenate([held, swapped(held, "fsdp", mask)])
        masks += [m ^ mask for m in masks]
        mask *= 2
    source_f = jnp.repeat(f ^ np.array(masks, np.int32), group_size)
    source_r = jnp.tile(jnp.arange(group_size, dtype=jnp.int32), len(masks))
    return held, source_f // 2, source_r


def columns_of(index, width):
    return pl.ds(pl.multiple_of(index * width, 128), width)


def started(*pairs_and_sem):
    *pairs, sem = pairs_and_sem
    copies = [pltpu.make_async_copy(src, dst, sem.at[i]) for i, (src, dst) in enumerate(pairs)]
    for copy in copies:
        copy.start()
    return copies


def factor_kernel(*refs):
    count = len(refs) - 4
    update_refs, (factor_ref, inverse_ref, held, sem) = refs[:count], refs[count:]
    copies = started(*[(u, held.at[i]) for i, u in enumerate(update_refs)], sem)
    gram = None
    for i, copy in enumerate(copies):
        copy.wait()
        rows = held[i]
        term = lax.dot_general(
            rows, rows, (((0,), (0,)), ((), ())), preferred_element_type=jnp.float32
        )
        gram = term if gram is None else gram + term
    diagonal = lax.broadcasted_iota(jnp.int32, gram.shape, 0) == lax.broadcasted_iota(
        jnp.int32, gram.shape, 1
    )
    inverse = 1.0 / (jnp.sqrt(jnp.sum(jnp.where(diagonal, gram, 0.0))) + eps)
    inverse_ref[0] = inverse
    gram0 = gram * inverse * inverse
    g0 = gram0.astype(jnp.bfloat16)
    p0 = (coef_second * gram0 + coef_third * dot(g0, g0)).astype(jnp.bfloat16)
    half_way = coef_first * gram0 + dot(g0, p0)
    gram1 = coef_first * half_way + dot(half_way.astype(jnp.bfloat16), p0)
    g1 = gram1.astype(jnp.bfloat16)
    p1 = (coef_second * gram1 + coef_third * dot(g1, g1)).astype(jnp.bfloat16)
    factor = coef_first * (p0.astype(jnp.float32) + p1.astype(jnp.float32)) + dot(p0, p1)
    factor_ref[...] = factor.astype(jnp.bfloat16)


def row_copies(order, at_ref, own_ref, other_ref, held):
    pairs = []
    for i, place in enumerate(order):
        columns = columns_of(at_ref[0] ^ place, held.shape[3])
        pairs.append((own_ref.at[:, columns], held.at[0, i]))
        pairs.append((other_ref.at[:, columns], held.at[1, i]))
    return pairs


def moved_kernel(order, at_ref, inverse_ref, factor_ref, own_ref, other_ref, *refs):
    count = len(order)
    update_refs = refs[:count]
    kept_ref, sent_ref, rows, update, factor, total, sem_u, sem_r, sem_f = refs[count:]
    pairs = row_copies(order, at_ref, own_ref, other_ref, rows)
    first = started(*[(u, update.at[i]) for i, u in enumerate(update_refs)], sem_u)
    second = started(*pairs, sem_r)
    (last,) = started((factor_ref, factor), sem_f)
    for i in range(count):
        first[i].wait()
        for side in range(2):
            second[2 * i + side].wait()
            term = dot(rows[side, i], update[i])
            total[side] = term if i == 0 else total[side] + term
    last.wait()
    width = kept_ref.shape[2]
    kind = lax.rem(at_ref[0], 2)
    for side in range(2):
        along = total[side] * inverse_ref[0]
        moved = coef_first * coef_first * along + dot(along.astype(jnp.bfloat16), factor[...])
        moved = moved.astype(jnp.bfloat16)
        left, right = moved[:, :width], moved[:, width:]
        kept_ref[side] = jnp.where(kind == 0, left, right)
        sent_ref[1 - side] = jnp.where(kind == 0, right, left)


def base_kernel(order, scale, at_ref, own_ref, other_ref, kept_ref, partner_ref, *refs):
    count = len(order)
    weight_refs = refs[:count]
    base_ref, rows, weight, moved, sem_w, sem_r, sem_m = refs[count:]
    first = started(*[(w, weight.at[i]) for i, w in enumerate(weight_refs)], sem_w)
    second = started(*row_copies(order, at_ref, own_ref, other_ref, rows), sem_r)
    third = started((kept_ref, moved.at[0]), (partner_ref, moved.at[1]), sem_m)
    for copy in first + second + third:
        copy.wait()
    width = moved.shape[3]
    own_kind = lax.rem(at_ref[0], 2)
    for side in range(2):
        for kind in range(2):
            part = jnp.where(own_kind == kind, moved[0, side], moved[1, side])
            total = -scale * part.astype(jnp.float32)
            for i in range(count):
                total += dot(rows[side, i], weight[i, kind])
            base_ref[side, :, kind * width : (kind + 1) * width] = total


def finish_kernel(order, group_size, at_ref, own_ref, other_ref, base_ref, *refs):
    count = len(order)
    weight_refs, refs = refs[:count], refs[count:]
    out_refs, (rows, weight, base, hidden, sem_w, sem_r, sem_b) = refs[:group_size], refs[group_size:]
    third = started(*[(base_ref.at[side], base.at[side]) for side in range(2)], sem_b)
    second = started(*row_copies(order, at_ref, own_ref, other_ref, rows), sem_r)
    first = started(*[(w, weight.at[i]) for i, w in enumerate(weight_refs)], sem_w)
    for copy in first:
        copy.wait()
    width = base.shape[2] // 2
    for side in range(2):
        third[side].wait()
        for i in range(count):
            second[2 * i + side].wait()
        products = []
        for kind in range(2):
            total = base[side, :, kind * width : (kind + 1) * width]
            for i in range(count):
                total += dot(rows[side, i], weight[i, kind])
            products.append(total)
        gate, up = products
        hidden[side] = (gate / (1.0 + jnp.exp(-gate)) * up).astype(jnp.bfloat16)
    chunk = hidden.shape[1] // group_size
    for mask in range(group_size):
        start = pl.multiple_of((at_ref[1] ^ mask) * chunk, chunk)
        out_refs[mask][...] = hidden[:, pl.ds(start, chunk), :]


def on_device(momentum, gradient, weights, tokens, routes, owners):
    fsdp_size = lax.axis_size("fsdp")
    group_size = lax.axis_size("expert")
    per_group = fsdp_size // 2
    experts = per_group * group_size
    local_rows = momentum.shape[2]
    hidden_width = momentum.shape[3]
    half_width = hidden_width // 2
    model_width = tokens.shape[2]
    tok_dev = tokens.shape[1]
    top_count = routes.shape[2]
    capacity = max(2, 2 * tok_dev * top_count // experts)
    f = lax.axis_index("fsdp")
    r = lax.axis_index("expert")
    own_expert = r * per_group + f // 2
    at = jnp.stack([f, r]).astype(jnp.int32)
    near = [0, 1]
    far = list(range(2, fsdp_size))
    order = near + far

    slot_lanes = -(-experts // 128) * 128
    slots = slots_of(routes, experts).astype(jnp.bfloat16)
    slots = jnp.pad(slots, ((0, 0), (0, 0), (0, slot_lanes - experts)))
    block = jnp.concatenate([tokens, slots], axis=2).reshape(2 * tok_dev, model_width + slot_lanes)
    blocks, source_pair, source_group = gathered(block)
    all_rows = blocks.reshape(-1, model_width + slot_lanes)
    lane = lax.broadcasted_iota(jnp.int32, (1, slot_lanes), 1)
    picked = jnp.where(lane == own_expert, all_rows[:, model_width:].astype(jnp.float32), 0.0)
    slot = jnp.sum(picked, axis=1).astype(jnp.int32).reshape(-1, 2, tok_dev)
    batch = jnp.arange(2, dtype=jnp.int32)[None, :, None]
    first = (source_group[:, None, None] * 2 + batch) * per_group + source_pair[:, None, None]
    listed_at = jnp.where(slot > 0, first * capacity + slot - 1, -1).reshape(1, -1)
    half_rows = group_size * 2 * per_group * capacity
    labels = lax.broadcasted_iota(jnp.int32, (half_rows, listed_at.shape[1]), 0)
    select = (labels == listed_at).astype(jnp.bfloat16)
    own_rows = dot(select, all_rows[:, :model_width]).astype(jnp.bfloat16)
    other_rows = swapped(own_rows, "fsdp", 1)

    moment = momentum.reshape(fsdp_size, local_rows, hidden_width)
    grad = gradient.reshape(fsdp_size, local_rows, hidden_width)
    weight = weights.reshape(fsdp_size, local_rows, hidden_width)
    update, held_weight = [None] * fsdp_size, [None] * fsdp_size
    for places in (far, near):
        for mask in reversed(places):
            moment_part = lax.dynamic_index_in_dim(moment, f ^ mask, 0, keepdims=False)
            grad_part = lax.dynamic_index_in_dim(grad, f ^ mask, 0, keepdims=False)
            grad_part = grad_part.astype(jnp.float32)
            accumulated = momentum_decay * moment_part.astype(jnp.float32) + grad_part
            update[mask] = (grad_part + momentum_decay * accumulated).astype(jnp.bfloat16)
        if places is far:
            moment, grad, *parts = lax.optimization_barrier(
                (moment, grad, *[update[m] for m in far])
            )
            for mask, part in zip(far, parts):
                update[mask] = part
    for mask in reversed(range(1, fsdp_size)):
        update[mask] = swapped(update[mask], "fsdp", mask)
    for mask in reversed(range(fsdp_size)):
        target = f ^ mask
        part = lax.dynamic_slice(
            weight,
            (target // 2 * 2, 0, target % 2 * half_width),
            (2, local_rows, half_width),
        )
        held_weight[mask] = swapped(part, "fsdp", mask) if mask else part

    full_rows = fsdp_size * local_rows
    update_scale = step_size * 0.2 * math.sqrt(max(full_rows, hidden_width))
    depth = local_rows
    any_ref = pl.BlockSpec(memory_space=pl.ANY)
    dma = pltpu.SemaphoreType.DMA
    bf16_scratch = lambda *shape: pltpu.VMEM(shape, jnp.bfloat16)
    shaped = lambda kind, *shape: jax.ShapeDtypeStruct(shape, kind)
    flops = 2 * 2 * half_rows * full_rows * hidden_width
    cost = lambda work, moved_bytes: pl.CostEstimate(
        flops=work, bytes_accessed=moved_bytes, transcendentals=0
    )
    factor, inverse = pl.pallas_call(
        factor_kernel,
        out_shape=[
            shaped(jnp.bfloat16, hidden_width, hidden_width),
            shaped(jnp.float32, 1),
        ],
        in_specs=[any_ref] * fsdp_size,
        out_specs=[VMEM, SMEM],
        scratch_shapes=[bf16_scratch(fsdp_size, depth, hidden_width), dma((fsdp_size,))],
        cost_estimate=cost(3 * flops, 4 << 20),
        name="factor",
    )(*[update[m] for m in order])

    kind = f % 2
    half_shape = (2, half_rows, half_width)
    count = len(order)
    kept, sent = pl.pallas_call(
        functools.partial(moved_kernel, order),
        out_shape=[shaped(jnp.bfloat16, *half_shape)] * 2,
        in_specs=[SMEM, SMEM] + [any_ref] * (3 + count),
        out_specs=[VMEM, VMEM],
        scratch_shapes=[
            bf16_scratch(2, count, half_rows, depth),
            bf16_scratch(count, depth, hidden_width),
            bf16_scratch(hidden_width, hidden_width),
            pltpu.VMEM((2, half_rows, hidden_width), jnp.float32),
            dma((count,)),
            dma((2 * count,)),
            dma((1,)),
        ],
        cost_estimate=cost(2 * flops, 12 << 20),
        name="moved",
    )(at, inverse, factor, own_rows, other_rows, *[update[m] for m in order])
    partner = swapped(sent, "fsdp", 1)
    count = len(near)
    base = pl.pallas_call(
        functools.partial(base_kernel, near, update_scale),
        out_shape=shaped(jnp.float32, 2, half_rows, hidden_width),
        in_specs=[SMEM] + [any_ref] * (4 + count),
        out_specs=VMEM,
        scratch_shapes=[
            bf16_scratch(2, count, half_rows, depth),
            bf16_scratch(count, 2, depth, half_width),
            bf16_scratch(2, *half_shape),
            dma((count,)),
            dma((2 * count,)),
            dma((2,)),
        ],
        cost_estimate=cost(flops, 10 << 20),
        name="base",
    )(at, own_rows, other_rows, kept, partner, *[held_weight[m] for m in near])
    chunk = half_rows // group_size
    count = len(far)
    pieces = pl.pallas_call(
        functools.partial(finish_kernel, far, group_size),
        out_shape=[shaped(jnp.bfloat16, 2, chunk, half_width)] * group_size,
        in_specs=[SMEM] + [any_ref] * (3 + count),
        out_specs=[VMEM] * group_size,
        scratch_shapes=[
            bf16_scratch(2, count, half_rows, depth),
            bf16_scratch(count, 2, depth, half_width),
            pltpu.VMEM((2, half_rows, hidden_width), jnp.float32),
            bf16_scratch(*half_shape),
            dma((count,)),
            dma((2 * count,)),
            dma((2,)),
        ],
        cost_estimate=cost(flops, 10 << 20),
        name="finish",
    )(at, own_rows, other_rows, base, *[held_weight[m] for m in far])

    spread = [swapped(pieces[m], "expert", m) if m else pieces[m] for m in range(group_size)]
    spread = jnp.stack(spread)
    owner_row = lax.dynamic_index_in_dim(owners, f, 0, keepdims=False)
    hidden = jnp.zeros((2, per_group, 2, group_size, capacity, half_width), jnp.bfloat16)
    for mask in range(group_size):
        wanted = lax.dynamic_index_in_dim(owner_row, r ^ mask, 0, keepdims=False) ^ r
        part = lax.dynamic_index_in_dim(spread, wanted, 0, keepdims=False)
        part = swapped(part, "expert", mask) if mask else part
        part = part.reshape(2, 2, per_group, 1, 1, capacity, half_width)
        hidden = lax.dynamic_update_slice(hidden, part[0], (0, 0, kind, r ^ mask, 0, 0))
        hidden = lax.dynamic_update_slice(hidden, part[1], (0, 0, 1 - kind, r ^ mask, 0, 0))
    return hidden.reshape(2, 1, 1, fsdp_size * group_size, capacity, half_width)


def solution(mesh):
    in_specs = (
        P("expert", None, "fsdp", None),
        P("expert", None, "fsdp", None),
        P("expert", None, "fsdp", None),
        P(None, ("fsdp", "expert"), None),
        P(None, ("fsdp", "expert"), None),
        P(),
    )
    out_specs = P(None, "fsdp", "expert", None, None, None)

    return jax.shard_map(
        on_device, mesh=mesh, in_specs=in_specs, out_specs=out_specs, check_vma=False
    )
```

time: 317 us -> 214 us (0.68)
  blocking collectives: 53.4 us -> 0 us
  waiting for transfers between devices: 145 us -> 93.5 us
  Pallas kernels: 0 us -> 37.8 us
  matrix products: 34.8 us -> 5.03 us
  starting transfers between devices: 25.7 us -> 52.4 us
  local copies, waits for them, and re-layouts: 34.7 us -> 9.24 us
  other arithmetic: 22.1 us -> 8.85 us
  between operations: 0.97 us -> 5.55 us
    all_to_all x6 -> x0, waiting for transfers between devices: 141 us -> none  [the longest x2 36.4 us: dispatch(): lax.all_to_all(lax.all_to_all(outgoing, 'fsdp', split_axis=0, concat_axis...]
    ppermute x1 -> x33, waiting for transfers between devices: 3.75 us -> 93.5 us  [the longest x27 78.1 us: swapped(): lax.ppermute(shard, axis, [(i, i ^ mask) for i in range(lax.axis_size(axi...]
    all_to_all x2 -> x0, blocking collectives: 53.4 us -> none  [the longest x1 29.8 us: dispatch(): lax.all_to_all(outgoing, 'fsdp', split_axis=0, concat_axis=0, tiled=True)]
    ppermute x1 -> x33, starting transfers between devices: 0.01 us -> 52.4 us  [the longest x27 37 us: swapped(): lax.ppermute(shard, axis, [(i, i ^ mask) for i in range(lax.axis_size(axi...]
    pallas_call x0 -> x4, Pallas kernels: none -> 37.8 us  [the longest x1 12.3 us: on_device(): pl.pallas_call(factor_kernel, out_shape=[shaped(jnp.bfloat16, hidden_widt...]
    dot_general x8 -> x1, matrix products: 34.8 us -> 5.03 us  [dot(): return jnp.dot(a, b, preferred_element_type=jnp.float32)]
    all_to_all x6 -> x0, starting transfers between devices: 25.7 us -> none  [the longest x2 10.2 us: dispatch(): lax.all_to_all(lax.all_to_all(outgoing, 'fsdp', split_axis=0, concat_axis...]
    convert_element_type x4 -> x0, local copies, waits for them, and re-layouts: 9.21 us -> none  [the longest x1 4.67 us: orthogonalize(): current = (values / (jnp.sqrt(squares_total) + eps)).astype(jnp.bfloat16)]
  transfers between devices with their start and end apart: 7 -> 33, of which waited for: 7 -> 17; matrix products, arithmetic and copies ran while one was open for 22% -> 6% of each run, Pallas kernels for 0% -> 14%
where the time goes in v1:
time: 214 us; the launch traced here: 212 us
  waiting for transfers between devices  93.5 us (44%)
  starting transfers between devices  52.4 us (24%)
  Pallas kernels  37.8 us (18%)
  local copies, waits for them, and re-layouts  9.24 us (4%)
  other arithmetic  8.85 us (4%)
  between operations  5.55 us (3%)
  matrix products  5.03 us (2%)
    ppermute x27, waiting for transfers between devices, swapped(): lax.ppermute(shard, axis, [(i, i ^ mask) for i in range(lax.axis_size(axi...  78.1 us
    ppermute x27, starting transfers between devices, swapped(): lax.ppermute(shard, axis, [(i, i ^ mask) for i in range(lax.axis_size(axi...  37 us
    ppermute x6, starting transfers between devices, moved_along(): return lax.ppermute(shard, 'expert', pairs)  15.5 us
    ppermute x6, waiting for transfers between devices, moved_along(): return lax.ppermute(shard, 'expert', pairs)  15.4 us
    pallas_call x1, Pallas kernels, on_device(): pl.pallas_call(factor_kernel, out_shape=[shaped(jnp.bfloat16, hidden_widt...  12.3 us
    pallas_call x1, Pallas kernels, on_device(): pl.pallas_call(functools.partial(moved_kernel, order), out_shape=[shaped(...  11.2 us
    pallas_call x1, Pallas kernels, on_device(): pl.pallas_call(functools.partial(base_kernel, near, update_scale), out_sh...  7.19 us
    pallas_call x1, Pallas kernels, on_device(): pl.pallas_call(functools.partial(finish_kernel, far, group_size), out_sha...  7.17 us
  transfers between devices with their start and end apart: 33, of which 17 were waited for; matrix products, arithmetic and copies ran while one was open for 6% of the time, Pallas kernels for 14%

profile of v1, /device:TPU:0, one launch (start us, length us, event | category | flops | bytes accessed | tf_op | source)
XLA Modules:
  0.0 212.4 jit_solution(14550804361333893441)
XLA Ops:
  2.0 3.1 %collective-permute-start = (bf16[1,32,2176]{2,1,0:T(8,128)(2,1)S(1)}, bf16[1,32,2176]{2,1,0:T(8,128)(2,1)S(1)}, u32[]{:S(2)}, u32[]{:S(2)}) collective-permute-start(bf16[1,32,2176]{2,1,0:T(8,128)(2,1)S(1)} %bitcast.98), channel_id=1, source_target_pairs={{0,16},{8,24},{16,0},{24,8},{1,17},{9,25},{17,1},{25,9},{2,18},{10... | collective-permute-start | bytes 417800 | tf_op jit(solution)/shard_map/ppermute | solution.py:30
  5.8 2.9 %collective-permute-done = bf16[1,32,2176]{2,1,0:T(8,128)(2,1)S(1)} collective-permute-done((bf16[1,32,2176]{2,1,0:T(8,128)(2,1)S(1)}, bf16[1,32,2176]{2,1,0:T(8,128)(2,1)S(1)}, u32[]{:S(2)}, u32[]{:S(2)}) %collective-permute-start) | collective-permute-done | bytes 139296 | tf_op jit(solution)/shard_map/ppermute | solution.py:30
  8.8 3.7 %collective-permute-start.1 = (bf16[2,32,2176]{2,1,0:T(8,128)(2,1)S(1)}, bf16[2,32,2176]{2,1,0:T(8,128)(2,1)S(1)}, u32[]{:S(2)}, u32[]{:S(2)}) collective-permute-start(bf16[2,32,2176]{2,1,0:T(8,128)(2,1)S(1)} %pad_maximum_fusion.1), channel_id=1, source_target_pairs={{0,2},{1,3},{2,4},{3,5},{4,6},{5,7},{8,10},{9,11},{10,12},{11,13},... | collective-permute-start | bytes 835592 | tf_op jit(solution)/shard_map/ppermute | solution.py:36
  17.5 4.1 %collective-permute-done.2 = bf16[2,32,2176]{2,1,0:T(8,128)(2,1)S(1)} collective-permute-done((bf16[2,32,2176]{2,1,0:T(8,128)(2,1)S(1)}, bf16[2,32,2176]{2,1,0:T(8,128)(2,1)S(1)}, u32[]{:S(2)}, u32[]{:S(2)}) %collective-permute-start.2) | collective-permute-done | bytes 278560 | tf_op jit(solution)/shard_map/ppermute | solution.py:36
  23.3 3.5 %collective-permute-start.3 = (bf16[2,32,2176]{2,1,0:T(8,128)(2,1)S(1)}, bf16[2,32,2176]{2,1,0:T(8,128)(2,1)S(1)}, u32[]{:S(2)}, u32[]{:S(2)}) collective-permute-start(bf16[2,32,2176]{2,1,0:T(8,128)(2,1)S(1)} %collective-permute-done.1), channel_id=1, source_target_pairs={{0,2},{1,3},{2,4},{3,5},{4,6},{5,7},{8,10},{9,11},{10,12},{11,13},... | collective-permute-start | bytes 835592 | tf_op jit(solution)/shard_map/ppermute | solution.py:36
  30.8 4.4 %collective-permute-start.5 = (bf16[2,32,2176]{2,1,0:T(8,128)(2,1)S(1)}, bf16[2,32,2176]{2,1,0:T(8,128)(2,1)S(1)}, u32[]{:S(2)}, u32[]{:S(2)}) collective-permute-start(bf16[2,32,2176]{2,1,0:T(8,128)(2,1)S(1)} %collective-permute-done.3), channel_id=1, source_target_pairs={{0,2},{1,3},{2,4},{3,5},{4,6},{5,7},{8,10},{9,11},{10,12},{11,13},... | collective-permute-start | bytes 835592 | tf_op jit(solution)/shard_map/ppermute | solution.py:36
  39.2 4.4 %collective-permute-done.6 = bf16[2,32,2176]{2,1,0:T(8,128)(2,1)S(1)} collective-permute-done((bf16[2,32,2176]{2,1,0:T(8,128)(2,1)S(1)}, bf16[2,32,2176]{2,1,0:T(8,128)(2,1)S(1)}, u32[]{:S(2)}, u32[]{:S(2)}) %collective-permute-start.6) | collective-permute-done | bytes 278560 | tf_op jit(solution)/shard_map/ppermute | solution.py:36
  44.7 5.6 %collective-permute-done.10 = bf16[2,32,2176]{2,1,0:T(8,128)(2,1)S(1)} collective-permute-done((bf16[2,32,2176]{2,1,0:T(8,128)(2,1)S(1)}, bf16[2,32,2176]{2,1,0:T(8,128)(2,1)S(1)}, u32[]{:S(2)}, u32[]{:S(2)}) %collective-permute-start.10) | collective-permute-done | bytes 278560 | tf_op jit(solution)/shard_map/ppermute | solution.py:30
  51.9 5.0 %convolution_convert_fusion.own_ref = bf16[512,2048]{1,0:T(8,128)(2,1)} fusion(bf16[640,2176]{1,0:T(8,128)(2,1)} %bitcast.118, s32[640]{0:T(1024)S(1)} %add_select_fusion), kind=kOutput, calls=%fused_computation | convolution fusion | flops 1343553536 | bytes 4721152 | tf_op jit(solution)/shard_map/dot_general | solution.py:26
  56.9 3.2 %fusion.4 = (bf16[512,768]{1,0:T(8,128)(2,1)}, bf16[512,768]{1,0:T(8,128)(2,1)}) fusion(bf16[4,512,768]{2,1,0:T(8,128)(2,1)S(1)} %bitcast.93, s32[]{:T(128)S(6)} %select_n.222, bf16[4,512,768]{2,1,0:T(8,128)(2,1)} %bitcast.95, s32[]{:T(128)S(6)} %select_n.221), kind=kLoop, calls=%fused_computation.13 | loop fusion | flops 5505024 | bytes 4718600 | tf_op jit(solution)/shard_map/convert_element_type | solution.py:260
  60.1 3.2 %fusion.8 = (bf16[512,768]{1,0:T(8,128)(2,1)}, bf16[512,768]{1,0:T(8,128)(2,1)}) fusion(bf16[4,512,768]{2,1,0:T(8,128)(2,1)S(1)} %bitcast.94, s32[]{:T(128)S(6)} %select_n.224, bf16[4,512,768]{2,1,0:T(8,128)(2,1)} %bitcast.96, s32[]{:T(128)S(6)} %select_n.223), kind=kLoop, calls=%fused_computation.17 | loop fusion | flops 5505024 | bytes 4718600 | tf_op jit(solution)/shard_map/convert_element_type | solution.py:260
  65.4 3.2 %constant_dynamic-slice_fusion.1 = (bf16[2,512,384]{2,1,0:T(8,128)(2,1)S(1)}, bf16[2,512,384]{2,1,0:T(8,128)(2,1)S(1)}, bf16[2,512,384]{2,1,0:T(8,128)(2,1)S(1)}, bf16[2,512,384]{2,1,0:T(8,128)(2,1)}) fusion(bf16[4,512,768]{2,1,0:T(8,128)(2,1)} %bitcast.97, s32[]{:T(128)S(6)} %select_n.237, s32[]{:T(128)S(6)} %select_n.239, s32[]{:T(128)S(6)} %select_n.233, ...), kind=kLoop, calls=%fused_computation.73 | loop fusion | bytes 6291488 | tf_op jit(solution)/shard_map/dynamic_slice | solution.py:271
  69.8 14.7 %collective-permute-done.13.refs_2_ = bf16[512,768]{1,0:T(8,128)(2,1)} collective-permute-done((bf16[512,768]{1,0:T(8,128)(2,1)}, bf16[512,768]{1,0:T(8,128)(2,1)}, u32[]{:S(2)}, u32[]{:S(2)}) %collective-permute-start.13) | collective-permute-done | bytes 786464 | tf_op jit(solution)/shard_map/ppermute | solution.py:30
  84.6 14.9 %collective-permute-done.14.refs_3_ = bf16[512,768]{1,0:T(8,128)(2,1)} collective-permute-done((bf16[512,768]{1,0:T(8,128)(2,1)}, bf16[512,768]{1,0:T(8,128)(2,1)}, u32[]{:S(2)}, u32[]{:S(2)}) %collective-permute-start.14) | collective-permute-done | bytes 786464 | tf_op jit(solution)/shard_map/ppermute | solution.py:30
  99.5 12.3 %factor.1 = (bf16[768,768]{1,0:T(8,128)(2,1)}, f32[1]{0:T(128)}) custom-call(bf16[512,768]{1,0:T(8,128)(2,1)} %get-tuple-element.42.refs_0_, bf16[512,768]{1,0:T(8,128)(2,1)} %copy-done.4, bf16[512,768]{1,0:T(8,128)(2,1)} %collective-permute-done.13.refs_2_, bf16[512,768]{1,0:T(8,128)(2,1)} %collective-permute-done.14.refs_3_), custom_call_target="tpu_custom_call" | custom-call | flops 9663676416 | bytes 4194304 | tf_op jit(solution)/shard_map/factor/pallas_call | solution.py:289
  111.8 11.2 %moved.1 = (bf16[2,512,384]{2,1,0:T(8,128)(2,1)}, bf16[2,512,384]{2,1,0:T(8,128)(2,1)}) custom-call(s32[2]{0:T(128)} %pad_add_fusion.at_ref, f32[1]{0:T(128)} %get-tuple-element.25.inverse_ref, bf16[768,768]{1,0:T(8,128)(2,1)} %get-tuple-element.26.factor_ref, bf16[512,2048]{1,0:T(8,128)(2,1)} %convolution_convert_fusion.own_ref, ...), custom_call_target="tpu_custom_call" | custom-call | flops 6442450944 | bytes 12582912 | tf_op jit(solution)/shard_map/moved/pallas_call | solution.py:305
  131.2 7.2 %base.1.base_ref = f32[2,512,768]{2,1,0:T(8,128)} custom-call(s32[2]{0:T(128)} %pad_add_fusion.at_ref, bf16[512,2048]{1,0:T(8,128)(2,1)} %convolution_convert_fusion.own_ref, bf16[512,2048]{1,0:T(8,128)(2,1)} %collective-permute-done.11.other_ref, bf16[2,512,384]{2,1,0:T(8,128)(2,1)} %get-tuple-element.27.kept_ref, ...), custom_call_target="tpu_custom_call" | custom-call | flops 3221225472 | bytes 10485760 | tf_op jit(solution)/shard_map/base/pallas_call | solution.py:324
  138.4 5.9 %collective-permute-done.17.refs_0_ = bf16[2,512,384]{2,1,0:T(8,128)(2,1)S(1)} collective-permute-done((bf16[2,512,384]{2,1,0:T(8,128)(2,1)S(1)}, bf16[2,512,384]{2,1,0:T(8,128)(2,1)S(1)}, u32[]{:S(2)}, u32[]{:S(2)}) %collective-permute-start.17) | collective-permute-done | bytes 786464 | tf_op jit(solution)/shard_map/ppermute | solution.py:30
  144.3 15.2 %collective-permute-done.18.refs_1_ = bf16[2,512,384]{2,1,0:T(8,128)(2,1)} collective-permute-done((bf16[2,512,384]{2,1,0:T(8,128)(2,1)S(1)}, bf16[2,512,384]{2,1,0:T(8,128)(2,1)}, u32[]{:S(2)}, u32[]{:S(2)}) %collective-permute-start.18) | collective-permute-done | bytes 786464 | tf_op jit(solution)/shard_map/ppermute | solution.py:30
  159.4 7.2 %finish.1 = (bf16[2,64,384]{2,1,0:T(8,128)(2,1)}, bf16[2,64,384]{2,1,0:T(8,128)(2,1)}, bf16[2,64,384]{2,1,0:T(8,128)(2,1)}, bf16[2,64,384]{2,1,0:T(8,128)(2,1)},...) custom-call(s32[2]{0:T(128)} %pad_add_fusion.at_ref, ...), custom_call_target="tpu_custom_call" | custom-call | flops 3221225472 | bytes 10485760 | tf_op jit(solution)/shard_map/finish/pallas_call | solution.py:342
  175.5 3.4 %collective-permute-start.25 = (bf16[2,64,384]{2,1,0:T(8,128)(2,1)}, bf16[2,64,384]{2,1,0:T(8,128)(2,1)S(1)}, u32[]{:S(2)}, u32[]{:S(2)}) collective-permute-start(bf16[2,64,384]{2,1,0:T(8,128)(2,1)} %get-tuple-element.36), channel_id=1, source_target_pairs={{0,7},{1,6},{2,5},{3,4},{4,3},{5,2},{6,1},{7,0},{8,15},{9,14},{10,... | collective-permute-start | bytes 294920 | tf_op jit(solution)/shard_map/ppermute | solution.py:30
  179.5 6.4 %collective-permute-done.22 = bf16[2,64,384]{2,1,0:T(8,128)(2,1)S(1)} collective-permute-done((bf16[2,64,384]{2,1,0:T(8,128)(2,1)}, bf16[2,64,384]{2,1,0:T(8,128)(2,1)S(1)}, u32[]{:S(2)}, u32[]{:S(2)}) %collective-permute-start.22) | collective-permute-done | bytes 98336 | tf_op jit(solution)/shard_map/ppermute | solution.py:30
  189.7 4.1 %collective-permute-start.27 = (bf16[2,64,384]{2,1,0:T(8,128)(2,1)S(1)}, bf16[2,64,384]{2,1,0:T(8,128)(2,1)S(1)}, u32[]{:S(2)}, u32[]{:S(2)}) collective-permute-start(bf16[2,64,384]{2,1,0:T(8,128)(2,1)S(1)} %get-tuple-element.54), channel_id=1, source_target_pairs={{0,2},{1,3},{2,0},{3,1},{4,6},{5,7},{6,4},{7,5},{8,10},{9,11},{10,... | collective-permute-start | bytes 294920 | tf_op jit(solution)/shard_map/ppermute | solution.py:30
  202.3 6.3 %collective-permute-done.29 = bf16[2,64,384]{2,1,0:T(8,128)(2,1)S(1)} collective-permute-done((bf16[2,64,384]{2,1,0:T(8,128)(2,1)S(1)}, bf16[2,64,384]{2,1,0:T(8,128)(2,1)S(1)}, u32[]{:S(2)}, u32[]{:S(2)}) %collective-permute-start.29) | collective-permute-done | bytes 98336 | tf_op jit(solution)/shard_map/ppermute | solution.py:30
  (132 shorter events, 51.7 us)
Async XLA Ops:
  8.8 8.8 %collective-permute-start.1 = (bf16[2,32,2176]{2,1,0:T(8,128)(2,1)S(1)}, bf16[2,32,2176]{2,1,0:T(8,128)(2,1)S(1)}, u32[]{:S(2)}, u32[]{:S(2)}) collective-permute-start(bf16[2,32,2176]{2,1,0:T(8,128)(2,1)S(1)} %pad_maximum_fusion.1), channel_id=1, source_target_pairs={{0,2},{1,3},{2,4},{3,5},{4,6},{5,7},{8,10},{9,11},{10,12},{11,13},... | collective-permute-start | bytes 835592 | tf_op jit(solution)/shard_map/ppermute | solution.py:36
  12.5 9.2 %collective-permute-start.2 = (bf16[2,32,2176]{2,1,0:T(8,128)(2,1)S(1)}, bf16[2,32,2176]{2,1,0:T(8,128)(2,1)S(1)}, u32[]{:S(2)}, u32[]{:S(2)}) collective-permute-start(bf16[2,32,2176]{2,1,0:T(8,128)(2,1)S(1)} %pad_maximum_fusion.1), channel_id=1, source_target_pairs={{2,0},{3,1},{4,2},{5,3},{6,4},{7,5},{10,8},{11,9},{12,10},{13,11},... | collective-permute-start | bytes 835592 | tf_op jit(solution)/shard_map/ppermute | solution.py:36
  13.8 30.5 %collective-permute-start.7 = (bf16[2,32,2176]{2,1,0:T(8,128)(2,1)S(1)}, bf16[2,32,2176]{2,1,0:T(8,128)(2,1)S(1)}, u32[]{:S(2)}, u32[]{:S(2)}) collective-permute-start(bf16[2,32,2176]{2,1,0:T(8,128)(2,1)S(1)} %pad_maximum_fusion.1), channel_id=1, source_target_pairs={{0,1},{1,0},{2,3},{3,2},{4,5},{5,4},{6,7},{7,6},{8,9},{9,8},{10,11... | collective-permute-start | bytes 835592 | tf_op jit(solution)/shard_map/ppermute | solution.py:30
  21.7 22.6 %collective-permute-start.8 = (bf16[4,32,2176]{2,1,0:T(8,128)(2,1)S(1)}, bf16[4,32,2176]{2,1,0:T(8,128)(2,1)S(1)}, u32[]{:S(2)}, u32[]{:S(2)}) collective-permute-start(bf16[4,32,2176]{2,1,0:T(8,128)(2,1)S(1)} %pad_maximum_fusion), channel_id=1, source_target_pairs={{0,1},{1,0},{2,3},{3,2},{4,5},{5,4},{6,7},{7,6},{8,9},{9,8},{10,11... | collective-permute-start | bytes 1671176 | tf_op jit(solution)/shard_map/ppermute | solution.py:30
  26.7 8.4 %collective-permute-start.4 = (bf16[2,32,2176]{2,1,0:T(8,128)(2,1)S(1)}, bf16[2,32,2176]{2,1,0:T(8,128)(2,1)S(1)}, u32[]{:S(2)}, u32[]{:S(2)}) collective-permute-start(bf16[2,32,2176]{2,1,0:T(8,128)(2,1)S(1)} %collective-permute-done.2), channel_id=1, source_target_pairs={{2,0},{3,1},{4,2},{5,3},{6,4},{7,5},{10,8},{11,9},{12,10},{13,11},... | collective-permute-start | bytes 835592 | tf_op jit(solution)/shard_map/ppermute | solution.py:36
  30.8 8.4 %collective-permute-start.5 = (bf16[2,32,2176]{2,1,0:T(8,128)(2,1)S(1)}, bf16[2,32,2176]{2,1,0:T(8,128)(2,1)S(1)}, u32[]{:S(2)}, u32[]{:S(2)}) collective-permute-start(bf16[2,32,2176]{2,1,0:T(8,128)(2,1)S(1)} %collective-permute-done.3), channel_id=1, source_target_pairs={{0,2},{1,3},{2,4},{3,5},{4,6},{5,7},{8,10},{9,11},{10,12},{11,13},... | collective-permute-start | bytes 835592 | tf_op jit(solution)/shard_map/ppermute | solution.py:36
  35.2 8.4 %collective-permute-start.6 = (bf16[2,32,2176]{2,1,0:T(8,128)(2,1)S(1)}, bf16[2,32,2176]{2,1,0:T(8,128)(2,1)S(1)}, u32[]{:S(2)}, u32[]{:S(2)}) collective-permute-start(bf16[2,32,2176]{2,1,0:T(8,128)(2,1)S(1)} %collective-permute-done.4), channel_id=1, source_target_pairs={{2,0},{3,1},{4,2},{5,3},{6,4},{7,5},{10,8},{11,9},{12,10},{13,11},... | collective-permute-start | bytes 835592 | tf_op jit(solution)/shard_map/ppermute | solution.py:36
  56.9 54.9 %collective-permute-start.11 = (bf16[512,2048]{1,0:T(8,128)(2,1)}, bf16[512,2048]{1,0:T(8,128)(2,1)}, u32[]{:S(2)}, u32[]{:S(2)}) collective-permute-start(bf16[512,2048]{1,0:T(8,128)(2,1)} %convolution_convert_fusion.own_ref), channel_id=1, source_target_pairs={{0,8},{8,0},{16,24},{24,16},{1,9},{9,1},{17,25},{25,17},{2,10},{10... | collective-permute-start | bytes 6291464 | tf_op jit(solution)/shard_map/ppermute | solution.py:30
  63.8 20.7 %collective-permute-start.13 = (bf16[512,768]{1,0:T(8,128)(2,1)}, bf16[512,768]{1,0:T(8,128)(2,1)}, u32[]{:S(2)}, u32[]{:S(2)}) collective-permute-start(bf16[512,768]{1,0:T(8,128)(2,1)} %get-tuple-element.23), channel_id=1, source_target_pairs={{0,16},{8,24},{16,0},{24,8},{1,17},{9,25},{17,1},{25,9},{2,18},{10... | collective-permute-start | bytes 2359304 | tf_op jit(solution)/shard_map/ppermute | solution.py:30
  65.4 34.1 %collective-permute-start.14 = (bf16[512,768]{1,0:T(8,128)(2,1)}, bf16[512,768]{1,0:T(8,128)(2,1)}, u32[]{:S(2)}, u32[]{:S(2)}) collective-permute-start(bf16[512,768]{1,0:T(8,128)(2,1)} %get-tuple-element.24), channel_id=1, source_target_pairs={{0,24},{8,16},{16,8},{24,0},{1,25},{9,17},{17,9},{25,1},{2,26},{10... | collective-permute-start | bytes 2359304 | tf_op jit(solution)/shard_map/ppermute | solution.py:30
  68.5 62.6 %collective-permute-start.16 = (bf16[2,512,384]{2,1,0:T(8,128)(2,1)S(1)}, bf16[2,512,384]{2,1,0:T(8,128)(2,1)}, u32[]{:S(2)}, u32[]{:S(2)}) collective-permute-start(bf16[2,512,384]{2,1,0:T(8,128)(2,1)S(1)} %get-tuple-element.47), channel_id=1, source_target_pairs={{0,8},{8,0},{16,24},{24,16},{1,9},{9,1},{17,25},{25,17},{2,10},{10... | collective-permute-start | bytes 2359304 | tf_op jit(solution)/shard_map/ppermute | solution.py:30
  123.8 20.4 %collective-permute-start.17 = (bf16[2,512,384]{2,1,0:T(8,128)(2,1)S(1)}, bf16[2,512,384]{2,1,0:T(8,128)(2,1)S(1)}, u32[]{:S(2)}, u32[]{:S(2)}) collective-permute-start(bf16[2,512,384]{2,1,0:T(8,128)(2,1)S(1)} %get-tuple-element.46), channel_id=1, source_target_pairs={{0,16},{8,24},{16,0},{24,8},{1,17},{9,25},{17,1},{25,9},{2,18},{10... | collective-permute-start | bytes 2359304 | tf_op jit(solution)/shard_map/ppermute | solution.py:30
  125.4 34.1 %collective-permute-start.18 = (bf16[2,512,384]{2,1,0:T(8,128)(2,1)S(1)}, bf16[2,512,384]{2,1,0:T(8,128)(2,1)}, u32[]{:S(2)}, u32[]{:S(2)}) collective-permute-start(bf16[2,512,384]{2,1,0:T(8,128)(2,1)S(1)} %get-tuple-element.45), channel_id=1, source_target_pairs={{0,24},{8,16},{16,8},{24,0},{1,25},{9,17},{17,9},{25,1},{2,26},{10... | collective-permute-start | bytes 2359304 | tf_op jit(solution)/shard_map/ppermute | solution.py:30
  169.8 9.7 %collective-permute-start.21 = (bf16[2,64,384]{2,1,0:T(8,128)(2,1)}, bf16[2,64,384]{2,1,0:T(8,128)(2,1)S(1)}, u32[]{:S(2)}, u32[]{:S(2)}) collective-permute-start(bf16[2,64,384]{2,1,0:T(8,128)(2,1)} %get-tuple-element.32), channel_id=1, source_target_pairs={{0,3},{1,2},{2,1},{3,0},{4,7},{5,6},{6,5},{7,4},{8,11},{9,10},{10,... | collective-permute-start | bytes 294920 | tf_op jit(solution)/shard_map/ppermute | solution.py:30
  171.1 14.7 %collective-permute-start.22 = (bf16[2,64,384]{2,1,0:T(8,128)(2,1)}, bf16[2,64,384]{2,1,0:T(8,128)(2,1)S(1)}, u32[]{:S(2)}, u32[]{:S(2)}) collective-permute-start(bf16[2,64,384]{2,1,0:T(8,128)(2,1)} %get-tuple-element.33), channel_id=1, source_target_pairs={{0,4},{1,5},{2,6},{3,7},{4,0},{5,1},{6,2},{7,3},{8,12},{9,13},{10,... | collective-permute-start | bytes 294920 | tf_op jit(solution)/shard_map/ppermute | solution.py:30
  173.0 15.5 %collective-permute-start.23 = (bf16[2,64,384]{2,1,0:T(8,128)(2,1)}, bf16[2,64,384]{2,1,0:T(8,128)(2,1)S(1)}, u32[]{:S(2)}, u32[]{:S(2)}) collective-permute-start(bf16[2,64,384]{2,1,0:T(8,128)(2,1)} %get-tuple-element.34), channel_id=1, source_target_pairs={{0,5},{1,4},{2,7},{3,6},{4,1},{5,0},{6,3},{7,2},{8,13},{9,12},{10,... | collective-permute-start | bytes 294920 | tf_op jit(solution)/shard_map/ppermute | solution.py:30
  174.0 14.5 %collective-permute-start.24 = (bf16[2,64,384]{2,1,0:T(8,128)(2,1)}, bf16[2,64,384]{2,1,0:T(8,128)(2,1)S(1)}, u32[]{:S(2)}, u32[]{:S(2)}) collective-permute-start(bf16[2,64,384]{2,1,0:T(8,128)(2,1)} %get-tuple-element.35), channel_id=1, source_target_pairs={{0,6},{1,7},{2,4},{3,5},{4,2},{5,3},{6,0},{7,1},{8,14},{9,15},{10,... | collective-permute-start | bytes 294920 | tf_op jit(solution)/shard_map/ppermute | solution.py:30
  175.5 13.1 %collective-permute-start.25 = (bf16[2,64,384]{2,1,0:T(8,128)(2,1)}, bf16[2,64,384]{2,1,0:T(8,128)(2,1)S(1)}, u32[]{:S(2)}, u32[]{:S(2)}) collective-permute-start(bf16[2,64,384]{2,1,0:T(8,128)(2,1)} %get-tuple-element.36), channel_id=1, source_target_pairs={{0,7},{1,6},{2,5},{3,4},{4,3},{5,2},{6,1},{7,0},{8,15},{9,14},{10,... | collective-permute-start | bytes 294920 | tf_op jit(solution)/shard_map/ppermute | solution.py:30
  188.7 9.1 %collective-permute-start.26 = (bf16[2,64,384]{2,1,0:T(8,128)(2,1)S(1)}, bf16[2,64,384]{2,1,0:T(8,128)(2,1)S(1)}, u32[]{:S(2)}, u32[]{:S(2)}) collective-permute-start(bf16[2,64,384]{2,1,0:T(8,128)(2,1)S(1)} %get-tuple-element.55), channel_id=1, source_target_pairs={{0,1},{1,0},{2,3},{3,2},{4,5},{5,4},{6,7},{7,6},{8,9},{9,8},{10,11... | collective-permute-start | bytes 294920 | tf_op jit(solution)/shard_map/ppermute | solution.py:30
  189.7 9.9 %collective-permute-start.27 = (bf16[2,64,384]{2,1,0:T(8,128)(2,1)S(1)}, bf16[2,64,384]{2,1,0:T(8,128)(2,1)S(1)}, u32[]{:S(2)}, u32[]{:S(2)}) collective-permute-start(bf16[2,64,384]{2,1,0:T(8,128)(2,1)S(1)} %get-tuple-element.54), channel_id=1, source_target_pairs={{0,2},{1,3},{2,0},{3,1},{4,6},{5,7},{6,4},{7,5},{8,10},{9,11},{10,... | collective-permute-start | bytes 294920 | tf_op jit(solution)/shard_map/ppermute | solution.py:30
  194.2 14.5 %collective-permute-start.29 = (bf16[2,64,384]{2,1,0:T(8,128)(2,1)S(1)}, bf16[2,64,384]{2,1,0:T(8,128)(2,1)S(1)}, u32[]{:S(2)}, u32[]{:S(2)}) collective-permute-start(bf16[2,64,384]{2,1,0:T(8,128)(2,1)S(1)} %get-tuple-element.52), channel_id=1, source_target_pairs={{0,4},{1,5},{2,6},{3,7},{4,0},{5,1},{6,2},{7,3},{8,12},{9,13},{10,... | collective-permute-start | bytes 294920 | tf_op jit(solution)/shard_map/ppermute | solution.py:30
  196.8 14.5 %collective-permute-start.30 = (bf16[2,64,384]{2,1,0:T(8,128)(2,1)S(1)}, bf16[2,64,384]{2,1,0:T(8,128)(2,1)S(1)}, u32[]{:S(2)}, u32[]{:S(2)}) collective-permute-start(bf16[2,64,384]{2,1,0:T(8,128)(2,1)S(1)} %get-tuple-element.51), channel_id=1, source_target_pairs={{0,5},{1,4},{2,7},{3,6},{4,1},{5,0},{6,3},{7,2},{8,13},{9,12},{10,... | collective-permute-start | bytes 294920 | tf_op jit(solution)/shard_map/ppermute | solution.py:30
  197.8 13.6 %collective-permute-start.31 = (bf16[2,64,384]{2,1,0:T(8,128)(2,1)S(1)}, bf16[2,64,384]{2,1,0:T(8,128)(2,1)S(1)}, u32[]{:S(2)}, u32[]{:S(2)}) collective-permute-start(bf16[2,64,384]{2,1,0:T(8,128)(2,1)S(1)} %get-tuple-element.50), channel_id=1, source_target_pairs={{0,6},{1,7},{2,4},{3,5},{4,2},{5,3},{6,0},{7,1},{8,14},{9,15},{10,... | collective-permute-start | bytes 294920 | tf_op jit(solution)/shard_map/ppermute | solution.py:30
  199.6 11.9 %collective-permute-start.32 = (bf16[2,64,384]{2,1,0:T(8,128)(2,1)S(1)}, bf16[2,64,384]{2,1,0:T(8,128)(2,1)S(1)}, u32[]{:S(2)}, u32[]{:S(2)}) collective-permute-start(bf16[2,64,384]{2,1,0:T(8,128)(2,1)S(1)} %get-tuple-element.49), channel_id=1, source_target_pairs={{0,7},{1,6},{2,5},{3,4},{4,3},{5,2},{6,1},{7,0},{8,15},{9,14},{10,... | collective-permute-start | bytes 294920 | tf_op jit(solution)/shard_map/ppermute | solution.py:30
  (15 other events, 132.7 us)

commit v2 on v1

v2 whole, which is shorter than its diff:
```python
import functools
import math

import jax
import jax.numpy as jnp
import numpy as np
from jax import lax
from jax.experimental import pallas as pl
from jax.experimental.pallas import tpu as pltpu
from jax.sharding import PartitionSpec as P


momentum_decay = 0.95
coef_first = 3.4445
coef_second = -4.775
coef_third = 2.0315
step_size = 0.02
eps = 1e-07


VMEM = pl.BlockSpec(memory_space=pltpu.VMEM)
SMEM = pl.BlockSpec(memory_space=pltpu.SMEM)


def dot(a, b):
    return jnp.dot(a, b, preferred_element_type=jnp.float32)


def swapped(shard, axis, mask):
    return lax.ppermute(shard, axis, [(i, i ^ mask) for i in range(lax.axis_size(axis))])


def slots_of(routes, experts):
    labels = lax.broadcasted_iota(jnp.int32, (1, 1, 1, experts), 3)
    routed = jnp.any(routes[:, :, :, None] == labels, axis=2).astype(jnp.int32)
    count = routes.shape[1]
    later = lax.broadcasted_iota(jnp.int32, (count, count), 0)
    earlier = lax.broadcasted_iota(jnp.int32, (count, count), 1)
    upto = (earlier <= later).astype(jnp.int32)
    place = jnp.sum(upto[None, :, :, None] * routed[:, None, :, :], axis=2)
    return jnp.where(routed == 1, place, 0)


def gathered(block):
    fsdp_size, group_size = lax.axis_size("fsdp"), lax.axis_size("expert")
    f, r = lax.axis_index("fsdp"), lax.axis_index("expert")
    held, masks = block[None], [0]
    if group_size == 8:
        mask = 2
        while mask < fsdp_size:
            held = jnp.concatenate([held, swapped(held, "fsdp", mask)])
            masks += [m ^ mask for m in masks]
            mask *= 2
        beside = swapped(held, "expert", 2)
        opposite = swapped(held, "expert", 6)
        across = [swapped(held, "expert", 1), swapped(beside, "expert", 1)]
        last = swapped(opposite, "expert", 2)
        across += [swapped(opposite, "expert", 1), swapped(last, "expert", 1)]
        rows = jnp.concatenate([held, beside, opposite, last, *across])
        source_r = jnp.repeat(r ^ np.array([0, 2, 6, 4, 1, 3, 7, 5], np.int32), len(masks))
        source_f = jnp.tile(f ^ np.array(masks, np.int32), 8)
        return rows, source_f // 2, source_r
    held = lax.all_gather(block, "expert")
    mask = 2
    while mask < fsdp_size:
        held = jnp.concatenate([held, swapped(held, "fsdp", mask)])
        masks += [m ^ mask for m in masks]
        mask *= 2
    source_f = jnp.repeat(f ^ np.array(masks, np.int32), group_size)
    source_r = jnp.tile(jnp.arange(group_size, dtype=jnp.int32), len(masks))
    return held, source_f // 2, source_r


def columns_of(index, width):
    return pl.ds(pl.multiple_of(index * width, 128), width)


def gram_of(update_refs, total):
    for rows_ref in update_refs:
        rows = rows_ref[...]
        term = lax.dot_general(
            rows, rows, (((0,), (0,)), ((), ())), preferred_element_type=jnp.float32
        )
        total = term if total is None else total + term
    return total


def gram_kernel(*refs):
    refs[-1][...] = gram_of(refs[:-1], None)


def factor_kernel(gram_ref, *refs):
    update_refs, (factor_ref, inverse_ref) = refs[:-2], refs[-2:]
    gram = gram_of(update_refs, gram_ref[...])
    diagonal = lax.broadcasted_iota(jnp.int32, gram.shape, 0) == lax.broadcasted_iota(
        jnp.int32, gram.shape, 1
    )
    inverse = 1.0 / (jnp.sqrt(jnp.sum(jnp.where(diagonal, gram, 0.0))) + eps)
    inverse_ref[0] = inverse
    gram0 = gram * inverse * inverse
    g0 = gram0.astype(jnp.bfloat16)
    p0 = (coef_second * gram0 + coef_third * dot(g0, g0)).astype(jnp.bfloat16)
    half_way = coef_first * gram0 + dot(g0, p0)
    gram1 = coef_first * half_way + dot(half_way.astype(jnp.bfloat16), p0)
    g1 = gram1.astype(jnp.bfloat16)
    p1 = (coef_second * gram1 + coef_third * dot(g1, g1)).astype(jnp.bfloat16)
    factor = coef_first * (p0.astype(jnp.float32) + p1.astype(jnp.float32)) + dot(p0, p1)
    factor_ref[...] = factor.astype(jnp.bfloat16)


def rows_at(at_ref, place, rows_ref, depth):
    return rows_ref[:, columns_of(at_ref[0] ^ place, depth)]


def along_kernel(order, scale, at_ref, inverse_ref, factor_ref, own_ref, other_ref, *refs):
    count = len(order)
    update_refs, weight_refs, (base_ref, sent_ref) = refs[:count], refs[count:-2], refs[-2:]
    width = sent_ref.shape[2]
    depth = update_refs[0].shape[0]
    own_kind = lax.rem(at_ref[0], 2)
    for side, rows_ref in enumerate((own_ref, other_ref)):
        total = sum(
            dot(rows_at(at_ref, place, rows_ref, depth), u[...])
            for place, u in zip(order, update_refs)
        )
        along = total * inverse_ref[0]
        moved = coef_first * coef_first * along + dot(along.astype(jnp.bfloat16), factor_ref[...])
        left, right = moved[:, :width], moved[:, width:]
        sent_ref[1 - side] = jnp.where(own_kind == 0, right, left).astype(jnp.bfloat16)
        kept = scale * jnp.where(own_kind == 0, left, right)
        for kind in range(2):
            product = sum(
                dot(rows_at(at_ref, place, rows_ref, depth), weight[kind])
                for place, weight in zip(order, weight_refs)
            )
            base_ref[kind, side] = product - jnp.where(own_kind == kind, kept, 0.0)


def finish_kernel(order, group_size, scale, at_ref, own_ref, other_ref, base_ref, moved_ref, *refs):
    count = len(order)
    weight_refs, out_refs, hidden = refs[:count], refs[count:-1], refs[-1]
    depth = weight_refs[0].shape[1]
    own_kind = lax.rem(at_ref[0], 2)
    for side, rows_ref in enumerate((own_ref, other_ref)):
        moved = scale * moved_ref[side].astype(jnp.float32)
        products = []
        for kind in range(2):
            total = base_ref[kind, side] - jnp.where(own_kind == kind, 0.0, moved)
            for place, weight in zip(order, weight_refs):
                total += dot(rows_at(at_ref, place, rows_ref, depth), weight[kind])
            products.append(total)
        gate, up = products
        hidden[side] = (gate / (1.0 + jnp.exp(-gate)) * up).astype(jnp.bfloat16)
    chunk = hidden.shape[1] // group_size
    for mask in range(group_size):
        start = pl.multiple_of((at_ref[1] ^ mask) * chunk, chunk)
        out_refs[mask][...] = hidden[:, pl.ds(start, chunk), :]


def choose_kernel(at_ref, owners_ref, *refs):
    held = refs[-1]
    count = held.shape[0]
    for mask in range(count):
        held[mask] = refs[mask][...]
    for mask in range(count):
        owner = owners_ref[at_ref[0], at_ref[1] ^ mask]
        refs[count + mask][...] = held[owner ^ at_ref[1]]


def on_device(momentum, gradient, weights, tokens, routes, owners):
    fsdp_size = lax.axis_size("fsdp")
    group_size = lax.axis_size("expert")
    per_group = fsdp_size // 2
    experts = per_group * group_size
    local_rows = momentum.shape[2]
    hidden_width = momentum.shape[3]
    half_width = hidden_width // 2
    model_width = tokens.shape[2]
    tok_dev = tokens.shape[1]
    top_count = routes.shape[2]
    capacity = max(2, 2 * tok_dev * top_count // experts)
    f = lax.axis_index("fsdp")
    r = lax.axis_index("expert")
    own_expert = r * per_group + f // 2
    at = jnp.stack([f, r]).astype(jnp.int32)
    near = [0, 1]
    far = list(range(2, fsdp_size))
    order = near + far

    slot_lanes = -(-experts // 128) * 128
    slots = slots_of(routes, experts).astype(jnp.bfloat16)
    slots = jnp.pad(slots, ((0, 0), (0, 0), (0, slot_lanes - experts)))
    block = jnp.concatenate([tokens, slots], axis=2).reshape(2 * tok_dev, model_width + slot_lanes)
    blocks, source_pair, source_group = gathered(block)
    all_rows = blocks.reshape(-1, model_width + slot_lanes)
    lane = lax.broadcasted_iota(jnp.int32, (1, slot_lanes), 1)
    picked = jnp.where(lane == own_expert, all_rows[:, model_width:].astype(jnp.float32), 0.0)
    slot = jnp.sum(picked, axis=1).astype(jnp.int32).reshape(-1, 2, tok_dev)
    batch = jnp.arange(2, dtype=jnp.int32)[None, :, None]
    first = (source_group[:, None, None] * 2 + batch) * per_group + source_pair[:, None, None]
    listed_at = jnp.where(slot > 0, first * capacity + slot - 1, -1).reshape(1, -1)
    half_rows = group_size * 2 * per_group * capacity
    labels = lax.broadcasted_iota(jnp.int32, (half_rows, listed_at.shape[1]), 0)
    select = (labels == listed_at).astype(jnp.bfloat16)
    own_rows = dot(select, all_rows[:, :model_width]).astype(jnp.bfloat16)
    other_rows = swapped(own_rows, "fsdp", 1)

    moment = momentum.reshape(fsdp_size, local_rows, hidden_width)
    grad = gradient.reshape(fsdp_size, local_rows, hidden_width)
    weight = weights.reshape(fsdp_size, local_rows, hidden_width)
    update, held_weight = [None] * fsdp_size, [None] * fsdp_size
    for places in (far, near):
        for mask in reversed(places):
            moment_part = lax.dynamic_index_in_dim(moment, f ^ mask, 0, keepdims=False)
            grad_part = lax.dynamic_index_in_dim(grad, f ^ mask, 0, keepdims=False)
            grad_part = grad_part.astype(jnp.float32)
            accumulated = momentum_decay * moment_part.astype(jnp.float32) + grad_part
            update[mask] = (grad_part + momentum_decay * accumulated).astype(jnp.bfloat16)
        if places is far:
            moment, grad, *parts = lax.optimization_barrier(
                (moment, grad, *[update[m] for m in far])
            )
            for mask, part in zip(far, parts):
                update[mask] = part
    for mask in reversed(range(1, fsdp_size)):
        update[mask] = swapped(update[mask], "fsdp", mask)
    for mask in reversed(range(fsdp_size)):
        target = f ^ mask
        part = lax.dynamic_slice(
            weight,
            (target // 2 * 2, 0, target % 2 * half_width),
            (2, local_rows, half_width),
        )
        held_weight[mask] = swapped(part, "fsdp", mask) if mask else part

    full_rows = fsdp_size * local_rows
    update_scale = step_size * 0.2 * math.sqrt(max(full_rows, hidden_width))
    bf16_scratch = lambda *shape: pltpu.VMEM(shape, jnp.bfloat16)
    shaped = lambda kind, *shape: jax.ShapeDtypeStruct(shape, kind)
    flops = 2 * 2 * half_rows * full_rows * hidden_width
    cost = lambda work, moved_bytes: pl.CostEstimate(
        flops=work, bytes_accessed=moved_bytes, transcendentals=0
    )
    limit = lambda mebibytes: pltpu.CompilerParams(vmem_limit_bytes=mebibytes << 20)
    early, late = near + far[1:], far[:1]
    gram = pl.pallas_call(
        gram_kernel,
        out_shape=shaped(jnp.float32, hidden_width, hidden_width),
        in_specs=[VMEM] * len(early),
        out_specs=VMEM,
        compiler_params=limit(8),
        cost_estimate=cost(flops, 4 << 20),
        name="gram",
    )(*[update[m] for m in early])
    factor, inverse = pl.pallas_call(
        factor_kernel,
        out_shape=[
            shaped(jnp.bfloat16, hidden_width, hidden_width),
            shaped(jnp.float32, 1),
        ],
        in_specs=[VMEM] * (1 + len(late)),
        out_specs=[VMEM, SMEM],
        compiler_params=limit(14),
        cost_estimate=cost(2 * flops, 4 << 20),
        name="factor",
    )(gram, *[update[m] for m in late])

    kind = f % 2
    half_shape = (2, half_rows, half_width)
    base, sent = pl.pallas_call(
        functools.partial(along_kernel, order, update_scale),
        out_shape=[
            shaped(jnp.float32, 2, *half_shape),
            shaped(jnp.bfloat16, *half_shape),
        ],
        in_specs=[SMEM, SMEM] + [VMEM] * (3 + len(order) + len(near)),
        out_specs=[VMEM, VMEM],
        cost_estimate=cost(2 * flops, 12 << 20),
        compiler_params=limit(10),
        name="along",
    )(
        at,
        inverse,
        factor,
        own_rows,
        other_rows,
        *[update[m] for m in order],
        *[held_weight[m] for m in near],
    )
    partner = swapped(sent, "fsdp", 1)
    chunk = half_rows // group_size
    pieces = pl.pallas_call(
        functools.partial(finish_kernel, far, group_size, update_scale),
        out_shape=[shaped(jnp.bfloat16, 2, chunk, half_width)] * group_size,
        in_specs=[SMEM] + [VMEM] * (4 + len(far)),
        out_specs=[VMEM] * group_size,
        scratch_shapes=[bf16_scratch(*half_shape)],
        cost_estimate=cost(flops, 10 << 20),
        compiler_params=limit(8),
        name="finish",
    )(at, own_rows, other_rows, base, partner, *[held_weight[m] for m in far])

    spread = [swapped(pieces[m], "expert", m) if m else pieces[m] for m in range(group_size)]
    part_shape = spread[0].shape
    chosen = pl.pallas_call(
        choose_kernel,
        out_shape=[shaped(jnp.bfloat16, *part_shape)] * group_size,
        in_specs=[SMEM, SMEM] + [VMEM] * group_size,
        out_specs=[VMEM] * group_size,
        scratch_shapes=[bf16_scratch(group_size, *part_shape)],
        cost_estimate=cost(0, 2 << 20),
        compiler_params=limit(8),
        name="choose",
    )(at, owners, *spread)
    hidden = jnp.zeros((2, per_group, 2, group_size, capacity, half_width), jnp.bfloat16)
    for mask in range(group_size):
        part = chosen[mask]
        part = swapped(part, "expert", mask) if mask else part
        part = part.reshape(2, 2, per_group, 1, 1, capacity, half_width)
        hidden = lax.dynamic_update_slice(hidden, part[0], (0, 0, kind, r ^ mask, 0, 0))
        hidden = lax.dynamic_update_slice(hidden, part[1], (0, 0, 1 - kind, r ^ mask, 0, 0))
    return hidden.reshape(2, 1, 1, fsdp_size * group_size, capacity, half_width)


def solution(mesh):
    in_specs = (
        P("expert", None, "fsdp", None),
        P("expert", None, "fsdp", None),
        P("expert", None, "fsdp", None),
        P(None, ("fsdp", "expert"), None),
        P(None, ("fsdp", "expert"), None),
        P(),
    )
    out_specs = P(None, "fsdp", "expert", None, None, None)

    return jax.shard_map(
        on_device, mesh=mesh, in_specs=in_specs, out_specs=out_specs, check_vma=False
    )
```

time: 214 us -> 176 us (0.82)
  Pallas kernels: 37.8 us -> 26.9 us
  starting transfers between devices: 52.4 us -> 42.5 us
  waiting for transfers between devices: 93.5 us -> 86.9 us
  between operations: 5.55 us -> 0.39 us
  local copies, waits for them, and re-layouts: 9.24 us -> 6.21 us
  matrix products: 5.03 us -> 2.84 us
    ppermute x6 -> x0, starting transfers between devices: 15.5 us -> none  [moved_along(): return lax.ppermute(shard, 'expert', pairs)]
    ppermute x6 -> x0, waiting for transfers between devices: 15.4 us -> none  [moved_along(): return lax.ppermute(shard, 'expert', pairs)]
    ppermute x27 -> x30, waiting for transfers between devices: 78.1 us -> 86.9 us  [swapped(): lax.ppermute(shard, axis, [(i, i ^ mask) for i in range(lax.axis_size(axi...]
    pallas_call x3 -> x4, Pallas kernels: 25.5 us -> 19.1 us  [the longest x1 10.9 us: on_device(): pl.pallas_call(functools.partial(along_kernel, order, update_scale), out_...]
    ppermute x27 -> x30, starting transfers between devices: 37 us -> 42.5 us  [swapped(): lax.ppermute(shard, axis, [(i, i ^ mask) for i in range(lax.axis_size(axi...]
    pallas_call x1, Pallas kernels: 12.3 us -> 7.75 us  [on_device(): pl.pallas_call(factor_kernel, out_shape=[shaped(jnp.bfloat16, hidden_widt...]
    dot_general x1, matrix products: 5.03 us -> 2.84 us  [dot(): return jnp.dot(a, b, preferred_element_type=jnp.float32)]
  transfers between devices with their start and end apart: 33 -> 30, of which waited for: 17 -> 12; matrix products, arithmetic and copies ran while one was open for 6% -> 6% of each run, Pallas kernels for 14% -> 13%
where the time goes in v2:
time: 176 us; the launch traced here: 175 us
  waiting for transfers between devices  86.9 us (49%)
  starting transfers between devices  42.5 us (24%)
  Pallas kernels  26.9 us (15%)
  other arithmetic  9.29 us (5%)
  local copies, waits for them, and re-layouts  6.21 us (4%)
  matrix products  2.84 us (2%)
    ppermute x30, waiting for transfers between devices, swapped(): lax.ppermute(shard, axis, [(i, i ^ mask) for i in range(lax.axis_size(axi...  86.9 us
    ppermute x30, starting transfers between devices, swapped(): lax.ppermute(shard, axis, [(i, i ^ mask) for i in range(lax.axis_size(axi...  42.5 us
    pallas_call x1, Pallas kernels, on_device(): pl.pallas_call(functools.partial(along_kernel, order, update_scale), out_...  10.9 us
    pallas_call x1, Pallas kernels, on_device(): pl.pallas_call(factor_kernel, out_shape=[shaped(jnp.bfloat16, hidden_widt...  7.75 us
    convert_element_type x2, other arithmetic, on_device(): (grad_part + momentum_decay * accumulated).astype(jnp.bfloat16)  7.1 us
    pallas_call x1, Pallas kernels, on_device(): pl.pallas_call(functools.partial(finish_kernel, far, group_size, update_s...  4.05 us
  transfers between devices with their start and end apart: 30, of which 12 were waited for; matrix products, arithmetic and copies ran while one was open for 6% of the time, Pallas kernels for 13%

profile of v2, /device:TPU:0, one launch (start us, length us, event | category | flops | bytes accessed | tf_op | source)
XLA Modules:
  0.0 174.9 jit_solution(3812185286662874820)
XLA Ops:
  2.0 3.1 %collective-permute-start = (bf16[1,32,2176]{2,1,0:T(8,128)(2,1)S(1)}, bf16[1,32,2176]{2,1,0:T(8,128)(2,1)S(1)}, u32[]{:S(2)}, u32[]{:S(2)}) collective-permute-start(bf16[1,32,2176]{2,1,0:T(8,128)(2,1)S(1)} %bitcast.83), channel_id=1, source_target_pairs={{0,16},{8,24},{16,0},{24,8},{1,17},{9,25},{17,1},{25,9},{2,18},{10... | collective-permute-start | bytes 417800 | tf_op jit(solution)/shard_map/ppermute | solution.py:30
  6.3 2.5 %collective-permute-done = bf16[1,32,2176]{2,1,0:T(8,128)(2,1)S(1)} collective-permute-done((bf16[1,32,2176]{2,1,0:T(8,128)(2,1)S(1)}, bf16[1,32,2176]{2,1,0:T(8,128)(2,1)S(1)}, u32[]{:S(2)}, u32[]{:S(2)}) %collective-permute-start) | collective-permute-done | bytes 139296 | tf_op jit(solution)/shard_map/ppermute | solution.py:30
  10.6 2.5 %collective-permute-start.2 = (bf16[2,32,2176]{2,1,0:T(8,128)(2,1)S(1)}, bf16[2,32,2176]{2,1,0:T(8,128)(2,1)S(1)}, u32[]{:S(2)}, u32[]{:S(2)}) collective-permute-start(bf16[2,32,2176]{2,1,0:T(8,128)(2,1)S(1)} %pad_maximum_fusion), channel_id=1, source_target_pairs={{0,6},{1,7},{2,4},{3,5},{4,2},{5,3},{6,0},{7,1},{8,14},{9,15},{10,... | collective-permute-start | bytes 835592 | tf_op jit(solution)/shard_map/ppermute | solution.py:30
  14.6 10.1 %collective-permute-done.2 = bf16[2,32,2176]{2,1,0:T(8,128)(2,1)S(1)} collective-permute-done((bf16[2,32,2176]{2,1,0:T(8,128)(2,1)S(1)}, bf16[2,32,2176]{2,1,0:T(8,128)(2,1)S(1)}, u32[]{:S(2)}, u32[]{:S(2)}) %collective-permute-start.2) | collective-permute-done | bytes 278560 | tf_op jit(solution)/shard_map/ppermute | solution.py:30
  27.4 4.0 %collective-permute-done.3 = bf16[2,32,2176]{2,1,0:T(8,128)(2,1)S(1)} collective-permute-done((bf16[2,32,2176]{2,1,0:T(8,128)(2,1)S(1)}, bf16[2,32,2176]{2,1,0:T(8,128)(2,1)S(1)}, u32[]{:S(2)}, u32[]{:S(2)}) %collective-permute-start.3) | collective-permute-done | bytes 278560 | tf_op jit(solution)/shard_map/ppermute | solution.py:30
  32.9 7.4 %collective-permute-done.5 = bf16[2,32,2176]{2,1,0:T(8,128)(2,1)S(1)} collective-permute-done((bf16[2,32,2176]{2,1,0:T(8,128)(2,1)S(1)}, bf16[2,32,2176]{2,1,0:T(8,128)(2,1)S(1)}, u32[]{:S(2)}, u32[]{:S(2)}) %collective-permute-start.5) | collective-permute-done | bytes 278560 | tf_op jit(solution)/shard_map/ppermute | solution.py:30
  40.3 2.9 %collective-permute-done.7 = bf16[2,32,2176]{2,1,0:T(8,128)(2,1)S(1)} collective-permute-done((bf16[2,32,2176]{2,1,0:T(8,128)(2,1)S(1)}, bf16[2,32,2176]{2,1,0:T(8,128)(2,1)S(1)}, u32[]{:S(2)}, u32[]{:S(2)}) %collective-permute-start.7) | collective-permute-done | bytes 278560 | tf_op jit(solution)/shard_map/ppermute | solution.py:30
  44.7 2.8 %convolution_convert_fusion.own_ref = bf16[512,2048]{1,0:T(8,128)(2,1)S(1)} fusion(bf16[512,2176]{1,0:T(8,128)(2,1)} %bitcast.103, s32[512]{0:T(512)S(1)} %add_select_fusion), kind=kOutput, calls=%fused_computation | convolution fusion | flops 1075052544 | bytes 4196352 | tf_op jit(solution)/shard_map/dot_general | solution.py:26
  47.6 3.7 %fusion.4 = (bf16[512,768]{1,0:T(8,128)(2,1)}, bf16[512,768]{1,0:T(8,128)(2,1)}) fusion(bf16[4,512,768]{2,1,0:T(8,128)(2,1)} %bitcast.78, s32[]{:T(128)S(6)} %select_n.159, bf16[4,512,768]{2,1,0:T(8,128)(2,1)} %bitcast.80, s32[]{:T(128)S(6)} %select_n.158), kind=kLoop, calls=%fused_computation.13 | loop fusion | flops 5505024 | bytes 4718600 | tf_op jit(solution)/shard_map/convert_element_type | solution.py:218
  51.3 3.4 %fusion.8 = (bf16[512,768]{1,0:T(8,128)(2,1)}, bf16[512,768]{1,0:T(8,128)(2,1)S(1)}) fusion(bf16[4,512,768]{2,1,0:T(8,128)(2,1)} %bitcast.79, s32[]{:T(128)S(6)} %select_n.161, bf16[4,512,768]{2,1,0:T(8,128)(2,1)} %bitcast.81, s32[]{:T(128)S(6)} %select_n.160), kind=kLoop, calls=%fused_computation.17 | loop fusion | flops 5505024 | bytes 4718600 | tf_op jit(solution)/shard_map/convert_element_type | solution.py:218
  60.9 14.2 %collective-permute-done.10.refs_2_.refs_3_ = bf16[512,768]{1,0:T(8,128)(2,1)} collective-permute-done((bf16[512,768]{1,0:T(8,128)(2,1)}, bf16[512,768]{1,0:T(8,128)(2,1)}, u32[]{:S(2)}, u32[]{:S(2)}) %collective-permute-start.10) | collective-permute-done | bytes 786464 | tf_op jit(solution)/shard_map/ppermute | solution.py:30
  76.5 3.4 %gram.1.gram_ref = f32[768,768]{1,0:T(8,128)S(1)} custom-call(bf16[512,768]{1,0:T(8,128)(2,1)S(1)} %get-tuple-element.54.refs_0_, bf16[512,768]{1,0:T(8,128)(2,1)} %collective-permute-done.9.refs_1_, bf16[512,768]{1,0:T(8,128)(2,1)} %collective-permute-done.10.refs_2_.refs_3_), custom_call_target="tpu_custom_call" | custom-call | flops 3221225472 | bytes 4194304 | tf_op jit(solution)/shard_map/gram/pallas_call | solution.py:246
  79.9 12.5 %collective-permute-done.11.refs_0_.refs_2_ = bf16[512,768]{1,0:T(8,128)(2,1)} collective-permute-done((bf16[512,768]{1,0:T(8,128)(2,1)}, bf16[512,768]{1,0:T(8,128)(2,1)}, u32[]{:S(2)}, u32[]{:S(2)}) %collective-permute-start.11) | collective-permute-done | bytes 786464 | tf_op jit(solution)/shard_map/ppermute | solution.py:30
  92.4 7.7 %factor.1 = (bf16[768,768]{1,0:T(8,128)(2,1)S(1)}, f32[1]{0:T(128)}) custom-call(f32[768,768]{1,0:T(8,128)S(1)} %gram.1.gram_ref, bf16[512,768]{1,0:T(8,128)(2,1)} %collective-permute-done.11.refs_0_.refs_2_), custom_call_target="tpu_custom_call" | custom-call | flops 6442450944 | bytes 4194304 | tf_op jit(solution)/shard_map/factor/pallas_call | solution.py:255
  100.2 10.9 %along.1 = (f32[2,2,512,384]{3,2,1,0:T(8,128)S(1)}, bf16[2,512,384]{2,1,0:T(8,128)(2,1)S(1)}) custom-call(s32[2]{0:T(128)S(1)} %pad_add_fusion.at_ref, f32[1]{0:T(128)} %get-tuple-element.33.inverse_ref, bf16[768,768]{1,0:T(8,128)(2,1)S(1)} %get-tuple-element.34.factor_ref, bf16[512,2048]{1,0:T(8,128)(2,1)S(1)} %convolution_convert_fusion.own_ref, ...), custom_call_target="tpu_custom_call" | custom-call | flops 6442450944 | bytes 12582912 | tf_op jit(solution)/shard_map/along/pallas_call | solution.py:270
  111.2 14.4 %collective-permute-done.15.refs_1_ = bf16[2,512,384]{2,1,0:T(8,128)(2,1)S(1)} collective-permute-done((bf16[2,512,384]{2,1,0:T(8,128)(2,1)S(1)}, bf16[2,512,384]{2,1,0:T(8,128)(2,1)S(1)}, u32[]{:S(2)}, u32[]{:S(2)}) %collective-permute-start.15) | collective-permute-done | bytes 786464 | tf_op jit(solution)/shard_map/ppermute | solution.py:30
  125.6 4.1 %finish.1 = (bf16[2,64,384]{2,1,0:T(8,128)(2,1)S(1)}, bf16[2,64,384]{2,1,0:T(8,128)(2,1)S(1)}, bf16[2,64,384]{2,1,0:T(8,128)(2,1)S(1)}, bf16[2,64,384]{2,1,0:T(8...) custom-call(s32[2]{0:T(128)S(1)} %pad_add_fusion.at_ref, ...), custom_call_target="tpu_custom_call" | custom-call | flops 3221225472 | bytes 10485760 | tf_op jit(solution)/shard_map/finish/pallas_call | solution.py:292
  138.4 2.4 %collective-permute-start.22 = (bf16[2,64,384]{2,1,0:T(8,128)(2,1)S(1)}, bf16[2,64,384]{2,1,0:T(8,128)(2,1)S(1)}, u32[]{:S(2)}, u32[]{:S(2)}) collective-permute-start(bf16[2,64,384]{2,1,0:T(8,128)(2,1)S(1)} %get-tuple-element.44), channel_id=1, source_target_pairs={{0,7},{1,6},{2,5},{3,4},{4,3},{5,2},{6,1},{7,0},{8,15},{9,14},{10,... | collective-permute-start | bytes 294920 | tf_op jit(solution)/shard_map/ppermute | solution.py:30
  140.9 7.0 %collective-permute-done.19.refs_4_ = bf16[2,64,384]{2,1,0:T(8,128)(2,1)S(1)} collective-permute-done((bf16[2,64,384]{2,1,0:T(8,128)(2,1)S(1)}, bf16[2,64,384]{2,1,0:T(8,128)(2,1)S(1)}, u32[]{:S(2)}, u32[]{:S(2)}) %collective-permute-start.19) | collective-permute-done | bytes 98336 | tf_op jit(solution)/shard_map/ppermute | solution.py:30
  147.8 3.1 %collective-permute-done.20.refs_5_ = bf16[2,64,384]{2,1,0:T(8,128)(2,1)S(1)} collective-permute-done((bf16[2,64,384]{2,1,0:T(8,128)(2,1)S(1)}, bf16[2,64,384]{2,1,0:T(8,128)(2,1)S(1)}, u32[]{:S(2)}, u32[]{:S(2)}) %collective-permute-start.20) | collective-permute-done | bytes 98336 | tf_op jit(solution)/shard_map/ppermute | solution.py:30
  152.2 4.1 %collective-permute-start.24 = (bf16[2,64,384]{2,1,0:T(8,128)(2,1)S(1)}, bf16[2,64,384]{2,1,0:T(8,128)(2,1)S(1)}, u32[]{:S(2)}, u32[]{:S(2)}) collective-permute-start(bf16[2,64,384]{2,1,0:T(8,128)(2,1)S(1)} %get-tuple-element.47), channel_id=1, source_target_pairs={{0,2},{1,3},{2,0},{3,1},{4,6},{5,7},{6,4},{7,5},{8,10},{9,11},{10,... | collective-permute-start | bytes 294920 | tf_op jit(solution)/shard_map/ppermute | solution.py:30
  162.2 2.6 %collective-permute-start.29 = (bf16[2,64,384]{2,1,0:T(8,128)(2,1)S(1)}, bf16[2,64,384]{2,1,0:T(8,128)(2,1)S(1)}, u32[]{:S(2)}, u32[]{:S(2)}) collective-permute-start(bf16[2,64,384]{2,1,0:T(8,128)(2,1)S(1)} %get-tuple-element.52), channel_id=1, source_target_pairs={{0,7},{1,6},{2,5},{3,4},{4,3},{5,2},{6,1},{7,0},{8,15},{9,14},{10,... | collective-permute-start | bytes 294920 | tf_op jit(solution)/shard_map/ppermute | solution.py:30
  164.9 6.1 %collective-permute-done.26 = bf16[2,64,384]{2,1,0:T(8,128)(2,1)S(1)} collective-permute-done((bf16[2,64,384]{2,1,0:T(8,128)(2,1)S(1)}, bf16[2,64,384]{2,1,0:T(8,128)(2,1)S(1)}, u32[]{:S(2)}, u32[]{:S(2)}) %collective-permute-start.26) | collective-permute-done | bytes 98336 | tf_op jit(solution)/shard_map/ppermute | solution.py:30
  171.1 2.7 %collective-permute-done.27 = bf16[2,64,384]{2,1,0:T(8,128)(2,1)S(1)} collective-permute-done((bf16[2,64,384]{2,1,0:T(8,128)(2,1)S(1)}, bf16[2,64,384]{2,1,0:T(8,128)(2,1)S(1)}, u32[]{:S(2)}, u32[]{:S(2)}) %collective-permute-start.27) | collective-permute-done | bytes 98336 | tf_op jit(solution)/shard_map/ppermute | solution.py:30
  (107 shorter events, 37.0 us)
Async XLA Ops:
  8.8 18.0 %collective-permute-start.1 = (bf16[2,32,2176]{2,1,0:T(8,128)(2,1)S(1)}, bf16[2,32,2176]{2,1,0:T(8,128)(2,1)S(1)}, u32[]{:S(2)}, u32[]{:S(2)}) collective-permute-start(bf16[2,32,2176]{2,1,0:T(8,128)(2,1)S(1)} %pad_maximum_fusion), channel_id=1, source_target_pairs={{0,2},{1,3},{2,0},{3,1},{4,6},{5,7},{6,4},{7,5},{8,10},{9,11},{10,... | collective-permute-start | bytes 835592 | tf_op jit(solution)/shard_map/ppermute | solution.py:30
  10.6 14.1 %collective-permute-start.2 = (bf16[2,32,2176]{2,1,0:T(8,128)(2,1)S(1)}, bf16[2,32,2176]{2,1,0:T(8,128)(2,1)S(1)}, u32[]{:S(2)}, u32[]{:S(2)}) collective-permute-start(bf16[2,32,2176]{2,1,0:T(8,128)(2,1)S(1)} %pad_maximum_fusion), channel_id=1, source_target_pairs={{0,6},{1,7},{2,4},{3,5},{4,2},{5,3},{6,0},{7,1},{8,14},{9,15},{10,... | collective-permute-start | bytes 835592 | tf_op jit(solution)/shard_map/ppermute | solution.py:30
  13.1 19.7 %collective-permute-start.4 = (bf16[2,32,2176]{2,1,0:T(8,128)(2,1)S(1)}, bf16[2,32,2176]{2,1,0:T(8,128)(2,1)S(1)}, u32[]{:S(2)}, u32[]{:S(2)}) collective-permute-start(bf16[2,32,2176]{2,1,0:T(8,128)(2,1)S(1)} %pad_maximum_fusion), channel_id=1, source_target_pairs={{0,1},{1,0},{2,3},{3,2},{4,5},{5,4},{6,7},{7,6},{8,9},{9,8},{10,11... | collective-permute-start | bytes 835592 | tf_op jit(solution)/shard_map/ppermute | solution.py:30
  25.3 15.0 %collective-permute-start.6 = (bf16[2,32,2176]{2,1,0:T(8,128)(2,1)S(1)}, bf16[2,32,2176]{2,1,0:T(8,128)(2,1)S(1)}, u32[]{:S(2)}, u32[]{:S(2)}) collective-permute-start(bf16[2,32,2176]{2,1,0:T(8,128)(2,1)S(1)} %collective-permute-done.2), channel_id=1, source_target_pairs={{0,1},{1,0},{2,3},{3,2},{4,5},{5,4},{6,7},{7,6},{8,9},{9,8},{10,11... | collective-permute-start | bytes 835592 | tf_op jit(solution)/shard_map/ppermute | solution.py:30
  26.8 13.5 %collective-permute-start.5 = (bf16[2,32,2176]{2,1,0:T(8,128)(2,1)S(1)}, bf16[2,32,2176]{2,1,0:T(8,128)(2,1)S(1)}, u32[]{:S(2)}, u32[]{:S(2)}) collective-permute-start(bf16[2,32,2176]{2,1,0:T(8,128)(2,1)S(1)} %collective-permute-done.1), channel_id=1, source_target_pairs={{0,1},{1,0},{2,3},{3,2},{4,5},{5,4},{6,7},{7,6},{8,9},{9,8},{10,11... | collective-permute-start | bytes 835592 | tf_op jit(solution)/shard_map/ppermute | solution.py:30
  31.3 11.9 %collective-permute-start.7 = (bf16[2,32,2176]{2,1,0:T(8,128)(2,1)S(1)}, bf16[2,32,2176]{2,1,0:T(8,128)(2,1)S(1)}, u32[]{:S(2)}, u32[]{:S(2)}) collective-permute-start(bf16[2,32,2176]{2,1,0:T(8,128)(2,1)S(1)} %collective-permute-done.3), channel_id=1, source_target_pairs={{0,1},{1,0},{2,3},{3,2},{4,5},{5,4},{6,7},{7,6},{8,9},{9,8},{10,11... | collective-permute-start | bytes 835592 | tf_op jit(solution)/shard_map/ppermute | solution.py:30
  47.5 52.7 %collective-permute-start.8 = (bf16[512,2048]{1,0:T(8,128)(2,1)S(1)}, bf16[512,2048]{1,0:T(8,128)(2,1)}, u32[]{:S(2)}, u32[]{:S(2)}) collective-permute-start(bf16[512,2048]{1,0:T(8,128)(2,1)S(1)} %convolution_convert_fusion.own_ref), channel_id=1, source_target_pairs={{0,8},{8,0},{16,24},{24,16},{1,9},{9,1},{17,25},{25,17},{2,10},{10... | collective-permute-start | bytes 6291464 | tf_op jit(solution)/shard_map/ppermute | solution.py:30
  55.2 19.9 %collective-permute-start.10 = (bf16[512,768]{1,0:T(8,128)(2,1)}, bf16[512,768]{1,0:T(8,128)(2,1)}, u32[]{:S(2)}, u32[]{:S(2)}) collective-permute-start(bf16[512,768]{1,0:T(8,128)(2,1)} %get-tuple-element.31), channel_id=1, source_target_pairs={{0,24},{8,16},{16,8},{24,0},{1,25},{9,17},{17,9},{25,1},{2,26},{10... | collective-permute-start | bytes 2359304 | tf_op jit(solution)/shard_map/ppermute | solution.py:30
  56.4 36.1 %collective-permute-start.11 = (bf16[512,768]{1,0:T(8,128)(2,1)}, bf16[512,768]{1,0:T(8,128)(2,1)}, u32[]{:S(2)}, u32[]{:S(2)}) collective-permute-start(bf16[512,768]{1,0:T(8,128)(2,1)} %get-tuple-element.32), channel_id=1, source_target_pairs={{0,16},{8,24},{16,0},{24,8},{1,17},{9,25},{17,1},{25,9},{2,18},{10... | collective-permute-start | bytes 2359304 | tf_op jit(solution)/shard_map/ppermute | solution.py:30
  59.0 41.1 %collective-permute-start.12 = (bf16[2,512,384]{2,1,0:T(8,128)(2,1)S(1)}, bf16[2,512,384]{2,1,0:T(8,128)(2,1)S(1)}, u32[]{:S(2)}, u32[]{:S(2)}) collective-permute-start(bf16[2,512,384]{2,1,0:T(8,128)(2,1)S(1)} %get-tuple-element.59), channel_id=1, source_target_pairs={{0,8},{8,0},{16,24},{24,16},{1,9},{9,1},{17,25},{25,17},{2,10},{10... | collective-permute-start | bytes 2359304 | tf_op jit(solution)/shard_map/ppermute | solution.py:30
  59.4 51.8 %collective-permute-start.14 = (bf16[2,512,384]{2,1,0:T(8,128)(2,1)S(1)}, bf16[2,512,384]{2,1,0:T(8,128)(2,1)S(1)}, u32[]{:S(2)}, u32[]{:S(2)}) collective-permute-start(bf16[2,512,384]{2,1,0:T(8,128)(2,1)S(1)} %get-tuple-element.58), channel_id=1, source_target_pairs={{0,16},{8,24},{16,0},{24,8},{1,17},{9,25},{17,1},{25,9},{2,18},{10... | collective-permute-start | bytes 2359304 | tf_op jit(solution)/shard_map/ppermute | solution.py:30
  75.1 50.5 %collective-permute-start.15 = (bf16[2,512,384]{2,1,0:T(8,128)(2,1)S(1)}, bf16[2,512,384]{2,1,0:T(8,128)(2,1)S(1)}, u32[]{:S(2)}, u32[]{:S(2)}) collective-permute-start(bf16[2,512,384]{2,1,0:T(8,128)(2,1)S(1)} %get-tuple-element.57), channel_id=1, source_target_pairs={{0,24},{8,16},{16,8},{24,0},{1,25},{9,17},{17,9},{25,1},{2,26},{10... | collective-permute-start | bytes 2359304 | tf_op jit(solution)/shard_map/ppermute | solution.py:30
  111.1 14.5 %collective-permute-start.13 = (bf16[2,512,384]{2,1,0:T(8,128)(2,1)S(1)}, bf16[2,512,384]{2,1,0:T(8,128)(2,1)S(1)}, u32[]{:S(2)}, u32[]{:S(2)}) collective-permute-start(bf16[2,512,384]{2,1,0:T(8,128)(2,1)S(1)} %get-tuple-element.36), channel_id=1, source_target_pairs={{0,8},{8,0},{16,24},{24,16},{1,9},{9,1},{17,25},{25,17},{2,10},{10... | collective-permute-start | bytes 2359304 | tf_op jit(solution)/shard_map/ppermute | solution.py:30
  133.2 14.6 %collective-permute-start.19 = (bf16[2,64,384]{2,1,0:T(8,128)(2,1)S(1)}, bf16[2,64,384]{2,1,0:T(8,128)(2,1)S(1)}, u32[]{:S(2)}, u32[]{:S(2)}) collective-permute-start(bf16[2,64,384]{2,1,0:T(8,128)(2,1)S(1)} %get-tuple-element.41), channel_id=1, source_target_pairs={{0,4},{1,5},{2,6},{3,7},{4,0},{5,1},{6,2},{7,3},{8,12},{9,13},{10,... | collective-permute-start | bytes 294920 | tf_op jit(solution)/shard_map/ppermute | solution.py:30
  134.8 16.1 %collective-permute-start.20 = (bf16[2,64,384]{2,1,0:T(8,128)(2,1)S(1)}, bf16[2,64,384]{2,1,0:T(8,128)(2,1)S(1)}, u32[]{:S(2)}, u32[]{:S(2)}) collective-permute-start(bf16[2,64,384]{2,1,0:T(8,128)(2,1)S(1)} %get-tuple-element.42), channel_id=1, source_target_pairs={{0,5},{1,4},{2,7},{3,6},{4,1},{5,0},{6,3},{7,2},{8,13},{9,12},{10,... | collective-permute-start | bytes 294920 | tf_op jit(solution)/shard_map/ppermute | solution.py:30
  137.1 13.9 %collective-permute-start.21 = (bf16[2,64,384]{2,1,0:T(8,128)(2,1)S(1)}, bf16[2,64,384]{2,1,0:T(8,128)(2,1)S(1)}, u32[]{:S(2)}, u32[]{:S(2)}) collective-permute-start(bf16[2,64,384]{2,1,0:T(8,128)(2,1)S(1)} %get-tuple-element.43), channel_id=1, source_target_pairs={{0,6},{1,7},{2,4},{3,5},{4,2},{5,3},{6,0},{7,1},{8,14},{9,15},{10,... | collective-permute-start | bytes 294920 | tf_op jit(solution)/shard_map/ppermute | solution.py:30
  138.4 12.6 %collective-permute-start.22 = (bf16[2,64,384]{2,1,0:T(8,128)(2,1)S(1)}, bf16[2,64,384]{2,1,0:T(8,128)(2,1)S(1)}, u32[]{:S(2)}, u32[]{:S(2)}) collective-permute-start(bf16[2,64,384]{2,1,0:T(8,128)(2,1)S(1)} %get-tuple-element.44), channel_id=1, source_target_pairs={{0,7},{1,6},{2,5},{3,4},{4,3},{5,2},{6,1},{7,0},{8,15},{9,14},{10,... | collective-permute-start | bytes 294920 | tf_op jit(solution)/shard_map/ppermute | solution.py:30
  151.7 8.5 %collective-permute-start.23 = (bf16[2,64,384]{2,1,0:T(8,128)(2,1)S(1)}, bf16[2,64,384]{2,1,0:T(8,128)(2,1)S(1)}, u32[]{:S(2)}, u32[]{:S(2)}) collective-permute-start(bf16[2,64,384]{2,1,0:T(8,128)(2,1)S(1)} %get-tuple-element.46), channel_id=1, source_target_pairs={{0,1},{1,0},{2,3},{3,2},{4,5},{5,4},{6,7},{7,6},{8,9},{9,8},{10,11... | collective-permute-start | bytes 294920 | tf_op jit(solution)/shard_map/ppermute | solution.py:30
  152.2 10.0 %collective-permute-start.24 = (bf16[2,64,384]{2,1,0:T(8,128)(2,1)S(1)}, bf16[2,64,384]{2,1,0:T(8,128)(2,1)S(1)}, u32[]{:S(2)}, u32[]{:S(2)}) collective-permute-start(bf16[2,64,384]{2,1,0:T(8,128)(2,1)S(1)} %get-tuple-element.47), channel_id=1, source_target_pairs={{0,2},{1,3},{2,0},{3,1},{4,6},{5,7},{6,4},{7,5},{8,10},{9,11},{10,... | collective-permute-start | bytes 294920 | tf_op jit(solution)/shard_map/ppermute | solution.py:30
  156.3 8.5 %collective-permute-start.25 = (bf16[2,64,384]{2,1,0:T(8,128)(2,1)S(1)}, bf16[2,64,384]{2,1,0:T(8,128)(2,1)S(1)}, u32[]{:S(2)}, u32[]{:S(2)}) collective-permute-start(bf16[2,64,384]{2,1,0:T(8,128)(2,1)S(1)} %get-tuple-element.48), channel_id=1, source_target_pairs={{0,3},{1,2},{2,1},{3,0},{4,7},{5,6},{6,5},{7,4},{8,11},{9,10},{10,... | collective-permute-start | bytes 294920 | tf_op jit(solution)/shard_map/ppermute | solution.py:30
  156.8 14.2 %collective-permute-start.26 = (bf16[2,64,384]{2,1,0:T(8,128)(2,1)S(1)}, bf16[2,64,384]{2,1,0:T(8,128)(2,1)S(1)}, u32[]{:S(2)}, u32[]{:S(2)}) collective-permute-start(bf16[2,64,384]{2,1,0:T(8,128)(2,1)S(1)} %get-tuple-element.49), channel_id=1, source_target_pairs={{0,4},{1,5},{2,6},{3,7},{4,0},{5,1},{6,2},{7,3},{8,12},{9,13},{10,... | collective-permute-start | bytes 294920 | tf_op jit(solution)/shard_map/ppermute | solution.py:30
  159.1 14.7 %collective-permute-start.27 = (bf16[2,64,384]{2,1,0:T(8,128)(2,1)S(1)}, bf16[2,64,384]{2,1,0:T(8,128)(2,1)S(1)}, u32[]{:S(2)}, u32[]{:S(2)}) collective-permute-start(bf16[2,64,384]{2,1,0:T(8,128)(2,1)S(1)} %get-tuple-element.50), channel_id=1, source_target_pairs={{0,5},{1,4},{2,7},{3,6},{4,1},{5,0},{6,3},{7,2},{8,13},{9,12},{10,... | collective-permute-start | bytes 294920 | tf_op jit(solution)/shard_map/ppermute | solution.py:30
  160.3 13.6 %collective-permute-start.28 = (bf16[2,64,384]{2,1,0:T(8,128)(2,1)S(1)}, bf16[2,64,384]{2,1,0:T(8,128)(2,1)S(1)}, u32[]{:S(2)}, u32[]{:S(2)}) collective-permute-start(bf16[2,64,384]{2,1,0:T(8,128)(2,1)S(1)} %get-tuple-element.51), channel_id=1, source_target_pairs={{0,6},{1,7},{2,4},{3,5},{4,2},{5,3},{6,0},{7,1},{8,14},{9,15},{10,... | collective-permute-start | bytes 294920 | tf_op jit(solution)/shard_map/ppermute | solution.py:30
  162.2 11.8 %collective-permute-start.29 = (bf16[2,64,384]{2,1,0:T(8,128)(2,1)S(1)}, bf16[2,64,384]{2,1,0:T(8,128)(2,1)S(1)}, u32[]{:S(2)}, u32[]{:S(2)}) collective-permute-start(bf16[2,64,384]{2,1,0:T(8,128)(2,1)S(1)} %get-tuple-element.52), channel_id=1, source_target_pairs={{0,7},{1,6},{2,5},{3,4},{4,3},{5,2},{6,1},{7,0},{8,15},{9,14},{10,... | collective-permute-start | bytes 294920 | tf_op jit(solution)/shard_map/ppermute | solution.py:30
  (9 other events, 68.2 us)

commit v3 on v2

--- a/solution.py
+++ b/solution.py
@@ -112,7 +112,7 @@
     return rows_ref[:, columns_of(at_ref[0] ^ place, depth)]
 
 
-def along_kernel(order, scale, at_ref, inverse_ref, factor_ref, own_ref, other_ref, *refs):
+def along_kernel(order, sooner, scale, at_ref, inverse_ref, factor_ref, own_ref, other_ref, *refs):
     count = len(order)
     update_refs, weight_refs, (base_ref, sent_ref) = refs[:count], refs[count:-2], refs[-2:]
     width = sent_ref.shape[2]
@@ -131,7 +131,7 @@
         for kind in range(2):
             product = sum(
                 dot(rows_at(at_ref, place, rows_ref, depth), weight[kind])
-                for place, weight in zip(order, weight_refs)
+                for place, weight in zip(sooner, weight_refs)
             )
             base_ref[kind, side] = product - jnp.where(own_kind == kind, kept, 0.0)
 
@@ -186,6 +186,7 @@
     near = [0, 1]
     far = list(range(2, fsdp_size))
     order = near + far
+    sooner, latest = near + far[:0:-1], far[:1]
 
     slot_lanes = -(-experts // 128) * 128
     slots = slots_of(routes, experts).astype(jnp.bfloat16)
@@ -268,12 +269,12 @@
     kind = f % 2
     half_shape = (2, half_rows, half_width)
     base, sent = pl.pallas_call(
-        functools.partial(along_kernel, order, update_scale),
+        functools.partial(along_kernel, order, sooner, update_scale),
         out_shape=[
             shaped(jnp.float32, 2, *half_shape),
             shaped(jnp.bfloat16, *half_shape),
         ],
-        in_specs=[SMEM, SMEM] + [VMEM] * (3 + len(order) + len(near)),
+        in_specs=[SMEM, SMEM] + [VMEM] * (3 + len(order) + len(sooner)),
         out_specs=[VMEM, VMEM],
         cost_estimate=cost(2 * flops, 12 << 20),
         compiler_params=limit(10),
@@ -285,20 +286,20 @@
         own_rows,
         other_rows,
         *[update[m] for m in order],
-        *[held_weight[m] for m in near],
+        *[held_weight[m] for m in sooner],
     )
     partner = swapped(sent, "fsdp", 1)
     chunk = half_rows // group_size
     pieces = pl.pallas_call(
-        functools.partial(finish_kernel, far, group_size, update_scale),
+        functools.partial(finish_kernel, latest, group_size, update_scale),
         out_shape=[shaped(jnp.bfloat16, 2, chunk, half_width)] * group_size,
-        in_specs=[SMEM] + [VMEM] * (4 + len(far)),
+        in_specs=[SMEM] + [VMEM] * (4 + len(latest)),
         out_specs=[VMEM] * group_size,
         scratch_shapes=[bf16_scratch(*half_shape)],
         cost_estimate=cost(flops, 10 << 20),
         compiler_params=limit(8),
         name="finish",
-    )(at, own_rows, other_rows, base, partner, *[held_weight[m] for m in far])
+    )(at, own_rows, other_rows, base, partner, *[held_weight[m] for m in latest])
 
     spread = [swapped(pieces[m], "expert", m) if m else pieces[m] for m in range(group_size)]
     part_shape = spread[0].shape

time: 176 us -> 175 us (level)
  transfers between devices with their start and end apart: 30 -> 30, of which waited for: 12 -> 13; matrix products, arithmetic and copies ran while one was open for 6% -> 6% of each run, Pallas kernels for 13% -> 13%
where the time goes in v3:
time: 175 us; the launch traced here: 174 us
  waiting for transfers between devices  85.6 us (49%)
  starting transfers between devices  42.6 us (24%)
  Pallas kernels  27.1 us (15%)
  other arithmetic  9.29 us (5%)
  local copies, waits for them, and re-layouts  6.21 us (4%)
  matrix products  2.84 us (2%)
    ppermute x30, waiting for transfers between devices, swapped(): lax.ppermute(shard, axis, [(i, i ^ mask) for i in range(lax.axis_size(axi...  85.6 us
    ppermute x30, starting transfers between devices, swapped(): lax.ppermute(shard, axis, [(i, i ^ mask) for i in range(lax.axis_size(axi...  42.6 us
    pallas_call x1, Pallas kernels, on_device(): pl.pallas_call(functools.partial(along_kernel, order, sooner, update_scal...  12.1 us
    pallas_call x1, Pallas kernels, on_device(): pl.pallas_call(factor_kernel, out_shape=[shaped(jnp.bfloat16, hidden_widt...  7.75 us
    convert_element_type x2, other arithmetic, on_device(): (grad_part + momentum_decay * accumulated).astype(jnp.bfloat16)  7.1 us
  transfers between devices with their start and end apart: 30, of which 13 were waited for; matrix products, arithmetic and copies ran while one was open for 6% of the time, Pallas kernels for 13%

profile of v3, /device:TPU:0, one launch (start us, length us, event | category | flops | bytes accessed | tf_op | source)
XLA Modules:
  0.0 174.0 jit_solution(2784327902072936398)
XLA Ops:
  2.0 3.1 %collective-permute-start = (bf16[1,32,2176]{2,1,0:T(8,128)(2,1)S(1)}, bf16[1,32,2176]{2,1,0:T(8,128)(2,1)S(1)}, u32[]{:S(2)}, u32[]{:S(2)}) collective-permute-start(bf16[1,32,2176]{2,1,0:T(8,128)(2,1)S(1)} %bitcast.83), channel_id=1, source_target_pairs={{0,16},{8,24},{16,0},{24,8},{1,17},{9,25},{17,1},{25,9},{2,18},{10... | collective-permute-start | bytes 417800 | tf_op jit(solution)/shard_map/ppermute | solution.py:30
  10.6 2.5 %collective-permute-start.2 = (bf16[2,32,2176]{2,1,0:T(8,128)(2,1)S(1)}, bf16[2,32,2176]{2,1,0:T(8,128)(2,1)S(1)}, u32[]{:S(2)}, u32[]{:S(2)}) collective-permute-start(bf16[2,32,2176]{2,1,0:T(8,128)(2,1)S(1)} %pad_maximum_fusion), channel_id=1, source_target_pairs={{0,6},{1,7},{2,4},{3,5},{4,2},{5,3},{6,0},{7,1},{8,14},{9,15},{10,... | collective-permute-start | bytes 835592 | tf_op jit(solution)/shard_map/ppermute | solution.py:30
  14.6 10.1 %collective-permute-done.2 = bf16[2,32,2176]{2,1,0:T(8,128)(2,1)S(1)} collective-permute-done((bf16[2,32,2176]{2,1,0:T(8,128)(2,1)S(1)}, bf16[2,32,2176]{2,1,0:T(8,128)(2,1)S(1)}, u32[]{:S(2)}, u32[]{:S(2)}) %collective-permute-start.2) | collective-permute-done | bytes 278560 | tf_op jit(solution)/shard_map/ppermute | solution.py:30
  27.4 4.0 %collective-permute-done.3 = bf16[2,32,2176]{2,1,0:T(8,128)(2,1)S(1)} collective-permute-done((bf16[2,32,2176]{2,1,0:T(8,128)(2,1)S(1)}, bf16[2,32,2176]{2,1,0:T(8,128)(2,1)S(1)}, u32[]{:S(2)}, u32[]{:S(2)}) %collective-permute-start.3) | collective-permute-done | bytes 278560 | tf_op jit(solution)/shard_map/ppermute | solution.py:30
  32.9 7.4 %collective-permute-done.5 = bf16[2,32,2176]{2,1,0:T(8,128)(2,1)S(1)} collective-permute-done((bf16[2,32,2176]{2,1,0:T(8,128)(2,1)S(1)}, bf16[2,32,2176]{2,1,0:T(8,128)(2,1)S(1)}, u32[]{:S(2)}, u32[]{:S(2)}) %collective-permute-start.5) | collective-permute-done | bytes 278560 | tf_op jit(solution)/shard_map/ppermute | solution.py:30
  40.3 2.9 %collective-permute-done.7 = bf16[2,32,2176]{2,1,0:T(8,128)(2,1)S(1)} collective-permute-done((bf16[2,32,2176]{2,1,0:T(8,128)(2,1)S(1)}, bf16[2,32,2176]{2,1,0:T(8,128)(2,1)S(1)}, u32[]{:S(2)}, u32[]{:S(2)}) %collective-permute-start.7) | collective-permute-done | bytes 278560 | tf_op jit(solution)/shard_map/ppermute | solution.py:30
  44.7 2.8 %convolution_convert_fusion.own_ref = bf16[512,2048]{1,0:T(8,128)(2,1)S(1)} fusion(bf16[512,2176]{1,0:T(8,128)(2,1)} %bitcast.103, s32[512]{0:T(512)S(1)} %add_select_fusion), kind=kOutput, calls=%fused_computation | convolution fusion | flops 1075052544 | bytes 4196352 | tf_op jit(solution)/shard_map/dot_general | solution.py:26
  47.6 3.7 %fusion.4 = (bf16[512,768]{1,0:T(8,128)(2,1)}, bf16[512,768]{1,0:T(8,128)(2,1)}) fusion(bf16[4,512,768]{2,1,0:T(8,128)(2,1)} %bitcast.78, s32[]{:T(128)S(6)} %select_n.159, bf16[4,512,768]{2,1,0:T(8,128)(2,1)} %bitcast.80, s32[]{:T(128)S(6)} %select_n.158), kind=kLoop, calls=%fused_computation.13 | loop fusion | flops 5505024 | bytes 4718600 | tf_op jit(solution)/shard_map/convert_element_type | solution.py:219
  51.3 3.4 %fusion.8 = (bf16[512,768]{1,0:T(8,128)(2,1)}, bf16[512,768]{1,0:T(8,128)(2,1)S(1)}) fusion(bf16[4,512,768]{2,1,0:T(8,128)(2,1)} %bitcast.79, s32[]{:T(128)S(6)} %select_n.161, bf16[4,512,768]{2,1,0:T(8,128)(2,1)} %bitcast.81, s32[]{:T(128)S(6)} %select_n.160), kind=kLoop, calls=%fused_computation.17 | loop fusion | flops 5505024 | bytes 4718600 | tf_op jit(solution)/shard_map/convert_element_type | solution.py:219
  60.8 14.3 %collective-permute-done.10.refs_2_.refs_3_ = bf16[512,768]{1,0:T(8,128)(2,1)} collective-permute-done((bf16[512,768]{1,0:T(8,128)(2,1)}, bf16[512,768]{1,0:T(8,128)(2,1)}, u32[]{:S(2)}, u32[]{:S(2)}) %collective-permute-start.10) | collective-permute-done | bytes 786464 | tf_op jit(solution)/shard_map/ppermute | solution.py:30
  76.6 3.4 %gram.1.gram_ref = f32[768,768]{1,0:T(8,128)S(1)} custom-call(bf16[512,768]{1,0:T(8,128)(2,1)S(1)} %get-tuple-element.54.refs_0_, bf16[512,768]{1,0:T(8,128)(2,1)} %collective-permute-done.9.refs_1_, bf16[512,768]{1,0:T(8,128)(2,1)} %collective-permute-done.10.refs_2_.refs_3_), custom_call_target="tpu_custom_call" | custom-call | flops 3221225472 | bytes 4194304 | tf_op jit(solution)/shard_map/gram/pallas_call | solution.py:247
  80.1 12.4 %collective-permute-done.11.refs_0_.refs_2_ = bf16[512,768]{1,0:T(8,128)(2,1)} collective-permute-done((bf16[512,768]{1,0:T(8,128)(2,1)}, bf16[512,768]{1,0:T(8,128)(2,1)}, u32[]{:S(2)}, u32[]{:S(2)}) %collective-permute-start.11) | collective-permute-done | bytes 786464 | tf_op jit(solution)/shard_map/ppermute | solution.py:30
  92.4 7.7 %factor.1 = (bf16[768,768]{1,0:T(8,128)(2,1)S(1)}, f32[1]{0:T(128)}) custom-call(f32[768,768]{1,0:T(8,128)S(1)} %gram.1.gram_ref, bf16[512,768]{1,0:T(8,128)(2,1)} %collective-permute-done.11.refs_0_.refs_2_), custom_call_target="tpu_custom_call" | custom-call | flops 6442450944 | bytes 4194304 | tf_op jit(solution)/shard_map/factor/pallas_call | solution.py:256
  100.2 8.5 %collective-permute-done.13.refs_6_ = bf16[2,512,384]{2,1,0:T(8,128)(2,1)S(1)} collective-permute-done((bf16[2,512,384]{2,1,0:T(8,128)(2,1)S(1)}, bf16[2,512,384]{2,1,0:T(8,128)(2,1)S(1)}, u32[]{:S(2)}, u32[]{:S(2)}) %collective-permute-start.13) | collective-permute-done | bytes 786464 | tf_op jit(solution)/shard_map/ppermute | solution.py:30
  108.7 12.1 %along.1 = (f32[2,2,512,384]{3,2,1,0:T(8,128)S(1)}, bf16[2,512,384]{2,1,0:T(8,128)(2,1)S(1)}) custom-call(s32[2]{0:T(128)S(1)} %pad_add_fusion.at_ref, f32[1]{0:T(128)} %get-tuple-element.33.inverse_ref, bf16[768,768]{1,0:T(8,128)(2,1)S(1)} %get-tuple-element.34.factor_ref, bf16[512,2048]{1,0:T(8,128)(2,1)S(1)} %convolution_convert_fusion.own_ref, ...), custom_call_target="tpu_custom_call" | custom-call | flops 6442450944 | bytes 12582912 | tf_op jit(solution)/shard_map/along/pallas_call | solution.py:271
  121.1 4.7 %collective-permute-done.15.refs_0_ = bf16[2,512,384]{2,1,0:T(8,128)(2,1)S(1)} collective-permute-done((bf16[2,512,384]{2,1,0:T(8,128)(2,1)S(1)}, bf16[2,512,384]{2,1,0:T(8,128)(2,1)S(1)}, u32[]{:S(2)}, u32[]{:S(2)}) %collective-permute-start.15) | collective-permute-done | bytes 786464 | tf_op jit(solution)/shard_map/ppermute | solution.py:30
  125.8 3.2 %finish.1 = (bf16[2,64,384]{2,1,0:T(8,128)(2,1)S(1)}, bf16[2,64,384]{2,1,0:T(8,128)(2,1)S(1)}, bf16[2,64,384]{2,1,0:T(8,128)(2,1)S(1)}, bf16[2,64,384]{2,1,0:T(8...) custom-call(s32[2]{0:T(128)S(1)} %pad_add_fusion.at_ref, ...), custom_call_target="tpu_custom_call" | custom-call | flops 3221225472 | bytes 10485760 | tf_op jit(solution)/shard_map/finish/pallas_call | solution.py:293
  140.2 7.0 %collective-permute-done.19.refs_4_ = bf16[2,64,384]{2,1,0:T(8,128)(2,1)S(1)} collective-permute-done((bf16[2,64,384]{2,1,0:T(8,128)(2,1)S(1)}, bf16[2,64,384]{2,1,0:T(8,128)(2,1)S(1)}, u32[]{:S(2)}, u32[]{:S(2)}) %collective-permute-start.19) | collective-permute-done | bytes 98336 | tf_op jit(solution)/shard_map/ppermute | solution.py:30
  147.2 3.0 %collective-permute-done.20.refs_5_ = bf16[2,64,384]{2,1,0:T(8,128)(2,1)S(1)} collective-permute-done((bf16[2,64,384]{2,1,0:T(8,128)(2,1)S(1)}, bf16[2,64,384]{2,1,0:T(8,128)(2,1)S(1)}, u32[]{:S(2)}, u32[]{:S(2)}) %collective-permute-start.20) | collective-permute-done | bytes 98336 | tf_op jit(solution)/shard_map/ppermute | solution.py:30
  151.6 3.9 %collective-permute-start.24 = (bf16[2,64,384]{2,1,0:T(8,128)(2,1)S(1)}, bf16[2,64,384]{2,1,0:T(8,128)(2,1)S(1)}, u32[]{:S(2)}, u32[]{:S(2)}) collective-permute-start(bf16[2,64,384]{2,1,0:T(8,128)(2,1)S(1)} %get-tuple-element.47), channel_id=1, source_target_pairs={{0,2},{1,3},{2,0},{3,1},{4,6},{5,7},{6,4},{7,5},{8,10},{9,11},{10,... | collective-permute-start | bytes 294920 | tf_op jit(solution)/shard_map/ppermute | solution.py:30
  155.9 2.5 %collective-permute-start.26 = (bf16[2,64,384]{2,1,0:T(8,128)(2,1)S(1)}, bf16[2,64,384]{2,1,0:T(8,128)(2,1)S(1)}, u32[]{:S(2)}, u32[]{:S(2)}) collective-permute-start(bf16[2,64,384]{2,1,0:T(8,128)(2,1)S(1)} %get-tuple-element.49), channel_id=1, source_target_pairs={{0,4},{1,5},{2,6},{3,7},{4,0},{5,1},{6,2},{7,3},{8,12},{9,13},{10,... | collective-permute-start | bytes 294920 | tf_op jit(solution)/shard_map/ppermute | solution.py:30
  161.2 2.7 %collective-permute-start.29 = (bf16[2,64,384]{2,1,0:T(8,128)(2,1)S(1)}, bf16[2,64,384]{2,1,0:T(8,128)(2,1)S(1)}, u32[]{:S(2)}, u32[]{:S(2)}) collective-permute-start(bf16[2,64,384]{2,1,0:T(8,128)(2,1)S(1)} %get-tuple-element.52), channel_id=1, source_target_pairs={{0,7},{1,6},{2,5},{3,4},{4,3},{5,2},{6,1},{7,0},{8,15},{9,14},{10,... | collective-permute-start | bytes 294920 | tf_op jit(solution)/shard_map/ppermute | solution.py:30
  164.1 6.0 %collective-permute-done.26 = bf16[2,64,384]{2,1,0:T(8,128)(2,1)S(1)} collective-permute-done((bf16[2,64,384]{2,1,0:T(8,128)(2,1)S(1)}, bf16[2,64,384]{2,1,0:T(8,128)(2,1)S(1)}, u32[]{:S(2)}, u32[]{:S(2)}) %collective-permute-start.26) | collective-permute-done | bytes 98336 | tf_op jit(solution)/shard_map/ppermute | solution.py:30
  170.1 2.8 %collective-permute-done.27 = bf16[2,64,384]{2,1,0:T(8,128)(2,1)S(1)} collective-permute-done((bf16[2,64,384]{2,1,0:T(8,128)(2,1)S(1)}, bf16[2,64,384]{2,1,0:T(8,128)(2,1)S(1)}, u32[]{:S(2)}, u32[]{:S(2)}) %collective-permute-start.27) | collective-permute-done | bytes 98336 | tf_op jit(solution)/shard_map/ppermute | solution.py:30
  (107 shorter events, 39.6 us)
Async XLA Ops:
  8.8 18.0 %collective-permute-start.1 = (bf16[2,32,2176]{2,1,0:T(8,128)(2,1)S(1)}, bf16[2,32,2176]{2,1,0:T(8,128)(2,1)S(1)}, u32[]{:S(2)}, u32[]{:S(2)}) collective-permute-start(bf16[2,32,2176]{2,1,0:T(8,128)(2,1)S(1)} %pad_maximum_fusion), channel_id=1, source_target_pairs={{0,2},{1,3},{2,0},{3,1},{4,6},{5,7},{6,4},{7,5},{8,10},{9,11},{10,... | collective-permute-start | bytes 835592 | tf_op jit(solution)/shard_map/ppermute | solution.py:30
  10.6 14.1 %collective-permute-start.2 = (bf16[2,32,2176]{2,1,0:T(8,128)(2,1)S(1)}, bf16[2,32,2176]{2,1,0:T(8,128)(2,1)S(1)}, u32[]{:S(2)}, u32[]{:S(2)}) collective-permute-start(bf16[2,32,2176]{2,1,0:T(8,128)(2,1)S(1)} %pad_maximum_fusion), channel_id=1, source_target_pairs={{0,6},{1,7},{2,4},{3,5},{4,2},{5,3},{6,0},{7,1},{8,14},{9,15},{10,... | collective-permute-start | bytes 835592 | tf_op jit(solution)/shard_map/ppermute | solution.py:30
  13.1 19.7 %collective-permute-start.4 = (bf16[2,32,2176]{2,1,0:T(8,128)(2,1)S(1)}, bf16[2,32,2176]{2,1,0:T(8,128)(2,1)S(1)}, u32[]{:S(2)}, u32[]{:S(2)}) collective-permute-start(bf16[2,32,2176]{2,1,0:T(8,128)(2,1)S(1)} %pad_maximum_fusion), channel_id=1, source_target_pairs={{0,1},{1,0},{2,3},{3,2},{4,5},{5,4},{6,7},{7,6},{8,9},{9,8},{10,11... | collective-permute-start | bytes 835592 | tf_op jit(solution)/shard_map/ppermute | solution.py:30
  25.3 15.0 %collective-permute-start.6 = (bf16[2,32,2176]{2,1,0:T(8,128)(2,1)S(1)}, bf16[2,32,2176]{2,1,0:T(8,128)(2,1)S(1)}, u32[]{:S(2)}, u32[]{:S(2)}) collective-permute-start(bf16[2,32,2176]{2,1,0:T(8,128)(2,1)S(1)} %collective-permute-done.2), channel_id=1, source_target_pairs={{0,1},{1,0},{2,3},{3,2},{4,5},{5,4},{6,7},{7,6},{8,9},{9,8},{10,11... | collective-permute-start | bytes 835592 | tf_op jit(solution)/shard_map/ppermute | solution.py:30
  26.8 13.5 %collective-permute-start.5 = (bf16[2,32,2176]{2,1,0:T(8,128)(2,1)S(1)}, bf16[2,32,2176]{2,1,0:T(8,128)(2,1)S(1)}, u32[]{:S(2)}, u32[]{:S(2)}) collective-permute-start(bf16[2,32,2176]{2,1,0:T(8,128)(2,1)S(1)} %collective-permute-done.1), channel_id=1, source_target_pairs={{0,1},{1,0},{2,3},{3,2},{4,5},{5,4},{6,7},{7,6},{8,9},{9,8},{10,11... | collective-permute-start | bytes 835592 | tf_op jit(solution)/shard_map/ppermute | solution.py:30
  31.3 11.9 %collective-permute-start.7 = (bf16[2,32,2176]{2,1,0:T(8,128)(2,1)S(1)}, bf16[2,32,2176]{2,1,0:T(8,128)(2,1)S(1)}, u32[]{:S(2)}, u32[]{:S(2)}) collective-permute-start(bf16[2,32,2176]{2,1,0:T(8,128)(2,1)S(1)} %collective-permute-done.3), channel_id=1, source_target_pairs={{0,1},{1,0},{2,3},{3,2},{4,5},{5,4},{6,7},{7,6},{8,9},{9,8},{10,11... | collective-permute-start | bytes 835592 | tf_op jit(solution)/shard_map/ppermute | solution.py:30
  47.5 61.2 %collective-permute-start.8 = (bf16[512,2048]{1,0:T(8,128)(2,1)S(1)}, bf16[512,2048]{1,0:T(8,128)(2,1)}, u32[]{:S(2)}, u32[]{:S(2)}) collective-permute-start(bf16[512,2048]{1,0:T(8,128)(2,1)S(1)} %convolution_convert_fusion.own_ref), channel_id=1, source_target_pairs={{0,8},{8,0},{16,24},{24,16},{1,9},{9,1},{17,25},{25,17},{2,10},{10... | collective-permute-start | bytes 6291464 | tf_op jit(solution)/shard_map/ppermute | solution.py:30
  55.2 19.9 %collective-permute-start.10 = (bf16[512,768]{1,0:T(8,128)(2,1)}, bf16[512,768]{1,0:T(8,128)(2,1)}, u32[]{:S(2)}, u32[]{:S(2)}) collective-permute-start(bf16[512,768]{1,0:T(8,128)(2,1)} %get-tuple-element.31), channel_id=1, source_target_pairs={{0,24},{8,16},{16,8},{24,0},{1,25},{9,17},{17,9},{25,1},{2,26},{10... | collective-permute-start | bytes 2359304 | tf_op jit(solution)/shard_map/ppermute | solution.py:30
  56.4 36.1 %collective-permute-start.11 = (bf16[512,768]{1,0:T(8,128)(2,1)}, bf16[512,768]{1,0:T(8,128)(2,1)}, u32[]{:S(2)}, u32[]{:S(2)}) collective-permute-start(bf16[512,768]{1,0:T(8,128)(2,1)} %get-tuple-element.32), channel_id=1, source_target_pairs={{0,16},{8,24},{16,0},{24,8},{1,17},{9,25},{17,1},{25,9},{2,18},{10... | collective-permute-start | bytes 2359304 | tf_op jit(solution)/shard_map/ppermute | solution.py:30
  59.0 41.1 %collective-permute-start.12 = (bf16[2,512,384]{2,1,0:T(8,128)(2,1)S(1)}, bf16[2,512,384]{2,1,0:T(8,128)(2,1)S(1)}, u32[]{:S(2)}, u32[]{:S(2)}) collective-permute-start(bf16[2,512,384]{2,1,0:T(8,128)(2,1)S(1)} %get-tuple-element.59), channel_id=1, source_target_pairs={{0,8},{8,0},{16,24},{24,16},{1,9},{9,1},{17,25},{25,17},{2,10},{10... | collective-permute-start | bytes 2359304 | tf_op jit(solution)/shard_map/ppermute | solution.py:30
  59.4 49.3 %collective-permute-start.13 = (bf16[2,512,384]{2,1,0:T(8,128)(2,1)S(1)}, bf16[2,512,384]{2,1,0:T(8,128)(2,1)S(1)}, u32[]{:S(2)}, u32[]{:S(2)}) collective-permute-start(bf16[2,512,384]{2,1,0:T(8,128)(2,1)S(1)} %get-tuple-element.58), channel_id=1, source_target_pairs={{0,24},{8,16},{16,8},{24,0},{1,25},{9,17},{17,9},{25,1},{2,26},{10... | collective-permute-start | bytes 2359304 | tf_op jit(solution)/shard_map/ppermute | solution.py:30
  75.1 50.7 %collective-permute-start.15 = (bf16[2,512,384]{2,1,0:T(8,128)(2,1)S(1)}, bf16[2,512,384]{2,1,0:T(8,128)(2,1)S(1)}, u32[]{:S(2)}, u32[]{:S(2)}) collective-permute-start(bf16[2,512,384]{2,1,0:T(8,128)(2,1)S(1)} %get-tuple-element.57), channel_id=1, source_target_pairs={{0,16},{8,24},{16,0},{24,8},{1,17},{9,25},{17,1},{25,9},{2,18},{10... | collective-permute-start | bytes 2359304 | tf_op jit(solution)/shard_map/ppermute | solution.py:30
  132.3 7.9 %collective-permute-start.18 = (bf16[2,64,384]{2,1,0:T(8,128)(2,1)S(1)}, bf16[2,64,384]{2,1,0:T(8,128)(2,1)S(1)}, u32[]{:S(2)}, u32[]{:S(2)}) collective-permute-start(bf16[2,64,384]{2,1,0:T(8,128)(2,1)S(1)} %get-tuple-element.40), channel_id=1, source_target_pairs={{0,3},{1,2},{2,1},{3,0},{4,7},{5,6},{6,5},{7,4},{8,11},{9,10},{10,... | collective-permute-start | bytes 294920 | tf_op jit(solution)/shard_map/ppermute | solution.py:30
  132.5 14.7 %collective-permute-start.19 = (bf16[2,64,384]{2,1,0:T(8,128)(2,1)S(1)}, bf16[2,64,384]{2,1,0:T(8,128)(2,1)S(1)}, u32[]{:S(2)}, u32[]{:S(2)}) collective-permute-start(bf16[2,64,384]{2,1,0:T(8,128)(2,1)S(1)} %get-tuple-element.41), channel_id=1, source_target_pairs={{0,4},{1,5},{2,6},{3,7},{4,0},{5,1},{6,2},{7,3},{8,12},{9,13},{10,... | collective-permute-start | bytes 294920 | tf_op jit(solution)/shard_map/ppermute | solution.py:30
  134.2 16.0 %collective-permute-start.20 = (bf16[2,64,384]{2,1,0:T(8,128)(2,1)S(1)}, bf16[2,64,384]{2,1,0:T(8,128)(2,1)S(1)}, u32[]{:S(2)}, u32[]{:S(2)}) collective-permute-start(bf16[2,64,384]{2,1,0:T(8,128)(2,1)S(1)} %get-tuple-element.42), channel_id=1, source_target_pairs={{0,5},{1,4},{2,7},{3,6},{4,1},{5,0},{6,3},{7,2},{8,13},{9,12},{10,... | collective-permute-start | bytes 294920 | tf_op jit(solution)/shard_map/ppermute | solution.py:30
  136.4 13.8 %collective-permute-start.21 = (bf16[2,64,384]{2,1,0:T(8,128)(2,1)S(1)}, bf16[2,64,384]{2,1,0:T(8,128)(2,1)S(1)}, u32[]{:S(2)}, u32[]{:S(2)}) collective-permute-start(bf16[2,64,384]{2,1,0:T(8,128)(2,1)S(1)} %get-tuple-element.43), channel_id=1, source_target_pairs={{0,6},{1,7},{2,4},{3,5},{4,2},{5,3},{6,0},{7,1},{8,14},{9,15},{10,... | collective-permute-start | bytes 294920 | tf_op jit(solution)/shard_map/ppermute | solution.py:30
  137.7 12.5 %collective-permute-start.22 = (bf16[2,64,384]{2,1,0:T(8,128)(2,1)S(1)}, bf16[2,64,384]{2,1,0:T(8,128)(2,1)S(1)}, u32[]{:S(2)}, u32[]{:S(2)}) collective-permute-start(bf16[2,64,384]{2,1,0:T(8,128)(2,1)S(1)} %get-tuple-element.44), channel_id=1, source_target_pairs={{0,7},{1,6},{2,5},{3,4},{4,3},{5,2},{6,1},{7,0},{8,15},{9,14},{10,... | collective-permute-start | bytes 294920 | tf_op jit(solution)/shard_map/ppermute | solution.py:30
  151.0 8.5 %collective-permute-start.23 = (bf16[2,64,384]{2,1,0:T(8,128)(2,1)S(1)}, bf16[2,64,384]{2,1,0:T(8,128)(2,1)S(1)}, u32[]{:S(2)}, u32[]{:S(2)}) collective-permute-start(bf16[2,64,384]{2,1,0:T(8,128)(2,1)S(1)} %get-tuple-element.46), channel_id=1, source_target_pairs={{0,1},{1,0},{2,3},{3,2},{4,5},{5,4},{6,7},{7,6},{8,9},{9,8},{10,11... | collective-permute-start | bytes 294920 | tf_op jit(solution)/shard_map/ppermute | solution.py:30
  151.6 9.6 %collective-permute-start.24 = (bf16[2,64,384]{2,1,0:T(8,128)(2,1)S(1)}, bf16[2,64,384]{2,1,0:T(8,128)(2,1)S(1)}, u32[]{:S(2)}, u32[]{:S(2)}) collective-permute-start(bf16[2,64,384]{2,1,0:T(8,128)(2,1)S(1)} %get-tuple-element.47), channel_id=1, source_target_pairs={{0,2},{1,3},{2,0},{3,1},{4,6},{5,7},{6,4},{7,5},{8,10},{9,11},{10,... | collective-permute-start | bytes 294920 | tf_op jit(solution)/shard_map/ppermute | solution.py:30
  155.5 8.5 %collective-permute-start.25 = (bf16[2,64,384]{2,1,0:T(8,128)(2,1)S(1)}, bf16[2,64,384]{2,1,0:T(8,128)(2,1)S(1)}, u32[]{:S(2)}, u32[]{:S(2)}) collective-permute-start(bf16[2,64,384]{2,1,0:T(8,128)(2,1)S(1)} %get-tuple-element.48), channel_id=1, source_target_pairs={{0,3},{1,2},{2,1},{3,0},{4,7},{5,6},{6,5},{7,4},{8,11},{9,10},{10,... | collective-permute-start | bytes 294920 | tf_op jit(solution)/shard_map/ppermute | solution.py:30
  155.9 14.1 %collective-permute-start.26 = (bf16[2,64,384]{2,1,0:T(8,128)(2,1)S(1)}, bf16[2,64,384]{2,1,0:T(8,128)(2,1)S(1)}, u32[]{:S(2)}, u32[]{:S(2)}) collective-permute-start(bf16[2,64,384]{2,1,0:T(8,128)(2,1)S(1)} %get-tuple-element.49), channel_id=1, source_target_pairs={{0,4},{1,5},{2,6},{3,7},{4,0},{5,1},{6,2},{7,3},{8,12},{9,13},{10,... | collective-permute-start | bytes 294920 | tf_op jit(solution)/shard_map/ppermute | solution.py:30
  158.4 14.5 %collective-permute-start.27 = (bf16[2,64,384]{2,1,0:T(8,128)(2,1)S(1)}, bf16[2,64,384]{2,1,0:T(8,128)(2,1)S(1)}, u32[]{:S(2)}, u32[]{:S(2)}) collective-permute-start(bf16[2,64,384]{2,1,0:T(8,128)(2,1)S(1)} %get-tuple-element.50), channel_id=1, source_target_pairs={{0,5},{1,4},{2,7},{3,6},{4,1},{5,0},{6,3},{7,2},{8,13},{9,12},{10,... | collective-permute-start | bytes 294920 | tf_op jit(solution)/shard_map/ppermute | solution.py:30
  159.5 13.5 %collective-permute-start.28 = (bf16[2,64,384]{2,1,0:T(8,128)(2,1)S(1)}, bf16[2,64,384]{2,1,0:T(8,128)(2,1)S(1)}, u32[]{:S(2)}, u32[]{:S(2)}) collective-permute-start(bf16[2,64,384]{2,1,0:T(8,128)(2,1)S(1)} %get-tuple-element.51), channel_id=1, source_target_pairs={{0,6},{1,7},{2,4},{3,5},{4,2},{5,3},{6,0},{7,1},{8,14},{9,15},{10,... | collective-permute-start | bytes 294920 | tf_op jit(solution)/shard_map/ppermute | solution.py:30
  161.2 11.8 %collective-permute-start.29 = (bf16[2,64,384]{2,1,0:T(8,128)(2,1)S(1)}, bf16[2,64,384]{2,1,0:T(8,128)(2,1)S(1)}, u32[]{:S(2)}, u32[]{:S(2)}) collective-permute-start(bf16[2,64,384]{2,1,0:T(8,128)(2,1)S(1)} %get-tuple-element.52), channel_id=1, source_target_pairs={{0,7},{1,6},{2,5},{3,4},{4,3},{5,2},{6,1},{7,0},{8,15},{9,14},{10,... | collective-permute-start | bytes 294920 | tf_op jit(solution)/shard_map/ppermute | solution.py:30
  (9 other events, 64.3 us)

commit v4 on v3

--- a/solution.py
+++ b/solution.py
@@ -112,6 +112,11 @@
     return rows_ref[:, columns_of(at_ref[0] ^ place, depth)]
 
 
+def rows_from(at_ref, place, first, rows_ref, block, depth):
+    start = pl.multiple_of((at_ref[0] ^ place) * block + first, 128)
+    return rows_ref[:, pl.ds(start, depth)]
+
+
 def along_kernel(order, sooner, scale, at_ref, inverse_ref, factor_ref, own_ref, other_ref, *refs):
     count = len(order)
     update_refs, weight_refs, (base_ref, sent_ref) = refs[:count], refs[count:-2], refs[-2:]
@@ -130,31 +135,35 @@
         kept = scale * jnp.where(own_kind == 0, left, right)
         for kind in range(2):
             product = sum(
-                dot(rows_at(at_ref, place, rows_ref, depth), weight[kind])
+                dot(rows_from(at_ref, *place, rows_ref, depth, weight.shape[1]), weight[kind])
                 for place, weight in zip(sooner, weight_refs)
             )
             base_ref[kind, side] = product - jnp.where(own_kind == kind, kept, 0.0)
 
 
-def finish_kernel(order, group_size, scale, at_ref, own_ref, other_ref, base_ref, moved_ref, *refs):
-    count = len(order)
-    weight_refs, out_refs, hidden = refs[:count], refs[count:-1], refs[-1]
-    depth = weight_refs[0].shape[1]
+def most_kernel(place, scale, at_ref, own_ref, other_ref, base_ref, moved_ref, weight_ref, total_ref, rows_ref):
     own_kind = lax.rem(at_ref[0], 2)
-    for side, rows_ref in enumerate((own_ref, other_ref)):
+    depth, last = weight_ref.shape[1], rows_ref.shape[2]
+    for side, listed_ref in enumerate((own_ref, other_ref)):
+        rows_ref[side] = rows_from(at_ref, place, depth, listed_ref, depth + last, last)
+        rows = rows_from(at_ref, place, 0, listed_ref, depth + last, depth)
         moved = scale * moved_ref[side].astype(jnp.float32)
-        products = []
         for kind in range(2):
             total = base_ref[kind, side] - jnp.where(own_kind == kind, 0.0, moved)
-            for place, weight in zip(order, weight_refs):
-                total += dot(rows_at(at_ref, place, rows_ref, depth), weight[kind])
-            products.append(total)
-        gate, up = products
+            total_ref[kind, side] = total + dot(rows, weight_ref[kind])
+
+
+def finish_kernel(at_ref, rows_ref, total_ref, weight_ref, *refs):
+    out_refs, hidden = refs[:-1], refs[-1]
+    for side in range(2):
+        gate, up = (
+            total_ref[kind, side] + dot(rows_ref[side], weight_ref[kind]) for kind in range(2)
+        )
         hidden[side] = (gate / (1.0 + jnp.exp(-gate)) * up).astype(jnp.bfloat16)
-    chunk = hidden.shape[1] // group_size
-    for mask in range(group_size):
+    chunk = hidden.shape[1] // len(out_refs)
+    for mask, out_ref in enumerate(out_refs):
         start = pl.multiple_of((at_ref[1] ^ mask) * chunk, chunk)
-        out_refs[mask][...] = hidden[:, pl.ds(start, chunk), :]
+        out_ref[...] = hidden[:, pl.ds(start, chunk), :]
 
 
 def choose_kernel(at_ref, owners_ref, *refs):
@@ -186,12 +195,26 @@
     near = [0, 1]
     far = list(range(2, fsdp_size))
     order = near + far
-    sooner, latest = near + far[:0:-1], far[:1]
+    weight = weights.reshape(fsdp_size, local_rows, hidden_width)
+
+    def weight_part(weight, mask, first=0, depth=local_rows):
+        target = f ^ mask
+        return lax.dynamic_slice(
+            weight,
+            (target // 2 * 2, first, target % 2 * half_width),
+            (2, depth, half_width),
+        )
+
+    lead, lead_rows = far[-1], max(128, local_rows // 4)
+    early_part = weight_part(weight, lead, 0, lead_rows)
+    early_part = swapped(early_part, "fsdp", lead)
 
     slot_lanes = -(-experts // 128) * 128
     slots = slots_of(routes, experts).astype(jnp.bfloat16)
     slots = jnp.pad(slots, ((0, 0), (0, 0), (0, slot_lanes - experts)))
-    block = jnp.concatenate([tokens, slots], axis=2).reshape(2 * tok_dev, model_width + slot_lanes)
+    block = jnp.concatenate([tokens, slots], axis=2)
+    block = block.reshape(2 * tok_dev, model_width + slot_lanes)
+    block, weight = lax.optimization_barrier((block, weight))
     blocks, source_pair, source_group = gathered(block)
     all_rows = blocks.reshape(-1, model_width + slot_lanes)
     lane = lax.broadcasted_iota(jnp.int32, (1, slot_lanes), 1)
@@ -208,7 +231,6 @@
 
     moment = momentum.reshape(fsdp_size, local_rows, hidden_width)
     grad = gradient.reshape(fsdp_size, local_rows, hidden_width)
-    weight = weights.reshape(fsdp_size, local_rows, hidden_width)
     update, held_weight = [None] * fsdp_size, [None] * fsdp_size
     for places in (far, near):
         for mask in reversed(places):
@@ -225,17 +247,22 @@
                 update[mask] = part
     for mask in reversed(range(1, fsdp_size)):
         update[mask] = swapped(update[mask], "fsdp", mask)
-    for mask in reversed(range(fsdp_size)):
-        target = f ^ mask
-        part = lax.dynamic_slice(
-            weight,
-            (target // 2 * 2, 0, target % 2 * half_width),
-            (2, local_rows, half_width),
-        )
-        held_weight[mask] = swapped(part, "fsdp", mask) if mask else part
+    latest, body_rows = far[0], local_rows - lead_rows
+    held_weight[0] = weight_part(weight, 0)
+    for mask in reversed(range(1, fsdp_size)):
+        first = lead_rows if mask == lead else 0
+        depth = body_rows if mask in (lead, latest) else local_rows
+        part = weight_part(weight, mask, first, depth)
+        held_weight[mask] = swapped(part, "fsdp", mask)
+    part = weight_part(weight, latest, body_rows, lead_rows)
+    last_part = swapped(part, "fsdp", latest)
+    sooner = [((place, 0), held_weight[place]) for place in near + far[1:-1]]
+    sooner += [((lead, 0), early_part), ((lead, lead_rows), held_weight[lead])]
+    places, parts = zip(*sooner)
 
     full_rows = fsdp_size * local_rows
     update_scale = step_size * 0.2 * math.sqrt(max(full_rows, hidden_width))
+    depth = local_rows
     bf16_scratch = lambda *shape: pltpu.VMEM(shape, jnp.bfloat16)
     shaped = lambda kind, *shape: jax.ShapeDtypeStruct(shape, kind)
     flops = 2 * 2 * half_rows * full_rows * hidden_width
@@ -269,7 +296,7 @@
     kind = f % 2
     half_shape = (2, half_rows, half_width)
     base, sent = pl.pallas_call(
-        functools.partial(along_kernel, order, sooner, update_scale),
+        functools.partial(along_kernel, order, places, update_scale),
         out_shape=[
             shaped(jnp.float32, 2, *half_shape),
             shaped(jnp.bfloat16, *half_shape),
@@ -286,20 +313,32 @@
         own_rows,
         other_rows,
         *[update[m] for m in order],
-        *[held_weight[m] for m in sooner],
+        *parts,
     )
     partner = swapped(sent, "fsdp", 1)
     chunk = half_rows // group_size
+    total, rows_left = pl.pallas_call(
+        functools.partial(most_kernel, latest, update_scale),
+        out_shape=[
+            shaped(jnp.float32, 2, *half_shape),
+            shaped(jnp.bfloat16, 2, half_rows, lead_rows),
+        ],
+        in_specs=[SMEM] + [VMEM] * 5,
+        out_specs=[VMEM, VMEM],
+        cost_estimate=cost(flops // 4, 8 << 20),
+        compiler_params=limit(8),
+        name="most",
+    )(at, own_rows, other_rows, base, partner, held_weight[latest])
     pieces = pl.pallas_call(
-        functools.partial(finish_kernel, latest, group_size, update_scale),
+        finish_kernel,
         out_shape=[shaped(jnp.bfloat16, 2, chunk, half_width)] * group_size,
-        in_specs=[SMEM] + [VMEM] * (4 + len(latest)),
+        in_specs=[SMEM] + [VMEM] * 3,
         out_specs=[VMEM] * group_size,
         scratch_shapes=[bf16_scratch(*half_shape)],
-        cost_estimate=cost(flops, 10 << 20),
+        cost_estimate=cost(flops // 8, 4 << 20),
         compiler_params=limit(8),
         name="finish",
-    )(at, own_rows, other_rows, base, partner, *[held_weight[m] for m in latest])
+    )(at, rows_left, total, last_part)
 
     spread = [swapped(pieces[m], "expert", m) if m else pieces[m] for m in range(group_size)]
     part_shape = spread[0].shape

time: 175 us -> 188 us (1.074)
  waiting for transfers between devices: 85.6 us -> 91.8 us
  local copies, waits for them, and re-layouts: 6.21 us -> 10.1 us
    ppermute x30 -> x32, waiting for transfers between devices: 85.6 us -> 91.8 us  [swapped(): lax.ppermute(shard, axis, [(i, i ^ mask) for i in range(lax.axis_size(axi...]
    dynamic_slice x1 -> x4, local copies, waits for them, and re-layouts: 2.17 us -> 6.07 us  [weight_part(): lax.dynamic_slice(weight, (target // 2 * 2, first, target % 2 * half_widt...]
    ppermute x30 -> x32, starting transfers between devices: 42.6 us -> 44.3 us  [swapped(): lax.ppermute(shard, axis, [(i, i ^ mask) for i in range(lax.axis_size(axi...]
    pallas_call x2 -> x3, Pallas kernels: 15.2 us -> 16.7 us  [the longest x1 12.3 us: on_device(): pl.pallas_call(functools.partial(along_kernel, order, places, update_scal...]
  transfers between devices with their start and end apart: 30 -> 32, of which waited for: 13 -> 14; matrix products, arithmetic and copies ran while one was open for 6% -> 8% of each run, Pallas kernels for 13% -> 7%
where the time goes in v4:
time: 188 us; the launch traced here: 187 us
  waiting for transfers between devices  91.8 us (49%)
  starting transfers between devices  44.3 us (24%)
  Pallas kernels  28.5 us (15%)
  local copies, waits for them, and re-layouts  10.1 us (5%)
  other arithmetic  9.32 us (5%)
  matrix products  2.84 us (2%)
    ppermute x32, waiting for transfers between devices, swapped(): lax.ppermute(shard, axis, [(i, i ^ mask) for i in range(lax.axis_size(axi...  91.8 us
    ppermute x32, starting transfers between devices, swapped(): lax.ppermute(shard, axis, [(i, i ^ mask) for i in range(lax.axis_size(axi...  44.3 us
    pallas_call x1, Pallas kernels, on_device(): pl.pallas_call(functools.partial(along_kernel, order, places, update_scal...  12.3 us
    pallas_call x1, Pallas kernels, on_device(): pl.pallas_call(factor_kernel, out_shape=[shaped(jnp.bfloat16, hidden_widt...  7.74 us
    convert_element_type x2, other arithmetic, on_device(): (grad_part + momentum_decay * accumulated).astype(jnp.bfloat16)  7.14 us
    dynamic_slice x4, local copies, waits for them, and re-layouts, weight_part(): lax.dynamic_slice(weight, (target // 2 * 2, first, target % 2 * half_widt...  6.07 us
  transfers between devices with their start and end apart: 32, of which 14 were waited for; matrix products, arithmetic and copies ran while one was open for 8% of the time, Pallas kernels for 7%

profile of v4, /device:TPU:0, one launch (start us, length us, event | category | flops | bytes accessed | tf_op | source)
XLA Modules:
  0.0 187.2 jit_solution(14585021721999058119)
XLA Ops:
  2.0 3.1 %collective-permute-start = (bf16[1,32,2176]{2,1,0:T(8,128)(2,1)S(1)}, bf16[1,32,2176]{2,1,0:T(8,128)(2,1)S(1)}, u32[]{:S(2)}, u32[]{:S(2)}) collective-permute-start(bf16[1,32,2176]{2,1,0:T(8,128)(2,1)S(1)} %bitcast.86), channel_id=1, source_target_pairs={{0,16},{8,24},{16,0},{24,8},{1,17},{9,25},{17,1},{25,9},{2,18},{10... | collective-permute-start | bytes 417800 | tf_op jit(solution)/shard_map/ppermute | solution.py:30
  14.6 10.1 %collective-permute-done.2 = bf16[2,32,2176]{2,1,0:T(8,128)(2,1)S(1)} collective-permute-done((bf16[2,32,2176]{2,1,0:T(8,128)(2,1)S(1)}, bf16[2,32,2176]{2,1,0:T(8,128)(2,1)S(1)}, u32[]{:S(2)}, u32[]{:S(2)}) %collective-permute-start.2) | collective-permute-done | bytes 278560 | tf_op jit(solution)/shard_map/ppermute | solution.py:30
  27.4 4.0 %collective-permute-done.3 = bf16[2,32,2176]{2,1,0:T(8,128)(2,1)S(1)} collective-permute-done((bf16[2,32,2176]{2,1,0:T(8,128)(2,1)S(1)}, bf16[2,32,2176]{2,1,0:T(8,128)(2,1)S(1)}, u32[]{:S(2)}, u32[]{:S(2)}) %collective-permute-start.3) | collective-permute-done | bytes 278560 | tf_op jit(solution)/shard_map/ppermute | solution.py:30
  32.9 7.4 %collective-permute-done.5 = bf16[2,32,2176]{2,1,0:T(8,128)(2,1)S(1)} collective-permute-done((bf16[2,32,2176]{2,1,0:T(8,128)(2,1)S(1)}, bf16[2,32,2176]{2,1,0:T(8,128)(2,1)S(1)}, u32[]{:S(2)}, u32[]{:S(2)}) %collective-permute-start.5) | collective-permute-done | bytes 278560 | tf_op jit(solution)/shard_map/ppermute | solution.py:30
  40.3 2.9 %collective-permute-done.7 = bf16[2,32,2176]{2,1,0:T(8,128)(2,1)S(1)} collective-permute-done((bf16[2,32,2176]{2,1,0:T(8,128)(2,1)S(1)}, bf16[2,32,2176]{2,1,0:T(8,128)(2,1)S(1)}, u32[]{:S(2)}, u32[]{:S(2)}) %collective-permute-start.7) | collective-permute-done | bytes 278560 | tf_op jit(solution)/shard_map/ppermute | solution.py:30
  44.7 2.8 %convolution_convert_fusion.own_ref = bf16[512,2048]{1,0:T(8,128)(2,1)S(1)} fusion(bf16[512,2176]{1,0:T(8,128)(2,1)} %bitcast.106, s32[512]{0:T(512)S(1)} %add_select_fusion), kind=kOutput, calls=%fused_computation | convolution fusion | flops 1075052544 | bytes 4196352 | tf_op jit(solution)/shard_map/dot_general | solution.py:26
  47.6 3.7 %fusion.4 = (bf16[512,768]{1,0:T(8,128)(2,1)}, bf16[512,768]{1,0:T(8,128)(2,1)}) fusion(bf16[4,512,768]{2,1,0:T(8,128)(2,1)} %bitcast.78, s32[]{:T(128)S(6)} %select_n.169, bf16[4,512,768]{2,1,0:T(8,128)(2,1)} %bitcast.80, s32[]{:T(128)S(6)} %select_n.168), kind=kLoop, calls=%fused_computation.13 | loop fusion | flops 5505024 | bytes 4718600 | tf_op jit(solution)/shard_map/convert_element_type | solution.py:241
  51.3 3.4 %fusion.8 = (bf16[512,768]{1,0:T(8,128)(2,1)}, bf16[512,768]{1,0:T(8,128)(2,1)S(1)}) fusion(bf16[4,512,768]{2,1,0:T(8,128)(2,1)} %bitcast.79, s32[]{:T(128)S(6)} %select_n.171, bf16[4,512,768]{2,1,0:T(8,128)(2,1)} %bitcast.81, s32[]{:T(128)S(6)} %select_n.170), kind=kLoop, calls=%fused_computation.17 | loop fusion | flops 5505024 | bytes 4718600 | tf_op jit(solution)/shard_map/convert_element_type | solution.py:241
  56.9 2.8 %constant_dynamic-slice_fusion.2 = (bf16[2,512,384]{2,1,0:T(8,128)(2,1)}, bf16[2,512,384]{2,1,0:T(8,128)(2,1)}) fusion(bf16[4,512,768]{2,1,0:T(8,128)(2,1)} %bitcast.82, s32[]{:T(128)S(6)} %select_n.176, s32[]{:T(128)S(6)} %select_n.178, s32[]{:T(128)S(6)} %select_n.172, s32[]{:T(128)S(6)} %select_n.174), kind=kLoop, calls=%fused_computation.57 | loop fusion | bytes 3145744 | tf_op jit(solution)/shard_map/dynamic_slice | solution.py:202
  63.8 11.3 %collective-permute-done.10.refs_2_.refs_3_ = bf16[512,768]{1,0:T(8,128)(2,1)} collective-permute-done((bf16[512,768]{1,0:T(8,128)(2,1)}, bf16[512,768]{1,0:T(8,128)(2,1)}, u32[]{:S(2)}, u32[]{:S(2)}) %collective-permute-start.10) | collective-permute-done | bytes 786464 | tf_op jit(solution)/shard_map/ppermute | solution.py:30
  76.5 3.4 %gram.1.gram_ref = f32[768,768]{1,0:T(8,128)S(1)} custom-call(bf16[512,768]{1,0:T(8,128)(2,1)S(1)} %get-tuple-element.62.refs_0_, bf16[512,768]{1,0:T(8,128)(2,1)} %collective-permute-done.9.refs_1_, bf16[512,768]{1,0:T(8,128)(2,1)} %collective-permute-done.10.refs_2_.refs_3_), custom_call_target="tpu_custom_call" | custom-call | flops 3221225472 | bytes 4194304 | tf_op jit(solution)/shard_map/gram/pallas_call | solution.py:274
  80.0 12.5 %collective-permute-done.11.refs_0_.refs_2_ = bf16[512,768]{1,0:T(8,128)(2,1)} collective-permute-done((bf16[512,768]{1,0:T(8,128)(2,1)}, bf16[512,768]{1,0:T(8,128)(2,1)}, u32[]{:S(2)}, u32[]{:S(2)}) %collective-permute-start.11) | collective-permute-done | bytes 786464 | tf_op jit(solution)/shard_map/ppermute | solution.py:30
  92.5 7.7 %factor.1 = (bf16[768,768]{1,0:T(8,128)(2,1)S(1)}, f32[1]{0:T(128)}) custom-call(f32[768,768]{1,0:T(8,128)S(1)} %gram.1.gram_ref, bf16[512,768]{1,0:T(8,128)(2,1)} %collective-permute-done.11.refs_0_.refs_2_), custom_call_target="tpu_custom_call" | custom-call | flops 6442450944 | bytes 4194304 | tf_op jit(solution)/shard_map/factor/pallas_call | solution.py:283
  100.2 8.6 %collective-permute-done.13.refs_6_ = bf16[2,128,384]{2,1,0:T(8,128)(2,1)S(1)} collective-permute-done((bf16[2,128,384]{2,1,0:T(8,128)(2,1)S(1)}, bf16[2,128,384]{2,1,0:T(8,128)(2,1)S(1)}, u32[]{:S(2)}, u32[]{:S(2)}) %collective-permute-start.13) | collective-permute-done | bytes 196640 | tf_op jit(solution)/shard_map/ppermute | solution.py:30
  108.8 12.3 %along.1 = (f32[2,2,512,384]{3,2,1,0:T(8,128)S(1)}, bf16[2,512,384]{2,1,0:T(8,128)(2,1)S(1)}) custom-call(s32[2]{0:T(128)S(1)} %pad_add_fusion.at_ref, f32[1]{0:T(128)} %get-tuple-element.38.inverse_ref, bf16[768,768]{1,0:T(8,128)(2,1)S(1)} %get-tuple-element.39.factor_ref, bf16[512,2048]{1,0:T(8,128)(2,1)S(1)} %convolution_convert_fusion.own_ref, ...), custom_call_target="tpu_custom_call" | custom-call | flops 6442450944 | bytes 12582912 | tf_op jit(solution)/shard_map/along/pallas_call | solution.py:298
  124.3 13.2 %collective-permute-done.16.weight_ref = bf16[2,384,384]{2,1,0:T(8,128)(2,1)S(1)} collective-permute-done((bf16[2,384,384]{2,1,0:T(8,128)(2,1)S(1)}, bf16[2,384,384]{2,1,0:T(8,128)(2,1)S(1)}, u32[]{:S(2)}, u32[]{:S(2)}) %collective-permute-start.16) | collective-permute-done | bytes 589856 | tf_op jit(solution)/shard_map/ppermute | solution.py:30
  137.5 2.9 %most.1 = (f32[2,2,512,384]{3,2,1,0:T(8,128)S(1)}, bf16[2,512,128]{2,1,0:T(8,128)(2,1)S(1)}) custom-call(s32[2]{0:T(128)S(1)} %pad_add_fusion.at_ref, bf16[512,2048]{1,0:T(8,128)(2,1)S(1)} %convolution_convert_fusion.own_ref, bf16[512,2048]{1,0:T(8,128)(2,1)} %collective-permute-done.8.other_ref, f32[2,2,512,384]{3,2,1,0:T(8,128)S(1)} %get-tuple-element.41.base_ref, ...), custom_call_target="tpu_custom_call" | custom-call | flops 805306368 | bytes 8388608 | tf_op jit(solution)/shard_map/most/pallas_call | solution.py:320
  153.8 6.8 %collective-permute-done.21.refs_4_ = bf16[2,64,384]{2,1,0:T(8,128)(2,1)S(1)} collective-permute-done((bf16[2,64,384]{2,1,0:T(8,128)(2,1)S(1)}, bf16[2,64,384]{2,1,0:T(8,128)(2,1)S(1)}, u32[]{:S(2)}, u32[]{:S(2)}) %collective-permute-start.21) | collective-permute-done | bytes 98336 | tf_op jit(solution)/shard_map/ppermute | solution.py:30
  160.7 3.0 %collective-permute-done.22.refs_5_ = bf16[2,64,384]{2,1,0:T(8,128)(2,1)S(1)} collective-permute-done((bf16[2,64,384]{2,1,0:T(8,128)(2,1)S(1)}, bf16[2,64,384]{2,1,0:T(8,128)(2,1)S(1)}, u32[]{:S(2)}, u32[]{:S(2)}) %collective-permute-start.22) | collective-permute-done | bytes 98336 | tf_op jit(solution)/shard_map/ppermute | solution.py:30
  165.1 3.7 %collective-permute-start.26 = (bf16[2,64,384]{2,1,0:T(8,128)(2,1)S(1)}, bf16[2,64,384]{2,1,0:T(8,128)(2,1)S(1)}, u32[]{:S(2)}, u32[]{:S(2)}) collective-permute-start(bf16[2,64,384]{2,1,0:T(8,128)(2,1)S(1)} %get-tuple-element.55), channel_id=1, source_target_pairs={{0,2},{1,3},{2,0},{3,1},{4,6},{5,7},{6,4},{7,5},{8,10},{9,11},{10,... | collective-permute-start | bytes 294920 | tf_op jit(solution)/shard_map/ppermute | solution.py:30
  169.2 2.5 %collective-permute-start.28 = (bf16[2,64,384]{2,1,0:T(8,128)(2,1)S(1)}, bf16[2,64,384]{2,1,0:T(8,128)(2,1)S(1)}, u32[]{:S(2)}, u32[]{:S(2)}) collective-permute-start(bf16[2,64,384]{2,1,0:T(8,128)(2,1)S(1)} %get-tuple-element.57), channel_id=1, source_target_pairs={{0,4},{1,5},{2,6},{3,7},{4,0},{5,1},{6,2},{7,3},{8,12},{9,13},{10,... | collective-permute-start | bytes 294920 | tf_op jit(solution)/shard_map/ppermute | solution.py:30
  174.7 2.5 %collective-permute-start.31 = (bf16[2,64,384]{2,1,0:T(8,128)(2,1)S(1)}, bf16[2,64,384]{2,1,0:T(8,128)(2,1)S(1)}, u32[]{:S(2)}, u32[]{:S(2)}) collective-permute-start(bf16[2,64,384]{2,1,0:T(8,128)(2,1)S(1)} %get-tuple-element.60), channel_id=1, source_target_pairs={{0,7},{1,6},{2,5},{3,4},{4,3},{5,2},{6,1},{7,0},{8,15},{9,14},{10,... | collective-permute-start | bytes 294920 | tf_op jit(solution)/shard_map/ppermute | solution.py:30
  177.3 6.2 %collective-permute-done.28 = bf16[2,64,384]{2,1,0:T(8,128)(2,1)S(1)} collective-permute-done((bf16[2,64,384]{2,1,0:T(8,128)(2,1)S(1)}, bf16[2,64,384]{2,1,0:T(8,128)(2,1)S(1)}, u32[]{:S(2)}, u32[]{:S(2)}) %collective-permute-start.28) | collective-permute-done | bytes 98336 | tf_op jit(solution)/shard_map/ppermute | solution.py:30
  183.6 2.5 %collective-permute-done.29 = bf16[2,64,384]{2,1,0:T(8,128)(2,1)S(1)} collective-permute-done((bf16[2,64,384]{2,1,0:T(8,128)(2,1)S(1)}, bf16[2,64,384]{2,1,0:T(8,128)(2,1)S(1)}, u32[]{:S(2)}, u32[]{:S(2)}) %collective-permute-start.29) | collective-permute-done | bytes 98336 | tf_op jit(solution)/shard_map/ppermute | solution.py:30
  (117 shorter events, 47.5 us)
Async XLA Ops:
  8.8 18.0 %collective-permute-start.1 = (bf16[2,32,2176]{2,1,0:T(8,128)(2,1)S(1)}, bf16[2,32,2176]{2,1,0:T(8,128)(2,1)S(1)}, u32[]{:S(2)}, u32[]{:S(2)}) collective-permute-start(bf16[2,32,2176]{2,1,0:T(8,128)(2,1)S(1)} %pad_maximum_fusion), channel_id=1, source_target_pairs={{0,2},{1,3},{2,0},{3,1},{4,6},{5,7},{6,4},{7,5},{8,10},{9,11},{10,... | collective-permute-start | bytes 835592 | tf_op jit(solution)/shard_map/ppermute | solution.py:30
  10.6 14.1 %collective-permute-start.2 = (bf16[2,32,2176]{2,1,0:T(8,128)(2,1)S(1)}, bf16[2,32,2176]{2,1,0:T(8,128)(2,1)S(1)}, u32[]{:S(2)}, u32[]{:S(2)}) collective-permute-start(bf16[2,32,2176]{2,1,0:T(8,128)(2,1)S(1)} %pad_maximum_fusion), channel_id=1, source_target_pairs={{0,6},{1,7},{2,4},{3,5},{4,2},{5,3},{6,0},{7,1},{8,14},{9,15},{10,... | collective-permute-start | bytes 835592 | tf_op jit(solution)/shard_map/ppermute | solution.py:30
  13.1 19.7 %collective-permute-start.4 = (bf16[2,32,2176]{2,1,0:T(8,128)(2,1)S(1)}, bf16[2,32,2176]{2,1,0:T(8,128)(2,1)S(1)}, u32[]{:S(2)}, u32[]{:S(2)}) collective-permute-start(bf16[2,32,2176]{2,1,0:T(8,128)(2,1)S(1)} %pad_maximum_fusion), channel_id=1, source_target_pairs={{0,1},{1,0},{2,3},{3,2},{4,5},{5,4},{6,7},{7,6},{8,9},{9,8},{10,11... | collective-permute-start | bytes 835592 | tf_op jit(solution)/shard_map/ppermute | solution.py:30
  25.3 15.0 %collective-permute-start.6 = (bf16[2,32,2176]{2,1,0:T(8,128)(2,1)S(1)}, bf16[2,32,2176]{2,1,0:T(8,128)(2,1)S(1)}, u32[]{:S(2)}, u32[]{:S(2)}) collective-permute-start(bf16[2,32,2176]{2,1,0:T(8,128)(2,1)S(1)} %collective-permute-done.2), channel_id=1, source_target_pairs={{0,1},{1,0},{2,3},{3,2},{4,5},{5,4},{6,7},{7,6},{8,9},{9,8},{10,11... | collective-permute-start | bytes 835592 | tf_op jit(solution)/shard_map/ppermute | solution.py:30
  26.8 13.5 %collective-permute-start.5 = (bf16[2,32,2176]{2,1,0:T(8,128)(2,1)S(1)}, bf16[2,32,2176]{2,1,0:T(8,128)(2,1)S(1)}, u32[]{:S(2)}, u32[]{:S(2)}) collective-permute-start(bf16[2,32,2176]{2,1,0:T(8,128)(2,1)S(1)} %collective-permute-done.1), channel_id=1, source_target_pairs={{0,1},{1,0},{2,3},{3,2},{4,5},{5,4},{6,7},{7,6},{8,9},{9,8},{10,11... | collective-permute-start | bytes 835592 | tf_op jit(solution)/shard_map/ppermute | solution.py:30
  31.3 11.9 %collective-permute-start.7 = (bf16[2,32,2176]{2,1,0:T(8,128)(2,1)S(1)}, bf16[2,32,2176]{2,1,0:T(8,128)(2,1)S(1)}, u32[]{:S(2)}, u32[]{:S(2)}) collective-permute-start(bf16[2,32,2176]{2,1,0:T(8,128)(2,1)S(1)} %collective-permute-done.3), channel_id=1, source_target_pairs={{0,1},{1,0},{2,3},{3,2},{4,5},{5,4},{6,7},{7,6},{8,9},{9,8},{10,11... | collective-permute-start | bytes 835592 | tf_op jit(solution)/shard_map/ppermute | solution.py:30
  47.5 61.3 %collective-permute-start.8 = (bf16[512,2048]{1,0:T(8,128)(2,1)S(1)}, bf16[512,2048]{1,0:T(8,128)(2,1)}, u32[]{:S(2)}, u32[]{:S(2)}) collective-permute-start(bf16[512,2048]{1,0:T(8,128)(2,1)S(1)} %convolution_convert_fusion.own_ref), channel_id=1, source_target_pairs={{0,8},{8,0},{16,24},{24,16},{1,9},{9,1},{17,25},{25,17},{2,10},{10... | collective-permute-start | bytes 6291464 | tf_op jit(solution)/shard_map/ppermute | solution.py:30
  55.2 19.9 %collective-permute-start.10 = (bf16[512,768]{1,0:T(8,128)(2,1)}, bf16[512,768]{1,0:T(8,128)(2,1)}, u32[]{:S(2)}, u32[]{:S(2)}) collective-permute-start(bf16[512,768]{1,0:T(8,128)(2,1)} %get-tuple-element.36), channel_id=1, source_target_pairs={{0,24},{8,16},{16,8},{24,0},{1,25},{9,17},{17,9},{25,1},{2,26},{10... | collective-permute-start | bytes 2359304 | tf_op jit(solution)/shard_map/ppermute | solution.py:30
  56.4 36.1 %collective-permute-start.11 = (bf16[512,768]{1,0:T(8,128)(2,1)}, bf16[512,768]{1,0:T(8,128)(2,1)}, u32[]{:S(2)}, u32[]{:S(2)}) collective-permute-start(bf16[512,768]{1,0:T(8,128)(2,1)} %get-tuple-element.37), channel_id=1, source_target_pairs={{0,16},{8,24},{16,0},{24,8},{1,17},{9,25},{17,1},{25,9},{2,18},{10... | collective-permute-start | bytes 2359304 | tf_op jit(solution)/shard_map/ppermute | solution.py:30
  59.7 49.1 %collective-permute-start.12 = (bf16[2,512,384]{2,1,0:T(8,128)(2,1)}, bf16[2,512,384]{2,1,0:T(8,128)(2,1)}, u32[]{:S(2)}, u32[]{:S(2)}) collective-permute-start(bf16[2,512,384]{2,1,0:T(8,128)(2,1)} %get-tuple-element.67), channel_id=1, source_target_pairs={{0,8},{8,0},{16,24},{24,16},{1,9},{9,1},{17,25},{25,17},{2,10},{10... | collective-permute-start | bytes 2359304 | tf_op jit(solution)/shard_map/ppermute | solution.py:30
  62.3 46.5 %collective-permute-start.14 = (bf16[2,384,384]{2,1,0:T(8,128)(2,1)S(1)}, bf16[2,384,384]{2,1,0:T(8,128)(2,1)S(1)}, u32[]{:S(2)}, u32[]{:S(2)}) collective-permute-start(bf16[2,384,384]{2,1,0:T(8,128)(2,1)S(1)} %get-tuple-element.66), channel_id=1, source_target_pairs={{0,24},{8,16},{16,8},{24,0},{1,25},{9,17},{17,9},{25,1},{2,26},{10... | collective-permute-start | bytes 1769480 | tf_op jit(solution)/shard_map/ppermute | solution.py:30
  75.2 33.6 %collective-permute-start.13 = (bf16[2,128,384]{2,1,0:T(8,128)(2,1)S(1)}, bf16[2,128,384]{2,1,0:T(8,128)(2,1)S(1)}, u32[]{:S(2)}, u32[]{:S(2)}) collective-permute-start(bf16[2,128,384]{2,1,0:T(8,128)(2,1)S(1)} %constant_dynamic-slice_fusion.1), channel_id=1, source_target_pairs={{0,24},{8,16},{16,8},{24,0},{1,25},{9,17},{17,9},{25,1},{2,26},{10... | collective-permute-start | bytes 589832 | tf_op jit(solution)/shard_map/ppermute | solution.py:30
  121.1 16.4 %collective-permute-start.15 = (bf16[2,512,384]{2,1,0:T(8,128)(2,1)S(1)}, bf16[2,512,384]{2,1,0:T(8,128)(2,1)S(1)}, u32[]{:S(2)}, u32[]{:S(2)}) collective-permute-start(bf16[2,512,384]{2,1,0:T(8,128)(2,1)S(1)} %get-tuple-element.42), channel_id=1, source_target_pairs={{0,8},{8,0},{16,24},{24,16},{1,9},{9,1},{17,25},{25,17},{2,10},{10... | collective-permute-start | bytes 2359304 | tf_op jit(solution)/shard_map/ppermute | solution.py:30
  121.2 16.3 %collective-permute-start.16 = (bf16[2,384,384]{2,1,0:T(8,128)(2,1)S(1)}, bf16[2,384,384]{2,1,0:T(8,128)(2,1)S(1)}, u32[]{:S(2)}, u32[]{:S(2)}) collective-permute-start(bf16[2,384,384]{2,1,0:T(8,128)(2,1)S(1)} %get-tuple-element.65), channel_id=1, source_target_pairs={{0,16},{8,24},{16,0},{24,8},{1,17},{9,25},{17,1},{25,9},{2,18},{10... | collective-permute-start | bytes 1769480 | tf_op jit(solution)/shard_map/ppermute | solution.py:30
  123.7 17.4 %collective-permute-start.17 = (bf16[2,128,384]{2,1,0:T(8,128)(2,1)S(1)}, bf16[2,128,384]{2,1,0:T(8,128)(2,1)S(1)}, u32[]{:S(2)}, u32[]{:S(2)}) collective-permute-start(bf16[2,128,384]{2,1,0:T(8,128)(2,1)S(1)} %constant_dynamic-slice_fusion.5), channel_id=1, source_target_pairs={{0,16},{8,24},{16,0},{24,8},{1,17},{9,25},{17,1},{25,9},{2,18},{10... | collective-permute-start | bytes 589832 | tf_op jit(solution)/shard_map/ppermute | solution.py:30
  146.2 14.5 %collective-permute-start.21 = (bf16[2,64,384]{2,1,0:T(8,128)(2,1)S(1)}, bf16[2,64,384]{2,1,0:T(8,128)(2,1)S(1)}, u32[]{:S(2)}, u32[]{:S(2)}) collective-permute-start(bf16[2,64,384]{2,1,0:T(8,128)(2,1)S(1)} %get-tuple-element.49), channel_id=1, source_target_pairs={{0,4},{1,5},{2,6},{3,7},{4,0},{5,1},{6,2},{7,3},{8,12},{9,13},{10,... | collective-permute-start | bytes 294920 | tf_op jit(solution)/shard_map/ppermute | solution.py:30
  147.8 15.9 %collective-permute-start.22 = (bf16[2,64,384]{2,1,0:T(8,128)(2,1)S(1)}, bf16[2,64,384]{2,1,0:T(8,128)(2,1)S(1)}, u32[]{:S(2)}, u32[]{:S(2)}) collective-permute-start(bf16[2,64,384]{2,1,0:T(8,128)(2,1)S(1)} %get-tuple-element.50), channel_id=1, source_target_pairs={{0,5},{1,4},{2,7},{3,6},{4,1},{5,0},{6,3},{7,2},{8,13},{9,12},{10,... | collective-permute-start | bytes 294920 | tf_op jit(solution)/shard_map/ppermute | solution.py:30
  150.0 13.6 %collective-permute-start.23 = (bf16[2,64,384]{2,1,0:T(8,128)(2,1)S(1)}, bf16[2,64,384]{2,1,0:T(8,128)(2,1)S(1)}, u32[]{:S(2)}, u32[]{:S(2)}) collective-permute-start(bf16[2,64,384]{2,1,0:T(8,128)(2,1)S(1)} %get-tuple-element.51), channel_id=1, source_target_pairs={{0,6},{1,7},{2,4},{3,5},{4,2},{5,3},{6,0},{7,1},{8,14},{9,15},{10,... | collective-permute-start | bytes 294920 | tf_op jit(solution)/shard_map/ppermute | solution.py:30
  151.4 12.3 %collective-permute-start.24 = (bf16[2,64,384]{2,1,0:T(8,128)(2,1)S(1)}, bf16[2,64,384]{2,1,0:T(8,128)(2,1)S(1)}, u32[]{:S(2)}, u32[]{:S(2)}) collective-permute-start(bf16[2,64,384]{2,1,0:T(8,128)(2,1)S(1)} %get-tuple-element.52), channel_id=1, source_target_pairs={{0,7},{1,6},{2,5},{3,4},{4,3},{5,2},{6,1},{7,0},{8,15},{9,14},{10,... | collective-permute-start | bytes 294920 | tf_op jit(solution)/shard_map/ppermute | solution.py:30
  165.1 9.7 %collective-permute-start.26 = (bf16[2,64,384]{2,1,0:T(8,128)(2,1)S(1)}, bf16[2,64,384]{2,1,0:T(8,128)(2,1)S(1)}, u32[]{:S(2)}, u32[]{:S(2)}) collective-permute-start(bf16[2,64,384]{2,1,0:T(8,128)(2,1)S(1)} %get-tuple-element.55), channel_id=1, source_target_pairs={{0,2},{1,3},{2,0},{3,1},{4,6},{5,7},{6,4},{7,5},{8,10},{9,11},{10,... | collective-permute-start | bytes 294920 | tf_op jit(solution)/shard_map/ppermute | solution.py:30
  169.2 14.3 %collective-permute-start.28 = (bf16[2,64,384]{2,1,0:T(8,128)(2,1)S(1)}, bf16[2,64,384]{2,1,0:T(8,128)(2,1)S(1)}, u32[]{:S(2)}, u32[]{:S(2)}) collective-permute-start(bf16[2,64,384]{2,1,0:T(8,128)(2,1)S(1)} %get-tuple-element.57), channel_id=1, source_target_pairs={{0,4},{1,5},{2,6},{3,7},{4,0},{5,1},{6,2},{7,3},{8,12},{9,13},{10,... | collective-permute-start | bytes 294920 | tf_op jit(solution)/shard_map/ppermute | solution.py:30
  171.7 14.4 %collective-permute-start.29 = (bf16[2,64,384]{2,1,0:T(8,128)(2,1)S(1)}, bf16[2,64,384]{2,1,0:T(8,128)(2,1)S(1)}, u32[]{:S(2)}, u32[]{:S(2)}) collective-permute-start(bf16[2,64,384]{2,1,0:T(8,128)(2,1)S(1)} %get-tuple-element.58), channel_id=1, source_target_pairs={{0,5},{1,4},{2,7},{3,6},{4,1},{5,0},{6,3},{7,2},{8,13},{9,12},{10,... | collective-permute-start | bytes 294920 | tf_op jit(solution)/shard_map/ppermute | solution.py:30
  172.7 13.5 %collective-permute-start.30 = (bf16[2,64,384]{2,1,0:T(8,128)(2,1)S(1)}, bf16[2,64,384]{2,1,0:T(8,128)(2,1)S(1)}, u32[]{:S(2)}, u32[]{:S(2)}) collective-permute-start(bf16[2,64,384]{2,1,0:T(8,128)(2,1)S(1)} %get-tuple-element.59), channel_id=1, source_target_pairs={{0,6},{1,7},{2,4},{3,5},{4,2},{5,3},{6,0},{7,1},{8,14},{9,15},{10,... | collective-permute-start | bytes 294920 | tf_op jit(solution)/shard_map/ppermute | solution.py:30
  174.7 11.6 %collective-permute-start.31 = (bf16[2,64,384]{2,1,0:T(8,128)(2,1)S(1)}, bf16[2,64,384]{2,1,0:T(8,128)(2,1)S(1)}, u32[]{:S(2)}, u32[]{:S(2)}) collective-permute-start(bf16[2,64,384]{2,1,0:T(8,128)(2,1)S(1)} %get-tuple-element.60), channel_id=1, source_target_pairs={{0,7},{1,6},{2,5},{3,4},{4,3},{5,2},{6,1},{7,0},{8,15},{9,14},{10,... | collective-permute-start | bytes 294920 | tf_op jit(solution)/shard_map/ppermute | solution.py:30
  (12 other events, 114.6 us)

commit v5 on v4

--- a/solution.py
+++ b/solution.py
@@ -41,12 +41,16 @@
     return jnp.where(routed == 1, place, 0)
 
 
-def gathered(block):
+def gathered(tokens, slots, sent):
     fsdp_size, group_size = lax.axis_size("fsdp"), lax.axis_size("expert")
     f, r = lax.axis_index("fsdp"), lax.axis_index("expert")
+    block = jnp.concatenate([tokens, slots], axis=1)
     held, masks = block[None], [0]
     if group_size == 8:
         mask = 2
+        came = jnp.concatenate([sent, swapped(slots, "fsdp", mask)], axis=1)
+        held, masks = jnp.stack([block, came]), [0, mask]
+        mask = 4
         while mask < fsdp_size:
             held = jnp.concatenate([held, swapped(held, "fsdp", mask)])
             masks += [m ^ mask for m in masks]
@@ -205,6 +209,8 @@
             (2, depth, half_width),
         )
 
+    token_rows = tokens.reshape(2 * tok_dev, model_width)
+    token_sent = swapped(token_rows, "fsdp", 2)
     lead, lead_rows = far[-1], max(128, local_rows // 4)
     early_part = weight_part(weight, lead, 0, lead_rows)
     early_part = swapped(early_part, "fsdp", lead)
@@ -212,10 +218,8 @@
     slot_lanes = -(-experts // 128) * 128
     slots = slots_of(routes, experts).astype(jnp.bfloat16)
     slots = jnp.pad(slots, ((0, 0), (0, 0), (0, slot_lanes - experts)))
-    block = jnp.concatenate([tokens, slots], axis=2)
-    block = block.reshape(2 * tok_dev, model_width + slot_lanes)
-    block, weight = lax.optimization_barrier((block, weight))
-    blocks, source_pair, source_group = gathered(block)
+    slots = slots.reshape(2 * tok_dev, slot_lanes)
+    blocks, source_pair, source_group = gathered(token_rows, slots, token_sent)
     all_rows = blocks.reshape(-1, model_width + slot_lanes)
     lane = lax.broadcasted_iota(jnp.int32, (1, slot_lanes), 1)
     picked = jnp.where(lane == own_expert, all_rows[:, model_width:].astype(jnp.float32), 0.0)

time: 188 us -> 187 us (level)
    ppermute x32 -> x33, starting transfers between devices: 44.3 us -> 43.4 us  [swapped(): lax.ppermute(shard, axis, [(i, i ^ mask) for i in range(lax.axis_size(axi...]
    dynamic_slice x4 -> x3, local copies, waits for them, and re-layouts: 6.07 us -> 5.23 us  [weight_part(): lax.dynamic_slice(weight, (target // 2 * 2, first, target % 2 * half_widt...]
    ppermute x32 -> x33, waiting for transfers between devices: 91.8 us -> 91.7 us  [swapped(): lax.ppermute(shard, axis, [(i, i ^ mask) for i in range(lax.axis_size(axi...]
  transfers between devices with their start and end apart: 32 -> 33, of which waited for: 14 -> 14; matrix products, arithmetic and copies ran while one was open for 8% -> 9% of each run, Pallas kernels for 7% -> 8%
where the time goes in v5:
time: 187 us; the launch traced here: 186 us
  waiting for transfers between devices  91.7 us (49%)
  starting transfers between devices  43.4 us (23%)
  Pallas kernels  28.5 us (15%)
  other arithmetic  10.3 us (6%)
  local copies, waits for them, and re-layouts  9.25 us (5%)
  matrix products  2.84 us (2%)
    ppermute x33, waiting for transfers between devices, swapped(): lax.ppermute(shard, axis, [(i, i ^ mask) for i in range(lax.axis_size(axi...  91.7 us
    ppermute x33, starting transfers between devices, swapped(): lax.ppermute(shard, axis, [(i, i ^ mask) for i in range(lax.axis_size(axi...  43.4 us
    pallas_call x1, Pallas kernels, on_device(): pl.pallas_call(functools.partial(along_kernel, order, places, update_scal...  12.3 us
    pallas_call x1, Pallas kernels, on_device(): pl.pallas_call(factor_kernel, out_shape=[shaped(jnp.bfloat16, hidden_widt...  7.91 us
    convert_element_type x2, other arithmetic, on_device(): (grad_part + momentum_decay * accumulated).astype(jnp.bfloat16)  7.14 us
    dynamic_slice x3, local copies, waits for them, and re-layouts, weight_part(): lax.dynamic_slice(weight, (target // 2 * 2, first, target % 2 * half_widt...  5.23 us
  transfers between devices with their start and end apart: 33, of which 14 were waited for; matrix products, arithmetic and copies ran while one was open for 9% of the time, Pallas kernels for 8%

profile of v5, /device:TPU:0, one launch (start us, length us, event | category | flops | bytes accessed | tf_op | source)
XLA Modules:
  0.0 186.4 jit_solution(17798556230513429117)
XLA Ops:
  1.1 3.1 %collective-permute-start.1 = (bf16[32,128]{1,0:T(8,128)(2,1)S(1)}, bf16[32,128]{1,0:T(8,128)(2,1)S(1)}, u32[]{:S(2)}, u32[]{:S(2)}) collective-permute-start(bf16[32,128]{1,0:T(8,128)(2,1)S(1)} %bitcast.111), channel_id=1, source_target_pairs={{0,16},{8,24},{16,0},{24,8},{1,17},{9,25},{17,1},{25,9},{2,18},{10... | collective-permute-start | bytes 24584 | tf_op jit(solution)/shard_map/ppermute | solution.py:30
  15.0 9.7 %collective-permute-done.3 = bf16[2,32,2176]{2,1,0:T(8,128)(2,1)S(1)} collective-permute-done((bf16[2,32,2176]{2,1,0:T(8,128)(2,1)S(1)}, bf16[2,32,2176]{2,1,0:T(8,128)(2,1)S(1)}, u32[]{:S(2)}, u32[]{:S(2)}) %collective-permute-start.3) | collective-permute-done | bytes 278560 | tf_op jit(solution)/shard_map/ppermute | solution.py:30
  26.9 4.3 %collective-permute-done.4 = bf16[2,32,2176]{2,1,0:T(8,128)(2,1)S(1)} collective-permute-done((bf16[2,32,2176]{2,1,0:T(8,128)(2,1)S(1)}, bf16[2,32,2176]{2,1,0:T(8,128)(2,1)S(1)}, u32[]{:S(2)}, u32[]{:S(2)}) %collective-permute-start.4) | collective-permute-done | bytes 278560 | tf_op jit(solution)/shard_map/ppermute | solution.py:30
  32.9 6.6 %collective-permute-done.6 = bf16[2,32,2176]{2,1,0:T(8,128)(2,1)S(1)} collective-permute-done((bf16[2,32,2176]{2,1,0:T(8,128)(2,1)S(1)}, bf16[2,32,2176]{2,1,0:T(8,128)(2,1)S(1)}, u32[]{:S(2)}, u32[]{:S(2)}) %collective-permute-start.6) | collective-permute-done | bytes 278560 | tf_op jit(solution)/shard_map/ppermute | solution.py:30
  39.5 2.9 %collective-permute-done.8 = bf16[2,32,2176]{2,1,0:T(8,128)(2,1)S(1)} collective-permute-done((bf16[2,32,2176]{2,1,0:T(8,128)(2,1)S(1)}, bf16[2,32,2176]{2,1,0:T(8,128)(2,1)S(1)}, u32[]{:S(2)}, u32[]{:S(2)}) %collective-permute-start.8) | collective-permute-done | bytes 278560 | tf_op jit(solution)/shard_map/ppermute | solution.py:30
  43.9 2.8 %convolution_convert_fusion.own_ref = bf16[512,2048]{1,0:T(8,128)(2,1)S(1)} fusion(bf16[512,2176]{1,0:T(8,128)(2,1)} %bitcast.115, s32[512]{0:T(512)S(1)} %add_select_fusion), kind=kOutput, calls=%fused_computation | convolution fusion | flops 1075052544 | bytes 4196352 | tf_op jit(solution)/shard_map/dot_general | solution.py:26
  46.8 3.7 %fusion.4 = (bf16[512,768]{1,0:T(8,128)(2,1)}, bf16[512,768]{1,0:T(8,128)(2,1)}) fusion(bf16[4,512,768]{2,1,0:T(8,128)(2,1)} %bitcast.85, s32[]{:T(128)S(6)} %select_n.169, bf16[4,512,768]{2,1,0:T(8,128)(2,1)} %bitcast.87, s32[]{:T(128)S(6)} %select_n.168), kind=kLoop, calls=%fused_computation.13 | loop fusion | flops 5505024 | bytes 4718600 | tf_op jit(solution)/shard_map/convert_element_type | solution.py:245
  50.6 3.4 %fusion.8 = (bf16[512,768]{1,0:T(8,128)(2,1)}, bf16[512,768]{1,0:T(8,128)(2,1)S(1)}) fusion(bf16[4,512,768]{2,1,0:T(8,128)(2,1)} %bitcast.86, s32[]{:T(128)S(6)} %select_n.171, bf16[4,512,768]{2,1,0:T(8,128)(2,1)} %bitcast.88, s32[]{:T(128)S(6)} %select_n.170), kind=kLoop, calls=%fused_computation.17 | loop fusion | flops 5505024 | bytes 4718600 | tf_op jit(solution)/shard_map/convert_element_type | solution.py:245
  56.1 2.8 %constant_dynamic-slice_fusion.2 = (bf16[2,512,384]{2,1,0:T(8,128)(2,1)}, bf16[2,512,384]{2,1,0:T(8,128)(2,1)}) fusion(bf16[4,512,768]{2,1,0:T(8,128)(2,1)} %bitcast.89, s32[]{:T(128)S(6)} %select_n.176, s32[]{:T(128)S(6)} %select_n.178, s32[]{:T(128)S(6)} %select_n.172, s32[]{:T(128)S(6)} %select_n.174), kind=kLoop, calls=%fused_computation.56 | loop fusion | bytes 3145744 | tf_op jit(solution)/shard_map/dynamic_slice | solution.py:206
  63.0 11.4 %collective-permute-done.11.refs_2_.refs_3_ = bf16[512,768]{1,0:T(8,128)(2,1)} collective-permute-done((bf16[512,768]{1,0:T(8,128)(2,1)}, bf16[512,768]{1,0:T(8,128)(2,1)}, u32[]{:S(2)}, u32[]{:S(2)}) %collective-permute-start.11) | collective-permute-done | bytes 786464 | tf_op jit(solution)/shard_map/ppermute | solution.py:30
  75.6 3.4 %gram.1.gram_ref = f32[768,768]{1,0:T(8,128)S(1)} custom-call(bf16[512,768]{1,0:T(8,128)(2,1)S(1)} %get-tuple-element.58.refs_0_, bf16[512,768]{1,0:T(8,128)(2,1)} %collective-permute-done.10.refs_1_, bf16[512,768]{1,0:T(8,128)(2,1)} %collective-permute-done.11.refs_2_.refs_3_), custom_call_target="tpu_custom_call" | custom-call | flops 3221225472 | bytes 4194304 | tf_op jit(solution)/shard_map/gram/pallas_call | solution.py:278
  79.1 12.6 %collective-permute-done.12.refs_0_.refs_2_ = bf16[512,768]{1,0:T(8,128)(2,1)} collective-permute-done((bf16[512,768]{1,0:T(8,128)(2,1)}, bf16[512,768]{1,0:T(8,128)(2,1)}, u32[]{:S(2)}, u32[]{:S(2)}) %collective-permute-start.12) | collective-permute-done | bytes 786464 | tf_op jit(solution)/shard_map/ppermute | solution.py:30
  91.7 7.9 %factor.1 = (bf16[768,768]{1,0:T(8,128)(2,1)S(1)}, f32[1]{0:T(128)}) custom-call(f32[768,768]{1,0:T(8,128)S(1)} %gram.1.gram_ref, bf16[512,768]{1,0:T(8,128)(2,1)} %collective-permute-done.12.refs_0_.refs_2_), custom_call_target="tpu_custom_call" | custom-call | flops 6442450944 | bytes 4194304 | tf_op jit(solution)/shard_map/factor/pallas_call | solution.py:287
  99.6 8.4 %collective-permute-done.14.refs_6_ = bf16[2,128,384]{2,1,0:T(8,128)(2,1)S(1)} collective-permute-done((bf16[2,128,384]{2,1,0:T(8,128)(2,1)S(1)}, bf16[2,128,384]{2,1,0:T(8,128)(2,1)S(1)}, u32[]{:S(2)}, u32[]{:S(2)}) %collective-permute-start.14) | collective-permute-done | bytes 196640 | tf_op jit(solution)/shard_map/ppermute | solution.py:30
  108.0 12.3 %along.1 = (f32[2,2,512,384]{3,2,1,0:T(8,128)S(1)}, bf16[2,512,384]{2,1,0:T(8,128)(2,1)S(1)}) custom-call(s32[2]{0:T(128)S(1)} %pad_add_fusion.at_ref, f32[1]{0:T(128)} %get-tuple-element.35.inverse_ref, bf16[768,768]{1,0:T(8,128)(2,1)S(1)} %get-tuple-element.36.factor_ref, bf16[512,2048]{1,0:T(8,128)(2,1)S(1)} %convolution_convert_fusion.own_ref, ...), custom_call_target="tpu_custom_call" | custom-call | flops 6442450944 | bytes 12582912 | tf_op jit(solution)/shard_map/along/pallas_call | solution.py:302
  122.5 14.2 %collective-permute-done.17.weight_ref = bf16[2,384,384]{2,1,0:T(8,128)(2,1)S(1)} collective-permute-done((bf16[2,384,384]{2,1,0:T(8,128)(2,1)S(1)}, bf16[2,384,384]{2,1,0:T(8,128)(2,1)S(1)}, u32[]{:S(2)}, u32[]{:S(2)}) %collective-permute-start.17) | collective-permute-done | bytes 589856 | tf_op jit(solution)/shard_map/ppermute | solution.py:30
  136.7 2.8 %most.1 = (f32[2,2,512,384]{3,2,1,0:T(8,128)S(1)}, bf16[2,512,128]{2,1,0:T(8,128)(2,1)S(1)}) custom-call(s32[2]{0:T(128)S(1)} %pad_add_fusion.at_ref, bf16[512,2048]{1,0:T(8,128)(2,1)S(1)} %convolution_convert_fusion.own_ref, bf16[512,2048]{1,0:T(8,128)(2,1)} %collective-permute-done.9.other_ref, f32[2,2,512,384]{3,2,1,0:T(8,128)S(1)} %get-tuple-element.37.base_ref, ...), custom_call_target="tpu_custom_call" | custom-call | flops 805306368 | bytes 8388608 | tf_op jit(solution)/shard_map/most/pallas_call | solution.py:324
  152.9 6.8 %collective-permute-done.22.refs_4_ = bf16[2,64,384]{2,1,0:T(8,128)(2,1)S(1)} collective-permute-done((bf16[2,64,384]{2,1,0:T(8,128)(2,1)S(1)}, bf16[2,64,384]{2,1,0:T(8,128)(2,1)S(1)}, u32[]{:S(2)}, u32[]{:S(2)}) %collective-permute-start.22) | collective-permute-done | bytes 98336 | tf_op jit(solution)/shard_map/ppermute | solution.py:30
  159.8 3.0 %collective-permute-done.23.refs_5_ = bf16[2,64,384]{2,1,0:T(8,128)(2,1)S(1)} collective-permute-done((bf16[2,64,384]{2,1,0:T(8,128)(2,1)S(1)}, bf16[2,64,384]{2,1,0:T(8,128)(2,1)S(1)}, u32[]{:S(2)}, u32[]{:S(2)}) %collective-permute-start.23) | collective-permute-done | bytes 98336 | tf_op jit(solution)/shard_map/ppermute | solution.py:30
  164.2 3.7 %collective-permute-start.27 = (bf16[2,64,384]{2,1,0:T(8,128)(2,1)S(1)}, bf16[2,64,384]{2,1,0:T(8,128)(2,1)S(1)}, u32[]{:S(2)}, u32[]{:S(2)}) collective-permute-start(bf16[2,64,384]{2,1,0:T(8,128)(2,1)S(1)} %get-tuple-element.51), channel_id=1, source_target_pairs={{0,2},{1,3},{2,0},{3,1},{4,6},{5,7},{6,4},{7,5},{8,10},{9,11},{10,... | collective-permute-start | bytes 294920 | tf_op jit(solution)/shard_map/ppermute | solution.py:30
  168.3 2.5 %collective-permute-start.29 = (bf16[2,64,384]{2,1,0:T(8,128)(2,1)S(1)}, bf16[2,64,384]{2,1,0:T(8,128)(2,1)S(1)}, u32[]{:S(2)}, u32[]{:S(2)}) collective-permute-start(bf16[2,64,384]{2,1,0:T(8,128)(2,1)S(1)} %get-tuple-element.53), channel_id=1, source_target_pairs={{0,4},{1,5},{2,6},{3,7},{4,0},{5,1},{6,2},{7,3},{8,12},{9,13},{10,... | collective-permute-start | bytes 294920 | tf_op jit(solution)/shard_map/ppermute | solution.py:30
  173.8 2.5 %collective-permute-start.32 = (bf16[2,64,384]{2,1,0:T(8,128)(2,1)S(1)}, bf16[2,64,384]{2,1,0:T(8,128)(2,1)S(1)}, u32[]{:S(2)}, u32[]{:S(2)}) collective-permute-start(bf16[2,64,384]{2,1,0:T(8,128)(2,1)S(1)} %get-tuple-element.56), channel_id=1, source_target_pairs={{0,7},{1,6},{2,5},{3,4},{4,3},{5,2},{6,1},{7,0},{8,15},{9,14},{10,... | collective-permute-start | bytes 294920 | tf_op jit(solution)/shard_map/ppermute | solution.py:30
  176.4 6.2 %collective-permute-done.29 = bf16[2,64,384]{2,1,0:T(8,128)(2,1)S(1)} collective-permute-done((bf16[2,64,384]{2,1,0:T(8,128)(2,1)S(1)}, bf16[2,64,384]{2,1,0:T(8,128)(2,1)S(1)}, u32[]{:S(2)}, u32[]{:S(2)}) %collective-permute-start.29) | collective-permute-done | bytes 98336 | tf_op jit(solution)/shard_map/ppermute | solution.py:30
  182.7 2.5 %collective-permute-done.30 = bf16[2,64,384]{2,1,0:T(8,128)(2,1)S(1)} collective-permute-done((bf16[2,64,384]{2,1,0:T(8,128)(2,1)S(1)}, bf16[2,64,384]{2,1,0:T(8,128)(2,1)S(1)}, u32[]{:S(2)}, u32[]{:S(2)}) %collective-permute-start.30) | collective-permute-done | bytes 98336 | tf_op jit(solution)/shard_map/ppermute | solution.py:30
  (120 shorter events, 46.3 us)
Async XLA Ops:
  9.4 17.0 %collective-permute-start.2 = (bf16[2,32,2176]{2,1,0:T(8,128)(2,1)S(1)}, bf16[2,32,2176]{2,1,0:T(8,128)(2,1)S(1)}, u32[]{:S(2)}, u32[]{:S(2)}) collective-permute-start(bf16[2,32,2176]{2,1,0:T(8,128)(2,1)S(1)} %pad_maximum_fusion), channel_id=1, source_target_pairs={{0,2},{1,3},{2,0},{3,1},{4,6},{5,7},{6,4},{7,5},{8,10},{9,11},{10,... | collective-permute-start | bytes 835592 | tf_op jit(solution)/shard_map/ppermute | solution.py:30
  11.0 13.7 %collective-permute-start.3 = (bf16[2,32,2176]{2,1,0:T(8,128)(2,1)S(1)}, bf16[2,32,2176]{2,1,0:T(8,128)(2,1)S(1)}, u32[]{:S(2)}, u32[]{:S(2)}) collective-permute-start(bf16[2,32,2176]{2,1,0:T(8,128)(2,1)S(1)} %pad_maximum_fusion), channel_id=1, source_target_pairs={{0,6},{1,7},{2,4},{3,5},{4,2},{5,3},{6,0},{7,1},{8,14},{9,15},{10,... | collective-permute-start | bytes 835592 | tf_op jit(solution)/shard_map/ppermute | solution.py:30
  13.5 19.3 %collective-permute-start.5 = (bf16[2,32,2176]{2,1,0:T(8,128)(2,1)S(1)}, bf16[2,32,2176]{2,1,0:T(8,128)(2,1)S(1)}, u32[]{:S(2)}, u32[]{:S(2)}) collective-permute-start(bf16[2,32,2176]{2,1,0:T(8,128)(2,1)S(1)} %pad_maximum_fusion), channel_id=1, source_target_pairs={{0,1},{1,0},{2,3},{3,2},{4,5},{5,4},{6,7},{7,6},{8,9},{9,8},{10,11... | collective-permute-start | bytes 835592 | tf_op jit(solution)/shard_map/ppermute | solution.py:30
  24.9 14.6 %collective-permute-start.7 = (bf16[2,32,2176]{2,1,0:T(8,128)(2,1)S(1)}, bf16[2,32,2176]{2,1,0:T(8,128)(2,1)S(1)}, u32[]{:S(2)}, u32[]{:S(2)}) collective-permute-start(bf16[2,32,2176]{2,1,0:T(8,128)(2,1)S(1)} %collective-permute-done.3), channel_id=1, source_target_pairs={{0,1},{1,0},{2,3},{3,2},{4,5},{5,4},{6,7},{7,6},{8,9},{9,8},{10,11... | collective-permute-start | bytes 835592 | tf_op jit(solution)/shard_map/ppermute | solution.py:30
  26.3 13.1 %collective-permute-start.6 = (bf16[2,32,2176]{2,1,0:T(8,128)(2,1)S(1)}, bf16[2,32,2176]{2,1,0:T(8,128)(2,1)S(1)}, u32[]{:S(2)}, u32[]{:S(2)}) collective-permute-start(bf16[2,32,2176]{2,1,0:T(8,128)(2,1)S(1)} %collective-permute-done.2), channel_id=1, source_target_pairs={{0,1},{1,0},{2,3},{3,2},{4,5},{5,4},{6,7},{7,6},{8,9},{9,8},{10,11... | collective-permute-start | bytes 835592 | tf_op jit(solution)/shard_map/ppermute | solution.py:30
  31.3 11.2 %collective-permute-start.8 = (bf16[2,32,2176]{2,1,0:T(8,128)(2,1)S(1)}, bf16[2,32,2176]{2,1,0:T(8,128)(2,1)S(1)}, u32[]{:S(2)}, u32[]{:S(2)}) collective-permute-start(bf16[2,32,2176]{2,1,0:T(8,128)(2,1)S(1)} %collective-permute-done.4), channel_id=1, source_target_pairs={{0,1},{1,0},{2,3},{3,2},{4,5},{5,4},{6,7},{7,6},{8,9},{9,8},{10,11... | collective-permute-start | bytes 835592 | tf_op jit(solution)/shard_map/ppermute | solution.py:30
  46.7 61.3 %collective-permute-start.9 = (bf16[512,2048]{1,0:T(8,128)(2,1)S(1)}, bf16[512,2048]{1,0:T(8,128)(2,1)}, u32[]{:S(2)}, u32[]{:S(2)}) collective-permute-start(bf16[512,2048]{1,0:T(8,128)(2,1)S(1)} %convolution_convert_fusion.own_ref), channel_id=1, source_target_pairs={{0,8},{8,0},{16,24},{24,16},{1,9},{9,1},{17,25},{25,17},{2,10},{10... | collective-permute-start | bytes 6291464 | tf_op jit(solution)/shard_map/ppermute | solution.py:30
  54.4 19.9 %collective-permute-start.11 = (bf16[512,768]{1,0:T(8,128)(2,1)}, bf16[512,768]{1,0:T(8,128)(2,1)}, u32[]{:S(2)}, u32[]{:S(2)}) collective-permute-start(bf16[512,768]{1,0:T(8,128)(2,1)} %get-tuple-element.33), channel_id=1, source_target_pairs={{0,24},{8,16},{16,8},{24,0},{1,25},{9,17},{17,9},{25,1},{2,26},{10... | collective-permute-start | bytes 2359304 | tf_op jit(solution)/shard_map/ppermute | solution.py:30
  55.5 36.2 %collective-permute-start.12 = (bf16[512,768]{1,0:T(8,128)(2,1)}, bf16[512,768]{1,0:T(8,128)(2,1)}, u32[]{:S(2)}, u32[]{:S(2)}) collective-permute-start(bf16[512,768]{1,0:T(8,128)(2,1)} %get-tuple-element.34), channel_id=1, source_target_pairs={{0,16},{8,24},{16,0},{24,8},{1,17},{9,25},{17,1},{25,9},{2,18},{10... | collective-permute-start | bytes 2359304 | tf_op jit(solution)/shard_map/ppermute | solution.py:30
  58.9 49.1 %collective-permute-start.13 = (bf16[2,512,384]{2,1,0:T(8,128)(2,1)}, bf16[2,512,384]{2,1,0:T(8,128)(2,1)}, u32[]{:S(2)}, u32[]{:S(2)}) collective-permute-start(bf16[2,512,384]{2,1,0:T(8,128)(2,1)} %get-tuple-element.65), channel_id=1, source_target_pairs={{0,8},{8,0},{16,24},{24,16},{1,9},{9,1},{17,25},{25,17},{2,10},{10... | collective-permute-start | bytes 2359304 | tf_op jit(solution)/shard_map/ppermute | solution.py:30
  61.6 46.4 %collective-permute-start.15 = (bf16[2,384,384]{2,1,0:T(8,128)(2,1)S(1)}, bf16[2,384,384]{2,1,0:T(8,128)(2,1)S(1)}, u32[]{:S(2)}, u32[]{:S(2)}) collective-permute-start(bf16[2,384,384]{2,1,0:T(8,128)(2,1)S(1)} %get-tuple-element.64), channel_id=1, source_target_pairs={{0,24},{8,16},{16,8},{24,0},{1,25},{9,17},{17,9},{25,1},{2,26},{10... | collective-permute-start | bytes 1769480 | tf_op jit(solution)/shard_map/ppermute | solution.py:30
  74.4 33.6 %collective-permute-start.14 = (bf16[2,128,384]{2,1,0:T(8,128)(2,1)S(1)}, bf16[2,128,384]{2,1,0:T(8,128)(2,1)S(1)}, u32[]{:S(2)}, u32[]{:S(2)}) collective-permute-start(bf16[2,128,384]{2,1,0:T(8,128)(2,1)S(1)} %get-tuple-element.62), channel_id=1, source_target_pairs={{0,24},{8,16},{16,8},{24,0},{1,25},{9,17},{17,9},{25,1},{2,26},{10... | collective-permute-start | bytes 589832 | tf_op jit(solution)/shard_map/ppermute | solution.py:30
  120.3 16.4 %collective-permute-start.16 = (bf16[2,512,384]{2,1,0:T(8,128)(2,1)S(1)}, bf16[2,512,384]{2,1,0:T(8,128)(2,1)S(1)}, u32[]{:S(2)}, u32[]{:S(2)}) collective-permute-start(bf16[2,512,384]{2,1,0:T(8,128)(2,1)S(1)} %get-tuple-element.38), channel_id=1, source_target_pairs={{0,8},{8,0},{16,24},{24,16},{1,9},{9,1},{17,25},{25,17},{2,10},{10... | collective-permute-start | bytes 2359304 | tf_op jit(solution)/shard_map/ppermute | solution.py:30
  120.4 16.3 %collective-permute-start.17 = (bf16[2,384,384]{2,1,0:T(8,128)(2,1)S(1)}, bf16[2,384,384]{2,1,0:T(8,128)(2,1)S(1)}, u32[]{:S(2)}, u32[]{:S(2)}) collective-permute-start(bf16[2,384,384]{2,1,0:T(8,128)(2,1)S(1)} %get-tuple-element.63), channel_id=1, source_target_pairs={{0,16},{8,24},{16,0},{24,8},{1,17},{9,25},{17,1},{25,9},{2,18},{10... | collective-permute-start | bytes 1769480 | tf_op jit(solution)/shard_map/ppermute | solution.py:30
  121.9 18.5 %collective-permute-start.18 = (bf16[2,128,384]{2,1,0:T(8,128)(2,1)S(1)}, bf16[2,128,384]{2,1,0:T(8,128)(2,1)S(1)}, u32[]{:S(2)}, u32[]{:S(2)}) collective-permute-start(bf16[2,128,384]{2,1,0:T(8,128)(2,1)S(1)} %get-tuple-element.61), channel_id=1, source_target_pairs={{0,16},{8,24},{16,0},{24,8},{1,17},{9,25},{17,1},{25,9},{2,18},{10... | collective-permute-start | bytes 589832 | tf_op jit(solution)/shard_map/ppermute | solution.py:30
  145.3 14.5 %collective-permute-start.22 = (bf16[2,64,384]{2,1,0:T(8,128)(2,1)S(1)}, bf16[2,64,384]{2,1,0:T(8,128)(2,1)S(1)}, u32[]{:S(2)}, u32[]{:S(2)}) collective-permute-start(bf16[2,64,384]{2,1,0:T(8,128)(2,1)S(1)} %get-tuple-element.45), channel_id=1, source_target_pairs={{0,4},{1,5},{2,6},{3,7},{4,0},{5,1},{6,2},{7,3},{8,12},{9,13},{10,... | collective-permute-start | bytes 294920 | tf_op jit(solution)/shard_map/ppermute | solution.py:30
  146.9 15.9 %collective-permute-start.23 = (bf16[2,64,384]{2,1,0:T(8,128)(2,1)S(1)}, bf16[2,64,384]{2,1,0:T(8,128)(2,1)S(1)}, u32[]{:S(2)}, u32[]{:S(2)}) collective-permute-start(bf16[2,64,384]{2,1,0:T(8,128)(2,1)S(1)} %get-tuple-element.46), channel_id=1, source_target_pairs={{0,5},{1,4},{2,7},{3,6},{4,1},{5,0},{6,3},{7,2},{8,13},{9,12},{10,... | collective-permute-start | bytes 294920 | tf_op jit(solution)/shard_map/ppermute | solution.py:30
  149.1 13.6 %collective-permute-start.24 = (bf16[2,64,384]{2,1,0:T(8,128)(2,1)S(1)}, bf16[2,64,384]{2,1,0:T(8,128)(2,1)S(1)}, u32[]{:S(2)}, u32[]{:S(2)}) collective-permute-start(bf16[2,64,384]{2,1,0:T(8,128)(2,1)S(1)} %get-tuple-element.47), channel_id=1, source_target_pairs={{0,6},{1,7},{2,4},{3,5},{4,2},{5,3},{6,0},{7,1},{8,14},{9,15},{10,... | collective-permute-start | bytes 294920 | tf_op jit(solution)/shard_map/ppermute | solution.py:30
  150.5 12.3 %collective-permute-start.25 = (bf16[2,64,384]{2,1,0:T(8,128)(2,1)S(1)}, bf16[2,64,384]{2,1,0:T(8,128)(2,1)S(1)}, u32[]{:S(2)}, u32[]{:S(2)}) collective-permute-start(bf16[2,64,384]{2,1,0:T(8,128)(2,1)S(1)} %get-tuple-element.48), channel_id=1, source_target_pairs={{0,7},{1,6},{2,5},{3,4},{4,3},{5,2},{6,1},{7,0},{8,15},{9,14},{10,... | collective-permute-start | bytes 294920 | tf_op jit(solution)/shard_map/ppermute | solution.py:30
  164.2 9.7 %collective-permute-start.27 = (bf16[2,64,384]{2,1,0:T(8,128)(2,1)S(1)}, bf16[2,64,384]{2,1,0:T(8,128)(2,1)S(1)}, u32[]{:S(2)}, u32[]{:S(2)}) collective-permute-start(bf16[2,64,384]{2,1,0:T(8,128)(2,1)S(1)} %get-tuple-element.51), channel_id=1, source_target_pairs={{0,2},{1,3},{2,0},{3,1},{4,6},{5,7},{6,4},{7,5},{8,10},{9,11},{10,... | collective-permute-start | bytes 294920 | tf_op jit(solution)/shard_map/ppermute | solution.py:30
  168.3 14.3 %collective-permute-start.29 = (bf16[2,64,384]{2,1,0:T(8,128)(2,1)S(1)}, bf16[2,64,384]{2,1,0:T(8,128)(2,1)S(1)}, u32[]{:S(2)}, u32[]{:S(2)}) collective-permute-start(bf16[2,64,384]{2,1,0:T(8,128)(2,1)S(1)} %get-tuple-element.53), channel_id=1, source_target_pairs={{0,4},{1,5},{2,6},{3,7},{4,0},{5,1},{6,2},{7,3},{8,12},{9,13},{10,... | collective-permute-start | bytes 294920 | tf_op jit(solution)/shard_map/ppermute | solution.py:30
  170.8 14.4 %collective-permute-start.30 = (bf16[2,64,384]{2,1,0:T(8,128)(2,1)S(1)}, bf16[2,64,384]{2,1,0:T(8,128)(2,1)S(1)}, u32[]{:S(2)}, u32[]{:S(2)}) collective-permute-start(bf16[2,64,384]{2,1,0:T(8,128)(2,1)S(1)} %get-tuple-element.54), channel_id=1, source_target_pairs={{0,5},{1,4},{2,7},{3,6},{4,1},{5,0},{6,3},{7,2},{8,13},{9,12},{10,... | collective-permute-start | bytes 294920 | tf_op jit(solution)/shard_map/ppermute | solution.py:30
  171.8 13.5 %collective-permute-start.31 = (bf16[2,64,384]{2,1,0:T(8,128)(2,1)S(1)}, bf16[2,64,384]{2,1,0:T(8,128)(2,1)S(1)}, u32[]{:S(2)}, u32[]{:S(2)}) collective-permute-start(bf16[2,64,384]{2,1,0:T(8,128)(2,1)S(1)} %get-tuple-element.55), channel_id=1, source_target_pairs={{0,6},{1,7},{2,4},{3,5},{4,2},{5,3},{6,0},{7,1},{8,14},{9,15},{10,... | collective-permute-start | bytes 294920 | tf_op jit(solution)/shard_map/ppermute | solution.py:30
  173.8 11.6 %collective-permute-start.32 = (bf16[2,64,384]{2,1,0:T(8,128)(2,1)S(1)}, bf16[2,64,384]{2,1,0:T(8,128)(2,1)S(1)}, u32[]{:S(2)}, u32[]{:S(2)}) collective-permute-start(bf16[2,64,384]{2,1,0:T(8,128)(2,1)S(1)} %get-tuple-element.56), channel_id=1, source_target_pairs={{0,7},{1,6},{2,5},{3,4},{4,3},{5,2},{6,1},{7,0},{8,15},{9,14},{10,... | collective-permute-start | bytes 294920 | tf_op jit(solution)/shard_map/ppermute | solution.py:30
  (13 other events, 119.4 us)
